TPU v7x, 32 devices: a whole 2x2x4 slice. The times are simulated.
32 devices in a mesh: fsdp: 8 (over z, x), dp: 4 (over y, core).
Axes of the slice: x: 2, y: 2, z: 4, core: 2. Of those that a mesh axis runs over, the one named last changes fastest.
Arguments:
- tokens: bfloat16 [32, 1024, 1152], P(('fsdp', 'dp')), may hold values from -6 to 6
- timesteps: int32 [32], P(('fsdp', 'dp')), may hold values from 0 to 999, as said below
- labels: int32 [32], P(('fsdp', 'dp')), may hold values from 0 to 999
- head_keep: int32 [32, 16], P(('fsdp', 'dp')), may hold values from 0 to 1, as said below
- chan_keep: int32 [32, 4608], P(('fsdp', 'dp')), may hold values from 0 to 1, as said below
- cotangent: bfloat16 [32, 1024, 1152], P(('fsdp', 'dp')), may hold values from -6 to 6
- qkv_weight: bfloat16 [1152, 3456], P('fsdp'), may hold values from -0.1875 to 0.1875
- qv_bias: bfloat16 [2, 1152], P(None, 'fsdp'), may hold values from -3 to 3
- out_weight: bfloat16 [1152, 1152], P('fsdp'), may hold values from -3 to 3
- out_bias: bfloat16 [1152], P('fsdp'), may hold values from -3 to 3
- up_weight: bfloat16 [1152, 4608], P('fsdp'), may hold values from -0.1875 to 0.1875
- up_bias: bfloat16 [4608], P('fsdp'), may hold values from -3 to 3
- down_weight: bfloat16 [4608, 1152], P('fsdp'), may hold values from -0.09375 to 0.09375
- down_bias: bfloat16 [1152], P('fsdp'), may hold values from -3 to 3
- ada_weight: bfloat16 [1152, 6912], P('fsdp'), may hold values from -0.1875 to 0.1875
- ada_bias: bfloat16 [6912], P('fsdp'), may hold values from -3 to 3
- class_table: bfloat16 [1000, 1152], P(None, 'fsdp'), may hold values from -6 to 6
Outputs:
- block_out: bfloat16 [32, 1024, 1152], P(('fsdp', 'dp'))
- tokens_grad: bfloat16 [32, 1024, 1152], P(('fsdp', 'dp'))
- qkv_weight_grad: float32 [1152, 3456], P('fsdp')
- qv_bias_grad: float32 [2, 1152], P(None, 'fsdp')
- out_weight_grad: float32 [1152, 1152], P('fsdp')
- out_bias_grad: float32 [1152], P('fsdp')
- up_weight_grad: float32 [1152, 4608], P('fsdp')
- up_bias_grad: float32 [4608], P('fsdp')
- down_weight_grad: float32 [4608, 1152], P('fsdp')
- down_bias_grad: float32 [1152], P('fsdp')
- ada_weight_grad: float32 [1152, 6912], P('fsdp')
- ada_bias_grad: float32 [6912], P('fsdp')
- class_table_grad: float32 [1000, 1152], P(None, 'fsdp')
Inputs may be any that keep to these rules, and one draw needn't show every extreme that they name: timesteps lean toward the noisy end. `head_keep`: each image draws its own keep rate, from a quarter to one, so kept heads differ from image to image. `chan_keep`: each image draws its own keep rate, from a quarter to one, so kept hidden units differ from image to image.
All inputs are finite; a program needn't handle non-finite values.
Results may differ from a plain program's by a relative error of at most 0.02.
The roundings to bfloat16 on the way count: a program that leaves them out, or rounds other values in their place, can miss the bound.
Values may be sent and summed in bfloat16 or wider, within the bound.
No kernel may reach another device: no remote copies, remote signals or barrier semaphores. Data moves between devices by JAX's collectives and lax.ppermute only.
A program may use at most 384 MiB of HBM per device.

v0:
```python
import math

import jax
import jax.numpy as jnp
from jax import lax
from jax.sharding import PartitionSpec as P


def time_embed(time_steps, model_width):
    half_width = model_width // 2
    frequency = jnp.exp(-math.log(10000.0) * jnp.arange(half_width, dtype=jnp.float32) / half_width)
    angles = time_steps.astype(jnp.float32)[:, None] * frequency[None, :]
    return jnp.concatenate([jnp.cos(angles), jnp.sin(angles)], axis=1)


def one_hot(label_rows, class_count, out_type):
    return (label_rows[:, None] == jnp.arange(class_count, dtype=jnp.int32)[None, :]).astype(
        out_type
    )


def norm_forward(values):
    row_mean = jnp.mean(values, axis=-1, keepdims=True)
    centred = values - row_mean
    inverse = lax.rsqrt(jnp.mean(centred * centred, axis=-1, keepdims=True) + 1e-06)
    return (centred * inverse, inverse)


def norm_backward(gradient, normed, inverse):
    return inverse * (
        gradient
        - jnp.mean(gradient, axis=-1, keepdims=True)
        - normed * jnp.mean(gradient * normed, axis=-1, keepdims=True)
    )


def gelu_tanh(values):
    return jax.nn.gelu(values, approximate=True)


def attend_forward(query_rows, key_rows, value_rows):
    seq_length = query_rows.shape[0]
    block_rows = min(512, seq_length)
    score_scale = query_rows.shape[2] ** (-0.5)
    outputs = []
    log_sums = []
    for start_row in range(0, seq_length, block_rows):
        query_block = query_rows[start_row : start_row + block_rows]
        scores = (
            jnp.einsum("qhd,khd->hqk", query_block, key_rows, preferred_element_type=jnp.float32)
            * score_scale
        )
        row_max = jnp.max(scores, axis=-1, keepdims=True)
        exp_scores = jnp.exp(scores - row_max)
        row_total = jnp.sum(exp_scores, axis=-1, keepdims=True)
        attn_probs = (exp_scores / row_total).astype(jnp.bfloat16)
        outputs.append(
            jnp.einsum("hqk,khd->qhd", attn_probs, value_rows, preferred_element_type=jnp.float32)
        )
        log_sums.append(row_max + jnp.log(row_total))
    return (jnp.concatenate(outputs, axis=0), jnp.concatenate(log_sums, axis=1))


def attend_backward(query_rows, key_rows, value_rows, grad_rows, log_sums):
    seq_length = query_rows.shape[0]
    block_rows = min(512, seq_length)
    score_scale = query_rows.shape[2] ** (-0.5)
    query_grads = []
    key_grad = jnp.zeros(key_rows.shape, jnp.float32)
    value_grad = jnp.zeros(value_rows.shape, jnp.float32)
    for start_row in range(0, seq_length, block_rows):
        query_block = query_rows[start_row : start_row + block_rows]
        grad_block = grad_rows[start_row : start_row + block_rows]
        lse_block = log_sums[:, start_row : start_row + block_rows]
        scores = (
            jnp.einsum("qhd,khd->hqk", query_block, key_rows, preferred_element_type=jnp.float32)
            * score_scale
        )
        attn_probs = jnp.exp(scores - lse_block)
        prob_grad = jnp.einsum(
            "qhd,khd->hqk", grad_block, value_rows, preferred_element_type=jnp.float32
        )
        row_dot = jnp.sum(prob_grad * attn_probs, axis=-1, keepdims=True)
        score_grad = (attn_probs * (prob_grad - row_dot) * score_scale).astype(jnp.bfloat16)
        query_grads.append(
            jnp.einsum("hqk,khd->qhd", score_grad, key_rows, preferred_element_type=jnp.float32)
        )
        key_grad = key_grad + jnp.einsum(
            "hqk,qhd->khd", score_grad, query_block, preferred_element_type=jnp.float32
        )
        value_grad = value_grad + jnp.einsum(
            "hqk,qhd->khd",
            attn_probs.astype(jnp.bfloat16),
            grad_block,
            preferred_element_type=jnp.float32,
        )
    return (jnp.concatenate(query_grads, axis=0), key_grad, value_grad)


def body(
    tokens,
    timesteps,
    labels,
    head_keep,
    chan_keep,
    cotangent,
    qkv_weight,
    qv_bias,
    out_weight,
    out_bias,
    up_weight,
    up_bias,
    down_weight,
    down_bias,
    ada_weight,
    ada_bias,
    class_table,
):
    seq_count, seq_length, model_width = tokens.shape
    row_count = seq_count * seq_length
    head_count = head_keep.shape[1]
    head_size = model_width // head_count
    hidden_count = chan_keep.shape[1]
    class_count = class_table.shape[0]
    ada_full, ada_bias_full, table_full = (
        lax.all_gather(ada_weight, "fsdp", axis=0, tiled=True),
        lax.all_gather(ada_bias, "fsdp", axis=0, tiled=True),
        lax.all_gather(class_table, "fsdp", axis=1, tiled=True),
    )
    cond_pre = time_embed(timesteps, model_width) + jnp.dot(
        one_hot(labels, class_count, jnp.bfloat16), table_full, preferred_element_type=jnp.float32
    )
    cond_act = jax.nn.silu(cond_pre).astype(jnp.bfloat16)
    ada_rows = jnp.dot(
        cond_act, ada_full, preferred_element_type=jnp.float32
    ) + ada_bias_full.astype(jnp.float32)
    ada_parts = ada_rows.reshape(seq_count, 6, 1, model_width)
    shift_attn = ada_parts[:, 0]
    scale_attn = ada_parts[:, 1]
    gate_attn = ada_parts[:, 2]
    shift_mlp = ada_parts[:, 3]
    scale_mlp = ada_parts[:, 4]
    gate_mlp = ada_parts[:, 5]
    qkv_full, out_full, qv_full, out_bias_full = (
        lax.all_gather(qkv_weight, "fsdp", axis=0, tiled=True),
        lax.all_gather(out_weight, "fsdp", axis=0, tiled=True),
        lax.all_gather(qv_bias, "fsdp", axis=1, tiled=True),
        lax.all_gather(out_bias, "fsdp", axis=0, tiled=True),
    )
    inputs = tokens.astype(jnp.float32)
    normed_one, inverse_one = norm_forward(inputs)
    mod_one = (
        (normed_one * (1.0 + scale_attn) + shift_attn)
        .astype(jnp.bfloat16)
        .reshape(row_count, model_width)
    )
    qkv_bias_row = jnp.concatenate(
        [qv_full[0], jnp.zeros((model_width,), jnp.bfloat16), qv_full[1]]
    ).astype(jnp.float32)
    qkv_rows = (
        jnp.dot(mod_one, qkv_full, preferred_element_type=jnp.float32) + qkv_bias_row
    ).astype(jnp.bfloat16)
    qkv_split = qkv_rows.reshape(seq_count, seq_length, 3, head_count, head_size)
    query_all = qkv_split[:, :, 0]
    key_all = qkv_split[:, :, 1]
    value_all = qkv_split[:, :, 2]
    attn_raw, log_sums = lax.map(
        lambda seq_group: attend_forward(*seq_group), (query_all, key_all, value_all)
    )
    head_mask = head_keep.astype(jnp.float32)[:, None, :, None]
    attn_low = (attn_raw * head_mask).astype(jnp.bfloat16).reshape(row_count, model_width)
    attn_branch = (
        jnp.dot(attn_low, out_full, preferred_element_type=jnp.float32)
        + out_bias_full.astype(jnp.float32)
    ).reshape(seq_count, seq_length, model_width)
    middle = inputs + gate_attn * attn_branch
    up_full, down_full, up_bias_full, down_bias_full = (
        lax.all_gather(up_weight, "fsdp", axis=0, tiled=True),
        lax.all_gather(down_weight, "fsdp", axis=0, tiled=True),
        lax.all_gather(up_bias, "fsdp", axis=0, tiled=True),
        lax.all_gather(down_bias, "fsdp", axis=0, tiled=True),
    )
    normed_two, inverse_two = norm_forward(middle)
    mod_two = (
        (normed_two * (1.0 + scale_mlp) + shift_mlp)
        .astype(jnp.bfloat16)
        .reshape(row_count, model_width)
    )
    pre_act = jnp.dot(mod_two, up_full, preferred_element_type=jnp.float32) + up_bias_full.astype(
        jnp.float32
    )
    chan_mask = chan_keep.astype(jnp.float32)[:, None, :]
    act_low = (
        (gelu_tanh(pre_act).reshape(seq_count, seq_length, hidden_count) * chan_mask)
        .astype(jnp.bfloat16)
        .reshape(row_count, hidden_count)
    )
    mlp_branch = (
        jnp.dot(act_low, down_full, preferred_element_type=jnp.float32)
        + down_bias_full.astype(jnp.float32)
    ).reshape(seq_count, seq_length, model_width)
    block_out = (middle + gate_mlp * mlp_branch).astype(jnp.bfloat16)
    out_grad_rows = cotangent.astype(jnp.float32)
    gate_mlp_grad = jnp.sum(out_grad_rows * mlp_branch, axis=1)
    branch_grad = (out_grad_rows * gate_mlp).astype(jnp.bfloat16).reshape(row_count, model_width)
    up_back, down_back = (
        lax.all_gather(up_weight, "fsdp", axis=0, tiled=True),
        lax.all_gather(down_weight, "fsdp", axis=0, tiled=True),
    )
    down_bias_g = jnp.sum(branch_grad.astype(jnp.float32), axis=0)
    down_weight_g = jnp.einsum(
        "tf,td->fd", act_low, branch_grad, preferred_element_type=jnp.float32
    )
    act_grad = jnp.einsum("td,fd->tf", branch_grad, down_back, preferred_element_type=jnp.float32)
    masked_grad = (act_grad.reshape(seq_count, seq_length, hidden_count) * chan_mask).reshape(
        row_count, hidden_count
    )
    gelu_out, gelu_pull = jax.vjp(gelu_tanh, pre_act)
    pre_grad = gelu_pull(masked_grad)[0].astype(jnp.bfloat16)
    up_bias_g = jnp.sum(pre_grad.astype(jnp.float32), axis=0)
    up_weight_g = jnp.einsum("td,tf->df", mod_two, pre_grad, preferred_element_type=jnp.float32)
    mod_two_grad = jnp.einsum(
        "tf,df->td", pre_grad, up_back, preferred_element_type=jnp.float32
    ).reshape(seq_count, seq_length, model_width)
    scale_mlp_grad = jnp.sum(mod_two_grad * normed_two, axis=1)
    shift_mlp_grad = jnp.sum(mod_two_grad, axis=1)
    middle_grad = out_grad_rows + norm_backward(
        mod_two_grad * (1.0 + scale_mlp), normed_two, inverse_two
    )
    mlp_shards = (
        lax.psum_scatter(
            up_weight_g.astype(jnp.bfloat16), "fsdp", scatter_dimension=0, tiled=True
        ).astype(jnp.float32),
        lax.psum_scatter(
            down_weight_g.astype(jnp.bfloat16), "fsdp", scatter_dimension=0, tiled=True
        ).astype(jnp.float32),
        lax.psum_scatter(
            up_bias_g.astype(jnp.bfloat16), "fsdp", scatter_dimension=0, tiled=True
        ).astype(jnp.float32),
        lax.psum_scatter(
            down_bias_g.astype(jnp.bfloat16), "fsdp", scatter_dimension=0, tiled=True
        ).astype(jnp.float32),
    )
    gate_attn_grad = jnp.sum(middle_grad * attn_branch, axis=1)
    attn_grad = (middle_grad * gate_attn).astype(jnp.bfloat16).reshape(row_count, model_width)
    qkv_back, out_back = (
        lax.all_gather(qkv_weight, "fsdp", axis=0, tiled=True),
        lax.all_gather(out_weight, "fsdp", axis=0, tiled=True),
    )
    out_bias_g = jnp.sum(attn_grad.astype(jnp.float32), axis=0)
    out_weight_g = jnp.einsum("td,te->de", attn_low, attn_grad, preferred_element_type=jnp.float32)
    low_grad = jnp.einsum(
        "te,de->td", attn_grad, out_back, preferred_element_type=jnp.float32
    ).astype(jnp.bfloat16)
    head_grad = (
        low_grad.reshape(seq_count, seq_length, head_count, head_size)
        * head_keep.astype(jnp.bfloat16)[:, None, :, None]
    )
    query_grad, key_grad, value_grad = lax.map(
        lambda seq_group: attend_backward(*seq_group),
        (query_all, key_all, value_all, head_grad, log_sums),
    )
    qkv_grad_rows = (
        jnp.stack([query_grad, key_grad, value_grad], axis=2)
        .astype(jnp.bfloat16)
        .reshape(row_count, 3 * model_width)
    )
    qkv_weight_g = jnp.einsum(
        "td,te->de", mod_one, qkv_grad_rows, preferred_element_type=jnp.float32
    )
    bias_sums = jnp.sum(qkv_grad_rows.astype(jnp.float32), axis=0).reshape(3, model_width)
    qv_bias_g = jnp.stack([bias_sums[0], bias_sums[2]], axis=0)
    mod_one_grad = jnp.einsum(
        "te,de->td", qkv_grad_rows, qkv_back, preferred_element_type=jnp.float32
    ).reshape(seq_count, seq_length, model_width)
    scale_attn_grad = jnp.sum(mod_one_grad * normed_one, axis=1)
    shift_attn_grad = jnp.sum(mod_one_grad, axis=1)
    tokens_grad = (
        middle_grad + norm_backward(mod_one_grad * (1.0 + scale_attn), normed_one, inverse_one)
    ).astype(jnp.bfloat16)
    attn_shards = (
        lax.psum_scatter(
            qkv_weight_g.astype(jnp.bfloat16), "fsdp", scatter_dimension=0, tiled=True
        ).astype(jnp.float32),
        lax.psum_scatter(
            out_weight_g.astype(jnp.bfloat16), "fsdp", scatter_dimension=0, tiled=True
        ).astype(jnp.float32),
        lax.psum_scatter(
            qv_bias_g.astype(jnp.bfloat16), "fsdp", scatter_dimension=1, tiled=True
        ).astype(jnp.float32),
        lax.psum_scatter(
            out_bias_g.astype(jnp.bfloat16), "fsdp", scatter_dimension=0, tiled=True
        ).astype(jnp.float32),
    )
    ada_grad = (
        jnp.stack(
            [
                shift_attn_grad,
                scale_attn_grad,
                gate_attn_grad,
                shift_mlp_grad,
                scale_mlp_grad,
                gate_mlp_grad,
            ],
            axis=1,
        )
        .reshape(seq_count, 6 * model_width)
        .astype(jnp.bfloat16)
    )
    ada_weight_g = jnp.einsum("sd,se->de", cond_act, ada_grad, preferred_element_type=jnp.float32)
    ada_bias_g = jnp.sum(ada_grad.astype(jnp.float32), axis=0)
    cond_act_grad = jnp.einsum("se,de->sd", ada_grad, ada_full, preferred_element_type=jnp.float32)
    silu_out, silu_pull = jax.vjp(jax.nn.silu, cond_pre)
    cond_grad = silu_pull(cond_act_grad)[0]
    table_g = jnp.einsum(
        "sc,sd->cd",
        one_hot(labels, class_count, jnp.float32),
        cond_grad,
        precision=lax.Precision.HIGHEST,
    )
    ada_shards = (
        lax.psum_scatter(
            ada_weight_g.astype(jnp.bfloat16), "fsdp", scatter_dimension=0, tiled=True
        ).astype(jnp.float32),
        lax.psum_scatter(
            ada_bias_g.astype(jnp.bfloat16), "fsdp", scatter_dimension=0, tiled=True
        ).astype(jnp.float32),
        lax.psum_scatter(
            table_g.astype(jnp.bfloat16), "fsdp", scatter_dimension=1, tiled=True
        ).astype(jnp.float32),
    )
    summed = (
        lax.psum(mlp_shards[0].astype(jnp.bfloat16), "dp").astype(jnp.float32),
        lax.psum(mlp_shards[1].astype(jnp.bfloat16), "dp").astype(jnp.float32),
        lax.psum(mlp_shards[2].astype(jnp.bfloat16), "dp").astype(jnp.float32),
        lax.psum(mlp_shards[3].astype(jnp.bfloat16), "dp").astype(jnp.float32),
        lax.psum(attn_shards[0].astype(jnp.bfloat16), "dp").astype(jnp.float32),
        lax.psum(attn_shards[1].astype(jnp.bfloat16), "dp").astype(jnp.float32),
        lax.psum(attn_shards[2].astype(jnp.bfloat16), "dp").astype(jnp.float32),
        lax.psum(attn_shards[3].astype(jnp.bfloat16), "dp").astype(jnp.float32),
        lax.psum(ada_shards[0].astype(jnp.bfloat16), "dp").astype(jnp.float32),
        lax.psum(ada_shards[1].astype(jnp.bfloat16), "dp").astype(jnp.float32),
        lax.psum(ada_shards[2].astype(jnp.bfloat16), "dp").astype(jnp.float32),
    )
    return (
        block_out,
        tokens_grad,
        summed[4],
        summed[6],
        summed[5],
        summed[7],
        summed[0],
        summed[2],
        summed[1],
        summed[3],
        summed[8],
        summed[9],
        summed[10],
    )


def solution(mesh):
    return jax.shard_map(
        body,
        mesh=mesh,
        in_specs=(
            P(("fsdp", "dp"), None, None),
            P(("fsdp", "dp")),
            P(("fsdp", "dp")),
            P(("fsdp", "dp"), None),
            P(("fsdp", "dp"), None),
            P(("fsdp", "dp"), None, None),
            P("fsdp", None),
            P(None, "fsdp"),
            P("fsdp", None),
            P("fsdp"),
            P("fsdp", None),
            P("fsdp"),
            P("fsdp", None),
            P("fsdp"),
            P("fsdp", None),
            P("fsdp"),
            P(None, "fsdp"),
        ),
        out_specs=(
            P(("fsdp", "dp"), None, None),
            P(("fsdp", "dp"), None, None),
            P("fsdp", None),
            P(None, "fsdp"),
            P("fsdp", None),
            P("fsdp"),
            P("fsdp", None),
            P("fsdp"),
            P("fsdp", None),
            P("fsdp"),
            P("fsdp", None),
            P("fsdp"),
            P(None, "fsdp"),
        ),
        check_vma=False,
    )
```

profile of v0, /device:TPU:1, one launch (start us, length us, event | category | flops | bytes accessed | tf_op | source)
XLA Modules:
  0.0 2330.5 jit_solution(8677541740796173860)
XLA Ops:
  19.7 18.0 all-gather
  38.9 27.6 %all-reduce.9 = (bf16[1152]{0:T(1024)(128)(2,1)S(1)}, bf16[6912]{0:T(1024)(128)(2,1)S(1)}, bf16[1152]{0:T(1024)(128)(2,1)S(1)}, bf16[4608]{0:T(1024)(128)(2,1)S(1)}) all-reduce(bf16[1152]{0:T(1024)(128)(2,1)S(1)} %dynamic-update-slice.1, bf16[6912]{0:T(1024)(128)(2,1)S(1)} %dynamic-update-slice, ...), channel_id=1, replica_groups=mesh['fsdp'=8,'dp'=4] {'fsdp'}, use_global_device_ids=true, to_apply=%add.1 | all-reduce | flops 13824 | bytes 55296
  72.6 210.2 %all-gather.10.cloned.1.call-done = bf16[1152,6912]{1,0:T(8,128)(2,1)} async-done(((bf16[144,6912]{1,0:T(8,128)(2,1)}), bf16[1152,6912]{1,0:T(8,128)(2,1)}) %all-gather.10.cloned.1.call-update) | async-done | bytes 15925264 | tf_op jit(solution)/shard_map/all_gather | solution.py:126
  291.2 111.5 %all-gather.12.cloned.1.call-done = bf16[1152,3456]{1,0:T(8,128)(2,1)} async-done(((bf16[144,3456]{1,0:T(8,128)(2,1)}), bf16[1152,3456]{1,0:T(8,128)(2,1)}) %all-gather.12.cloned.1.call-update) | async-done | bytes 7962640 | tf_op jit(solution)/shard_map/all_gather | solution.py:145
  529.3 81.9 %all-gather.16.cloned.1.call-done = bf16[1152,4608]{1,0:T(8,128)(2,1)} async-done(((bf16[144,4608]{1,0:T(8,128)(2,1)}), bf16[1152,4608]{1,0:T(8,128)(2,1)}) %all-gather.16.cloned.1.call-update) | async-done | bytes 10616848 | tf_op jit(solution)/shard_map/all_gather | solution.py:178
  611.2 21.1 fusion.119
  632.3 131.6 %all-gather.18.cloned.1.call-done = bf16[4608,1152]{1,0:T(8,128)(2,1)} async-done(((bf16[576,1152]{1,0:T(8,128)(2,1)}), bf16[4608,1152]{1,0:T(8,128)(2,1)}) %all-gather.18.cloned.1.call-update) | async-done | bytes 10616848 | tf_op jit(solution)/shard_map/all_gather | solution.py:179
  763.9 30.0 %fusion.129 = (bf16[4608]{0:T(1024)(128)(2,1)}, bf16[1024,4608]{1,0:T(8,128)(2,1)}) fusion(f32[1024,4608]{1,0:T(8,128)} %fusion.119, f32[4608]{0:T(1024)S(1)} %copy-done.33, f32[4608]{0:T(1024)S(1)} %copy-done.31, bf16[4608,1152]{1,0:T(8,128)(2,1)} %all-gather.18.cloned.1.call-done, f32[1152]{0:T(1024)S(1)} %copy-done.28, ...), kind=kOutput, calls=%fused_computation.182 | convolution fusion | flops 10983698432 | bytes 41338368 | tf_op jit(solution)/shard_map/td,fd->tf/dot_general | solution.py:214
  793.9 19.9 fusion.121
  813.8 26.5 %fusion.61 = (bf16[1152]{0:T(1024)(128)(2,1)}, bf16[1,1024,1152]{2,1,0:T(8,128)(2,1)}, f32[1024]{0:T(1024)S(1)}, bf16[1152]{0:T(1024)(128)(2,1)}) fusion(bf16[1,1024,1152]{2,1,0:T(8,128)(2,1)S(1)} %copy-done.8, f32[1,1024,1152]{2,1,0:T(8,128)} %copy-done.7, f32[1152]{0:T(1024)S(1)} %copy-done.28, f32[1024,1152]{1,0:T(8,128)} %get-tuple-element.120, ...), kind=kOutput, calls=%fused_computation.76 | convolution fusion | flops 10940052480 | bytes 43714560 | tf_op jit(solution)/shard_map/dot_general | solution.py:199
  889.5 57.4 %fusion.84 = bf16[512,16,72]{0,2,1:T(8,128)(2,1)S(1)} fusion(f32[16,512,1024]{2,1,0:T(8,128)} %fusion.88, f32[16,512,1024]{2,1,0:T(8,128)} %get-tuple-element.118, f32[16,512]{1,0:T(8,128)} %log_add_fusion.1, bf16[1,1024,3,16,72]{1,4,3,2,0:T(8,128)(2,1)} %bitcast.156), kind=kOutput, calls=%fused_computation.111 | convolution fusion | flops 1283466240 | bytes 137822208 | tf_op jit(solution)/shard_map/while/body/eval_jaxpr/hqk,khd->qhd/dot_general | solution.py:86
  946.9 60.7 %fusion.34 = f32[16,72,1024]{2,1,0:T(8,128)} fusion(f32[16,512,1024]{2,1,0:T(8,128)} %fusion.88, f32[16,512,1024]{2,1,0:T(8,128)} %get-tuple-element.118, f32[16,512]{1,0:T(8,128)} %log_add_fusion.1, bf16[1,1024,3,16,72]{1,4,3,2,0:T(8,128)(2,1)} %bitcast.157), kind=kOutput, calls=%fused_computation.48 | convolution fusion | flops 1283466240 | bytes 140181504 | tf_op jit(solution)/shard_map/while/body/eval_jaxpr/hqk,qhd->khd/dot_general | solution.py:88
  1041.5 57.4 %fusion.81 = bf16[512,16,72]{0,2,1:T(8,128)(2,1)S(1)} fusion(f32[16,512,1024]{2,1,0:T(8,128)} %fusion.87, f32[16,512,1024]{2,1,0:T(8,128)} %get-tuple-element.116, f32[16,512]{1,0:T(8,128)} %log_add_fusion, bf16[1,1024,3,16,72]{1,4,3,2,0:T(8,128)(2,1)} %bitcast.158), kind=kOutput, calls=%fused_computation.110 | convolution fusion | flops 1283466240 | bytes 137822208 | tf_op jit(solution)/shard_map/while/body/eval_jaxpr/hqk,khd->qhd/dot_general | solution.py:86
  1098.9 60.7 %add_bitcast_fusion.1 = bf16[1,1024,1,16,72]{1,4,3,2,0:T(8,128)(2,1)} fusion(f32[16,72,1024]{2,1,0:T(8,128)} %fusion.34, f32[16,512,1024]{2,1,0:T(8,128)} %fusion.87, f32[16,512,1024]{2,1,0:T(8,128)} %get-tuple-element.116, f32[16,512]{1,0:T(8,128)} %log_add_fusion, bf16[1,1024,3,16,72]{1,4,3,2,0:T(8,128)(2,1)} %bitcast.159), kind=kOutput, calls=%fused_computation.92 | convolution fusion | flops 1285825536 | bytes 142540800 | tf_op jit(solution)/shard_map/while/body/eval_jaxpr/hqk,qhd->khd/dot_general | solution.py:88
  1224.4 23.8 %convolution_convert_fusion = bf16[4608,1152]{1,0:T(8,128)(2,1)} fusion(bf16[1,1024,1152]{2,1,0:T(8,128)(2,1)S(1)} %copy-done.9, f32[1152]{0:T(1024)S(1)} %copy-done.29, f32[1024,4608]{1,0:T(8,128)} %fusion.119, f32[4608]{0:T(1024)S(1)} %copy-done.32, f32[4608]{0:T(1024)S(1)} %copy-done.34), kind=kOutput, calls=%fused_computation.23 | convolution fusion | flops 10932387840 | bytes 31891968 | tf_op jit(solution)/shard_map/tf,td->fd/dot_general | solution.py:211
  1248.9 18.4 convolution_convert_fusion.1
  1275.2 64.8 %reduce-scatter.12.cloned.1.call-done = bf16[144,1152]{1,0:T(8,128)(2,1)} async-done(((bf16[1152,1152]{1,0:T(8,128)(2,1)}), bf16[144,1152]{1,0:T(8,128)(2,1)}) %reduce-scatter.12.cloned.1.call-update) | async-done | bytes 331792 | tf_op jit(solution)/shard_map/reduce_scatter | solution.py:285
  1340.0 147.2 %reduce-scatter.10.cloned.1.call-done = bf16[144,3456]{1,0:T(8,128)(2,1)} async-done(((bf16[1152,3456]{1,0:T(8,128)(2,1)}), bf16[144,3456]{1,0:T(8,128)(2,1)}) %reduce-scatter.10.cloned.1.call-update) | async-done | bytes 995344 | tf_op jit(solution)/shard_map/reduce_scatter | solution.py:282
  1487.2 182.9 %reduce-scatter.16.cloned.1.call-done = bf16[576,1152]{1,0:T(8,128)(2,1)} async-done(((bf16[4608,1152]{1,0:T(8,128)(2,1)}), bf16[576,1152]{1,0:T(8,128)(2,1)}) %reduce-scatter.16.cloned.1.call-update) | async-done | bytes 1327120 | tf_op jit(solution)/shard_map/reduce_scatter | solution.py:234
  1670.1 182.7 %reduce-scatter.14.cloned.1.call-done = bf16[144,4608]{1,0:T(8,128)(2,1)} async-done(((bf16[1152,4608]{1,0:T(8,128)(2,1)}), bf16[144,4608]{1,0:T(8,128)(2,1)}) %reduce-scatter.14.cloned.1.call-update) | async-done | bytes 1327120 | tf_op jit(solution)/shard_map/reduce_scatter | solution.py:231
  1852.8 273.2 %reduce-scatter.18.cloned.1.call-done = bf16[144,6912]{1,0:T(8,128)(2,1)} async-done(((bf16[1152,6912]{1,0:T(8,128)(2,1)}), bf16[144,6912]{1,0:T(8,128)(2,1)}) %reduce-scatter.18.cloned.1.call-update) | async-done | bytes 1990672 | tf_op jit(solution)/shard_map/reduce_scatter | solution.py:322
  2128.0 28.2 %all-reduce.8 = (bf16[1152]{0:T(1024)(128)(2,1)S(1)}, bf16[4608]{0:T(1024)(128)(2,1)S(1)}, bf16[1152]{0:T(1024)(128)(2,1)S(1)}, bf16[6912]{0:T(1024)(128)(2,1)S(1)}) all-reduce(bf16[1152]{0:T(1024)(128)(2,1)S(1)} %copy-done.42, bf16[4608]{0:T(1024)(128)(2,1)S(1)} %copy-done.44, ...), channel_id=5, replica_groups=mesh['fsdp'=8,'dp'=4] {'fsdp'}, use_global_device_ids=true, to_apply=%region_22.23.clone | all-reduce | flops 13824 | bytes 55296
  2156.5 29.6 %reduce-scatter.22.cloned.1.call-done = bf16[144,2]{1,0:T(8,128)(2,1)} async-done(((bf16[1152,2]{1,0:T(8,128)(2,1)}), bf16[144,2]{1,0:T(8,128)(2,1)}) %reduce-scatter.22.cloned.1.call-update) | async-done | bytes 592
  2197.6 112.7 %all-reduce.14.cloned.1.call-done = (bf16[144,3456]{1,0:T(8,128)(2,1)}, bf16[144,1152]{1,0:T(8,128)(2,1)}, bf16[144,4608]{1,0:T(8,128)(2,1)}, bf16[576,1152]{1,0...) async-done(((bf16[144,3456]{1,0:T(8,128)(2,1)}, bf16[144,1152]{1,0:T(8,128)(2,1)}, bf16[144,4608]{1,0:T(8,128)(2,1)}, bf16[576,1152]{1,0:T(8,128)(2,1)}, ...) | async-done | bytes 6259984 | tf_op jit(solution)/shard_map/psum | solution.py:337
  (266 shorter events, 332.3 us)
Async XLA Ops:
  7.3 61.7 %all-gather.8.cloned.1.call-start = ((), (), s32[]{:S(2)}) async-start(), calls=%async_computation.7 | async-start | bytes 2654208 | tf_op jit(solution)/shard_map/all_gather | solution.py:128
  8.0 274.8 %all-gather.10.cloned.1.call-start = ((), (), s32[]{:S(2)}) async-start(), calls=%async_computation.8 | async-start | bytes 17915904 | tf_op jit(solution)/shard_map/all_gather | solution.py:126
  8.7 394.0 %all-gather.12.cloned.1.call-start = ((), (), s32[]{:S(2)}) async-start(), calls=%async_computation.9 | async-start | bytes 8957952 | tf_op jit(solution)/shard_map/all_gather | solution.py:145
  9.5 506.0 %all-gather.14.cloned.1.call-start = ((), (), s32[]{:S(2)}) async-start(), calls=%async_computation.10 | async-start | bytes 2985984 | tf_op jit(solution)/shard_map/all_gather | solution.py:146
  10.0 601.1 %all-gather.16.cloned.1.call-start = ((), (), s32[]{:S(2)}) async-start(), calls=%async_computation.11 | async-start | bytes 11943936 | tf_op jit(solution)/shard_map/all_gather | solution.py:178
  10.6 753.2 %all-gather.18.cloned.1.call-start = ((), (), s32[]{:S(2)}) async-start(), calls=%async_computation.12 | async-start | bytes 11943936 | tf_op jit(solution)/shard_map/all_gather | solution.py:179
  11.2 1264.0 %reduce-scatter.20.cloned.1.call-start = ((), (), s32[]{:S(2)}) async-start(), calls=%async_computation.18 | async-start | bytes 2654208 | tf_op jit(solution)/shard_map/reduce_scatter | solution.py:328
  17.5 385.2 %copy-start.21 = (f32[1024]{0:T(1024)}, f32[1024]{0:T(1024)S(1)}, u32[]{:S(2)}) copy-start(f32[1024]{0:T(1024)S(1)} %broadcast_multiply_fusion.6) | copy-start | bytes 12292
  18.3 384.5 %copy-start.38 = (f32[1024]{0:T(1024)}, f32[1024]{0:T(1024)S(1)}, u32[]{:S(2)}) copy-start(f32[1024]{0:T(1024)S(1)} %add_rsqrt_fusion.1) | copy-start | bytes 12292
  19.0 271.5 %copy-start.17 = (f32[576]{0:T(1024)}, f32[576]{0:T(1024)S(1)}, u32[]{:S(2)}) copy-start(f32[576]{0:T(1024)S(1)} %get-tuple-element.124) | copy-start | bytes 6916
  19.0 271.5 %copy-start.19 = (f32[576]{0:T(1024)}, f32[576]{0:T(1024)S(1)}, u32[]{:S(2)}) copy-start(f32[576]{0:T(1024)S(1)} %get-tuple-element.125) | copy-start | bytes 6916
  525.2 315.1 %copy-start.23 = (f32[1024]{0:T(1024)}, f32[1024]{0:T(1024)S(1)}, u32[]{:S(2)}) copy-start(f32[1024]{0:T(1024)S(1)} %broadcast_multiply_fusion.5) | copy-start | bytes 12292
  528.0 312.3 %copy-start.40 = (f32[1024]{0:T(1024)}, f32[1024]{0:T(1024)S(1)}, u32[]{:S(2)}) copy-start(f32[1024]{0:T(1024)S(1)} %add_rsqrt_fusion) | copy-start | bytes 12292
  611.2 152.7 %copy-start.28 = (f32[1152]{0:T(1024)S(1)}, f32[1152]{0:T(1024)}, u32[]{:S(2)}) copy-start(f32[1152]{0:T(1024)} %get-tuple-element.66) | copy-start | bytes 13828
  1199.8 140.2 %reduce-scatter.12.cloned.1.call-start = ((), (), s32[]{:S(2)}) async-start(), calls=%async_computation.14 | async-start | bytes 2985984 | tf_op jit(solution)/shard_map/reduce_scatter | solution.py:285
  1207.7 279.4 %reduce-scatter.10.cloned.1.call-start = ((), (), s32[]{:S(2)}) async-start(), calls=%async_computation.13 | async-start | bytes 8957952 | tf_op jit(solution)/shard_map/reduce_scatter | solution.py:282
  1222.7 447.4 %reduce-scatter.16.cloned.1.call-start = ((), (), s32[]{:S(2)}) async-start(), calls=%async_computation.16 | async-start | bytes 11943936 | tf_op jit(solution)/shard_map/reduce_scatter | solution.py:234
  1248.2 604.6 %reduce-scatter.14.cloned.1.call-start = ((), (), s32[]{:S(2)}) async-start(), calls=%async_computation.15 | async-start | bytes 11943936 | tf_op jit(solution)/shard_map/reduce_scatter | solution.py:231
  1267.4 858.6 %reduce-scatter.18.cloned.1.call-start = ((), (), s32[]{:S(2)}) async-start(), calls=%async_computation.17 | async-start | bytes 17915904 | tf_op jit(solution)/shard_map/reduce_scatter | solution.py:322
  1273.9 854.1 %copy-start.42 = (bf16[1152]{0:T(1024)(128)(2,1)S(1)}, bf16[1152]{0:T(1024)(128)(2,1)}, u32[]{:S(2)}) copy-start(bf16[1152]{0:T(1024)(128)(2,1)} %get-tuple-element.93) | copy-start | bytes 6916
  1273.9 854.1 %copy-start.43 = (bf16[1152]{0:T(1024)(128)(2,1)S(1)}, bf16[1152]{0:T(1024)(128)(2,1)}, u32[]{:S(2)}) copy-start(bf16[1152]{0:T(1024)(128)(2,1)} %get-tuple-element.108) | copy-start | bytes 6916
  1273.9 854.1 %copy-start.44 = (bf16[4608]{0:T(1024)(128)(2,1)S(1)}, bf16[4608]{0:T(1024)(128)(2,1)}, u32[]{:S(2)}) copy-start(bf16[4608]{0:T(1024)(128)(2,1)} %get-tuple-element.122) | copy-start | bytes 27652
  1273.9 912.2 %reduce-scatter.22.cloned.1.call-start = ((), (), s32[]{:S(2)}) async-start(), calls=%async_computation.19 | async-start | bytes 331776
  1275.1 1035.2 %all-reduce.14.cloned.1.call-start = ((), (), s32[]{:S(2)}) async-start(), calls=%async_computation.20 | async-start | bytes 12533760 | tf_op jit(solution)/shard_map/psum | solution.py:337
  (54 other events, 1519.2 us)
Sparse Core Ops, SparseCore 0:
  10.3 53.7 all-gather.7
  66.3 216.4 all-gather.9
  285.0 117.7 all-gather.11
  404.8 52.4 all-gather.13
  459.3 151.7 all-gather.15
  613.2 150.6 all-gather.17
  1199.9 66.6 reduce-scatter.19
  1270.8 69.0 reduce-scatter.11
  1344.0 143.0 reduce-scatter.9
  1491.0 179.0 reduce-scatter.15
  1673.7 179.0 reduce-scatter.13
  1857.0 268.9 reduce-scatter.17
  2130.2 55.9 reduce-scatter.21
  2189.0 121.2 all-reduce.13
where the time goes:
time: 2340 us; the launch traced here: 2330 us
  waiting for transfers between devices  1530 us (65%)
  matrix products  583 us (25%)
  blocking collectives  81.4 us (3%)
  other arithmetic  78 us (3%)
  local copies, waits for them, and re-layouts  35.5 us (2%)
    reduce_scatter x1, waiting for transfers between devices, body(): lax.psum_scatter(ada_weight_g.astype(jnp.bfloat16), 'fsdp', scatter_dimen...  273 us
    all_gather x1, waiting for transfers between devices, body(): lax.all_gather(ada_weight, 'fsdp', axis=0, tiled=True)  210 us
    reduce_scatter x1, waiting for transfers between devices, body(): lax.psum_scatter(down_weight_g.astype(jnp.bfloat16), 'fsdp', scatter_dime...  183 us
    reduce_scatter x1, waiting for transfers between devices, body(): lax.psum_scatter(up_weight_g.astype(jnp.bfloat16), 'fsdp', scatter_dimens...  183 us
    reduce_scatter x1, waiting for transfers between devices, body(): lax.psum_scatter(qkv_weight_g.astype(jnp.bfloat16), 'fsdp', scatter_dimen...  147 us
    all_gather x1, waiting for transfers between devices, body(): lax.all_gather(down_weight, 'fsdp', axis=0, tiled=True)  132 us
    dot_general x2, matrix products, attend_backward(): jnp.einsum('hqk,qhd->khd', score_grad, query_block, preferred_element_typ...  121 us
    dot_general x2, matrix products, attend_backward(): jnp.einsum('hqk,khd->qhd', score_grad, key_rows, preferred_element_type=j...  115 us
  transfers between devices with their start and end apart: 14, of which 11 were waited for; matrix products, arithmetic and copies ran while one was open for 10% of the time, Pallas kernels for 0%

commit v1 on v0

v1 whole, which is shorter than its diff:
```python
import functools
import math

import jax
import jax.numpy as jnp
from jax import lax
from jax.experimental import pallas as pl
from jax.experimental.pallas import tpu as pltpu
from jax.sharding import PartitionSpec as P

LOG2E = 1.4426950408889634
ROWS_NT = (((1,), (1,)), ((), ()))
ROWS_NN = (((1,), (0,)), ((), ()))


def matmul(left, right, dims):
    return lax.dot_general(left, right, dims, preferred_element_type=jnp.float32)


def norm_forward(values):
    row_mean = jnp.mean(values, axis=-1, keepdims=True)
    centred = values - row_mean
    inverse = lax.rsqrt(jnp.mean(centred * centred, axis=-1, keepdims=True) + 1e-06)
    return (centred * inverse, inverse)


def norm_backward(gradient, normed, inverse):
    return inverse * (
        gradient
        - jnp.mean(gradient, axis=-1, keepdims=True)
        - normed * jnp.mean(gradient * normed, axis=-1, keepdims=True)
    )


def gelu_tanh(values):
    return jax.nn.gelu(values, approximate=True)


def head_window(head, head_size, width):
    tile = jnp.minimum((head * head_size) // 128, width // 128 - 2)
    base = pl.multiple_of(tile * 128, 128)
    lane = lax.broadcasted_iota(jnp.int32, (1, 256), 1) + (base - head * head_size)
    return base, (lane >= 0) & (lane < head_size)


def as_row(column):
    return jnp.transpose(jnp.broadcast_to(column, (column.shape[0], 128)))[0:1]


def attend_forward_kernel(keep_ref, qkv_ref, out_ref, lse_ref, *, head_size, width, rows):
    head = pl.program_id(0)
    base, mask = head_window(head, head_size, width)
    scale = head_size**-0.5 * LOG2E
    zero = jnp.zeros((), jnp.bfloat16)
    keys = qkv_ref[:, pl.ds(width + base, 256)]
    values = qkv_ref[:, pl.ds(2 * width + base, 256)]
    keep = keep_ref[head].astype(jnp.float32)
    for start in range(0, qkv_ref.shape[0], rows):
        block = (pl.ds(start, rows), pl.ds(base, 256))
        query = jnp.where(mask, qkv_ref[block], zero)
        scores = matmul(query, keys, ROWS_NT)
        top = jnp.max(scores, axis=-1, keepdims=True)
        probs = jnp.exp2((scores - top) * scale)
        total = jnp.sum(probs, axis=-1, keepdims=True)
        mixed = matmul(probs.astype(jnp.bfloat16), values, ROWS_NN)
        mixed = (mixed * (keep / total)).astype(jnp.bfloat16)
        out_ref[block] = jnp.where(mask, mixed, out_ref[block])
        lse_ref[pl.ds(head, 1), pl.ds(start, rows)] = as_row(top * scale + jnp.log2(total))


def attend_backward_kernel(
    keep_ref, qkv_ref, out_ref, grad_ref, lse_ref, dqkv_ref, *, head_size, width, rows
):
    head = pl.program_id(0)
    base, mask = head_window(head, head_size, width)
    scale = head_size**-0.5
    zero = jnp.zeros((), jnp.bfloat16)
    length = qkv_ref.shape[0]
    key_block = (slice(None), pl.ds(width + base, 256))
    value_block = (slice(None), pl.ds(2 * width + base, 256))
    keys = qkv_ref[key_block]
    values = qkv_ref[value_block]
    keys_across = jnp.transpose(keys)
    key_grad = jnp.zeros((length, 256), jnp.float32)
    value_grad = jnp.zeros((length, 256), jnp.float32)
    kept = mask & (keep_ref[head] > 0)
    for start in range(0, length, rows):
        block = (pl.ds(start, rows), pl.ds(base, 256))
        query = jnp.where(mask, qkv_ref[block], zero)
        grad = jnp.where(kept, grad_ref[block], zero)
        row_dot = as_row(
            jnp.sum(
                grad.astype(jnp.float32) * out_ref[block].astype(jnp.float32), axis=-1, keepdims=True
            )
        )
        lse = lse_ref[pl.ds(head, 1), pl.ds(start, rows)]
        probs = jnp.exp2(matmul(keys, query, ROWS_NT) * (scale * LOG2E) - lse)
        score_grad = (probs * (matmul(values, grad, ROWS_NT) - row_dot)).astype(jnp.bfloat16)
        value_grad = value_grad + matmul(probs.astype(jnp.bfloat16), grad, ROWS_NN)
        key_grad = key_grad + matmul(score_grad, query, ROWS_NN)
        query_grad = jnp.transpose(matmul(keys_across, score_grad, ROWS_NN)) * scale
        dqkv_ref[block] = jnp.where(mask, query_grad.astype(jnp.bfloat16), dqkv_ref[block])
    dqkv_ref[key_block] = jnp.where(
        mask, (key_grad * scale).astype(jnp.bfloat16), dqkv_ref[key_block]
    )
    dqkv_ref[value_block] = jnp.where(mask, value_grad.astype(jnp.bfloat16), dqkv_ref[value_block])


def whole(shape):
    return pl.BlockSpec(shape, lambda *_: (0,) * len(shape), pipeline_mode=pl.Buffered(1))


def attend_forward(qkv, keep, rows=512):
    length, triple = qkv.shape
    width, heads = triple // 3, keep.shape[0]
    cells = heads * length * length
    return pl.pallas_call(
        functools.partial(
            attend_forward_kernel, head_size=width // heads, width=width, rows=min(rows, length)
        ),
        grid=(heads,),
        in_specs=[pl.BlockSpec(memory_space=pltpu.SMEM), whole((length, triple))],
        out_specs=[
            pl.BlockSpec((length, width), lambda head: (0, 0)),
            pl.BlockSpec((heads, length), lambda head: (0, 0)),
        ],
        out_shape=[
            jax.ShapeDtypeStruct((length, width), jnp.bfloat16),
            jax.ShapeDtypeStruct((heads, length), jnp.float32),
        ],
        compiler_params=pltpu.CompilerParams(vmem_limit_bytes=48 << 20),
        cost_estimate=pl.CostEstimate(
            flops=cells * 1024, transcendentals=cells, bytes_accessed=length * width * 8
        ),
        name="attend_forward",
    )(keep, qkv)


def attend_backward(qkv, out, grad, lse, keep, rows=256):
    length, triple = qkv.shape
    width, heads = triple // 3, keep.shape[0]
    cells = heads * length * length
    return pl.pallas_call(
        functools.partial(
            attend_backward_kernel, head_size=width // heads, width=width, rows=min(rows, length)
        ),
        grid=(heads,),
        in_specs=[
            pl.BlockSpec(memory_space=pltpu.SMEM),
            whole((length, triple)),
            whole((length, width)),
            whole((length, width)),
            whole((heads, length)),
        ],
        out_specs=pl.BlockSpec((length, triple), lambda head: (0, 0)),
        out_shape=jax.ShapeDtypeStruct((length, triple), jnp.bfloat16),
        compiler_params=pltpu.CompilerParams(vmem_limit_bytes=56 << 20),
        cost_estimate=pl.CostEstimate(
            flops=cells * 2560, transcendentals=cells, bytes_accessed=length * width * 16
        ),
        name="attend_backward",
    )(keep, qkv, out, grad, lse)


def gather_rows(rows, axis, size):
    place = lax.axis_index(axis)
    step = 1
    while step < size:
        other = lax.ppermute(rows, axis, [(i, i ^ step) for i in range(size)])
        high = (place // step) % 2 == 1
        rows = jnp.concatenate([jnp.where(high, other, rows), jnp.where(high, rows, other)], axis=0)
        step *= 2
    return rows


def conditioning(times, labels, table, shard, width):
    class_count, columns = table.shape
    half = width // 2
    column = shard * columns + jnp.arange(columns, dtype=jnp.int32)
    frequency = jnp.exp(-math.log(10000.0) * (column % half).astype(jnp.float32) / half)
    angles = times.astype(jnp.float32)[:, None] * frequency[None, :]
    embed = jnp.where(column[None, :] < half, jnp.cos(angles), jnp.sin(angles))
    picked = labels[:, None] == jnp.arange(class_count, dtype=jnp.int32)[None, :]
    return embed + jnp.dot(
        picked.astype(jnp.bfloat16), table, preferred_element_type=jnp.float32
    )


def own_part(values, shard, size):
    return lax.dynamic_slice_in_dim(values, shard * size, size, axis=values.ndim - 1)


def body(
    shard_count,
    image_count,
    tokens,
    timesteps,
    labels,
    head_keep,
    chan_keep,
    cotangent,
    qkv_weight,
    qv_bias,
    out_weight,
    out_bias,
    up_weight,
    up_bias,
    down_weight,
    down_bias,
    ada_weight,
    ada_bias,
    class_table,
):
    _, length, width = tokens.shape
    hidden = chan_keep.shape[1]
    class_count = class_table.shape[0]
    columns = width // shard_count
    group_count = image_count // shard_count
    shard = lax.axis_index("fsdp")
    bf16, f32 = jnp.bfloat16, jnp.float32

    facts = gather_rows(jnp.stack([timesteps, labels], axis=1), "fsdp", shard_count)
    group_act = jax.nn.silu(
        conditioning(facts[:, 0], facts[:, 1], class_table, shard, width)
    ).astype(bf16)
    partial = jnp.dot(group_act, ada_weight, preferred_element_type=f32)
    bias_row = lax.dynamic_update_slice_in_dim(
        jnp.zeros((6 * width,), f32), ada_bias.astype(f32), shard * ada_bias.shape[0], axis=0
    )
    small = jnp.concatenate([qv_bias.reshape(-1), out_bias, up_bias, down_bias]).astype(f32)
    sent = jnp.concatenate(
        [partial + bias_row, jnp.broadcast_to(small, (shard_count, small.shape[0]))], axis=1
    )
    parts = lax.all_to_all(sent, "fsdp", 0, 0, tiled=True)
    ada_rows = jnp.sum(parts[:, : 6 * width], axis=0).reshape(6, 1, width)
    shift_attn, scale_attn, gate_attn, shift_mlp, scale_mlp, gate_mlp = [ada_rows[i] for i in range(6)]
    small = parts[:, 6 * width :]
    query_bias = small[:, :columns].reshape(-1)
    value_bias = small[:, columns : 2 * columns].reshape(-1)
    out_bias_full = small[:, 2 * columns : 3 * columns].reshape(-1)
    up_end = 3 * columns + up_bias.shape[0]
    up_bias_full = small[:, 3 * columns : up_end].reshape(-1)
    down_bias_full = small[:, up_end:].reshape(-1)

    qkv_full = lax.all_gather(qkv_weight, "fsdp", axis=0, tiled=True)
    out_full = lax.all_gather(out_weight, "fsdp", axis=0, tiled=True)
    up_full = lax.all_gather(up_weight, "fsdp", axis=0, tiled=True)
    down_full = lax.all_gather(down_weight, "fsdp", axis=0, tiled=True)

    inputs = tokens[0].astype(f32)
    normed_one, inverse_one = norm_forward(inputs)
    mod_one = (normed_one * (1.0 + scale_attn) + shift_attn).astype(bf16)
    qkv_bias = jnp.concatenate([query_bias, jnp.zeros((width,), f32), value_bias])
    qkv = (jnp.dot(mod_one, qkv_full, preferred_element_type=f32) + qkv_bias).astype(bf16)
    attn_low, lse = attend_forward(qkv, head_keep[0])
    attn_branch = jnp.dot(attn_low, out_full, preferred_element_type=f32) + out_bias_full
    middle = inputs + gate_attn * attn_branch
    normed_two, inverse_two = norm_forward(middle)
    mod_two = (normed_two * (1.0 + scale_mlp) + shift_mlp).astype(bf16)
    pre_act = jnp.dot(mod_two, up_full, preferred_element_type=f32) + up_bias_full
    chan_mask = chan_keep.astype(f32)
    act_low = (gelu_tanh(pre_act) * chan_mask).astype(bf16)
    mlp_branch = jnp.dot(act_low, down_full, preferred_element_type=f32) + down_bias_full
    block_out = (middle + gate_mlp * mlp_branch).astype(bf16)

    out_grad = cotangent[0].astype(f32)
    gate_mlp_grad = jnp.sum(out_grad * mlp_branch, axis=0)
    branch_grad = (out_grad * gate_mlp).astype(bf16)
    down_bias_g = jnp.sum(branch_grad.astype(f32), axis=0)
    down_weight_g = jnp.einsum("tf,td->fd", act_low, branch_grad, preferred_element_type=f32)
    act_grad = jnp.einsum("td,fd->tf", branch_grad, down_full, preferred_element_type=f32)
    _, gelu_pull = jax.vjp(gelu_tanh, pre_act)
    pre_grad = gelu_pull(act_grad * chan_mask)[0].astype(bf16)
    up_bias_g = jnp.sum(pre_grad.astype(f32), axis=0)
    up_weight_g = jnp.einsum("td,tf->df", mod_two, pre_grad, preferred_element_type=f32)
    mod_two_grad = jnp.einsum("tf,df->td", pre_grad, up_full, preferred_element_type=f32)
    mlp_grads = lax.optimization_barrier(
        (down_weight_g.astype(bf16), up_weight_g.astype(bf16), mod_two_grad)
    )
    down_weight_g, up_weight_g, mod_two_grad = mlp_grads

    def reduce(grad):
        return lax.psum(
            lax.psum_scatter(grad, "fsdp", scatter_dimension=0, tiled=True), "dp"
        ).astype(f32)

    down_shard = reduce(down_weight_g)
    up_shard = reduce(up_weight_g)
    scale_mlp_grad = jnp.sum(mod_two_grad * normed_two, axis=0)
    shift_mlp_grad = jnp.sum(mod_two_grad, axis=0)
    middle_grad = out_grad + norm_backward(
        mod_two_grad * (1.0 + scale_mlp), normed_two, inverse_two
    )
    gate_attn_grad = jnp.sum(middle_grad * attn_branch, axis=0)
    attn_grad = (middle_grad * gate_attn).astype(bf16)
    out_bias_g = jnp.sum(attn_grad.astype(f32), axis=0)
    out_weight_g = jnp.einsum("td,te->de", attn_low, attn_grad, preferred_element_type=f32)
    low_grad = jnp.einsum("te,de->td", attn_grad, out_full, preferred_element_type=f32).astype(bf16)
    out_weight_g, low_grad = lax.optimization_barrier((out_weight_g.astype(bf16), low_grad))
    out_shard = reduce(out_weight_g)
    qkv_grad = attend_backward(qkv, attn_low, low_grad, lse, head_keep[0])
    qkv_weight_g = jnp.einsum("td,te->de", mod_one, qkv_grad, preferred_element_type=f32)
    qkv_weight_g, qkv_grad = lax.optimization_barrier((qkv_weight_g.astype(bf16), qkv_grad))
    qkv_shard = reduce(qkv_weight_g)
    bias_sums = jnp.sum(qkv_grad.astype(f32), axis=0)
    mod_one_grad = jnp.einsum("te,de->td", qkv_grad, qkv_full, preferred_element_type=f32)
    scale_attn_grad = jnp.sum(mod_one_grad * normed_one, axis=0)
    shift_attn_grad = jnp.sum(mod_one_grad, axis=0)
    tokens_grad = (
        middle_grad + norm_backward(mod_one_grad * (1.0 + scale_attn), normed_one, inverse_one)
    ).astype(bf16)

    row = jnp.concatenate(
        [
            shift_attn_grad,
            scale_attn_grad,
            gate_attn_grad,
            shift_mlp_grad,
            scale_mlp_grad,
            gate_mlp_grad,
            bias_sums[:width],
            bias_sums[2 * width :],
            out_bias_g,
            up_bias_g,
            down_bias_g,
        ]
    ).astype(bf16)[None]
    rows = gather_rows(gather_rows(row, "fsdp", shard_count), "dp", group_count)
    all_facts = gather_rows(facts, "dp", group_count)
    cond = conditioning(all_facts[:, 0], all_facts[:, 1], class_table, shard, width)
    cond_act, silu_pull = jax.vjp(jax.nn.silu, cond)
    ada_grad = rows[:, : 6 * width]
    ada_weight_g = jnp.einsum(
        "sd,se->de", cond_act.astype(bf16), ada_grad, preferred_element_type=f32
    )
    cond_act_grad = jnp.einsum("se,de->sd", ada_grad, ada_weight, preferred_element_type=f32)
    cond_grad = silu_pull(cond_act_grad)[0]
    picked = all_facts[:, 1][:, None] == jnp.arange(class_count, dtype=jnp.int32)[None, :]
    table_g = jnp.einsum(
        "sc,sd->cd", picked.astype(f32), cond_grad, precision=lax.Precision.HIGHEST
    )
    sums = jnp.sum(rows.astype(f32), axis=0)
    ada_bias_g = own_part(sums[: 6 * width], shard, ada_bias.shape[0])
    qv_bias_g = own_part(sums[6 * width : 8 * width].reshape(2, width), shard, columns)
    out_bias_g = own_part(sums[8 * width : 9 * width], shard, columns)
    up_bias_g = own_part(sums[9 * width : 9 * width + hidden], shard, up_bias.shape[0])
    down_bias_g = own_part(sums[9 * width + hidden :], shard, columns)
    return (
        block_out[None],
        tokens_grad[None],
        qkv_shard,
        qv_bias_g,
        out_shard,
        out_bias_g,
        up_shard,
        up_bias_g,
        down_shard,
        down_bias_g,
        ada_weight_g,
        ada_bias_g,
        table_g,
    )


def solution(mesh):
    shard_count = mesh.shape["fsdp"]
    image_count = shard_count * mesh.shape["dp"]
    images = ("fsdp", "dp")
    return jax.shard_map(
        functools.partial(body, shard_count, image_count),
        mesh=mesh,
        in_specs=(
            P(images, None, None),
            P(images),
            P(images),
            P(images, None),
            P(images, None),
            P(images, None, None),
            P("fsdp", None),
            P(None, "fsdp"),
            P("fsdp", None),
            P("fsdp"),
            P("fsdp", None),
            P("fsdp"),
            P("fsdp", None),
            P("fsdp"),
            P("fsdp", None),
            P("fsdp"),
            P(None, "fsdp"),
        ),
        out_specs=(
            P(images, None, None),
            P(images, None, None),
            P("fsdp", None),
            P(None, "fsdp"),
            P("fsdp", None),
            P("fsdp"),
            P("fsdp", None),
            P("fsdp"),
            P("fsdp", None),
            P("fsdp"),
            P("fsdp", None),
            P("fsdp"),
            P(None, "fsdp"),
        ),
        check_vma=False,
    )
```

time: 2340 us -> 1310 us (0.56)
  waiting for transfers between devices: 1530 us -> 908 us
  matrix products: 583 us -> 212 us
  Pallas kernels: 0 us -> 97.8 us
  blocking collectives: 81.4 us -> 0 us
  other arithmetic: 78 us -> 35.9 us
    reduce_scatter x6 -> x4, waiting for transfers between devices: 851 us -> 447 us  [reduce(): lax.psum_scatter(grad, 'fsdp', scatter_dimension=0, tiled=True)]
    dot_general x27 -> x17, matrix products: 583 us -> 212 us  [the longest x1 29.1 us: body(): jnp.einsum('td,fd->tf', branch_grad, down_full, preferred_element_type=f32)]
    all_gather x6 -> x4, waiting for transfers between devices: 535 us -> 338 us  [the longest x1 142 us: body(): up_full = lax.all_gather(up_weight, 'fsdp', axis=0, tiled=True)]
    pallas_call x0 -> x2, Pallas kernels: none -> 97.8 us  [the longest x1 60.8 us: attend_backward(): pl.pallas_call(functools.partial(attend_backward_kernel, head_size=width...]
    unnamed x2 -> x0, blocking collectives: 55.8 us -> none
    psum x1, waiting for transfers between devices: 113 us -> 73.6 us  [reduce(): lax.psum(lax.psum_scatter(grad, 'fsdp', scatter_dimension=0, tiled=True),...]
    ppermute x0 -> x10, waiting for transfers between devices: none -> 35.2 us  [gather_rows(): other = lax.ppermute(rows, axis, [(i, i ^ step) for i in range(size)])]
    unnamed x15 -> x9, waiting for transfers between devices: 33.4 us -> 3.34 us
  transfers between devices with their start and end apart: 14 -> 20, of which waited for: 11 -> 14; matrix products, arithmetic and copies ran while one was open for 10% -> 10% of each run, Pallas kernels for 0% -> 7%
where the time goes in v1:
time: 1310 us; the launch traced here: 1300 us
  waiting for transfers between devices  908 us (69%)
  matrix products  212 us (16%)
  Pallas kernels  97.8 us (7%)
  other arithmetic  35.9 us (3%)
  local copies, waits for them, and re-layouts  18.4 us (1%)
  between operations  16.1 us (1%)
  starting transfers between devices  15.7 us (1%)
    reduce_scatter x4, waiting for transfers between devices, reduce(): lax.psum_scatter(grad, 'fsdp', scatter_dimension=0, tiled=True)  447 us
    all_gather x1, waiting for transfers between devices, body(): up_full = lax.all_gather(up_weight, 'fsdp', axis=0, tiled=True)  142 us
    all_gather x1, waiting for transfers between devices, body(): down_full = lax.all_gather(down_weight, 'fsdp', axis=0, tiled=True)  108 us
    all_gather x1, waiting for transfers between devices, body(): qkv_full = lax.all_gather(qkv_weight, 'fsdp', axis=0, tiled=True)  88.1 us
    psum x1, waiting for transfers between devices, reduce(): lax.psum(lax.psum_scatter(grad, 'fsdp', scatter_dimension=0, tiled=True),...  73.6 us
    pallas_call x1, Pallas kernels, attend_backward(): pl.pallas_call(functools.partial(attend_backward_kernel, head_size=width...  60.8 us
    pallas_call x1, Pallas kernels, attend_forward(): pl.pallas_call(functools.partial(attend_forward_kernel, head_size=width /...  37 us
    ppermute x10, waiting for transfers between devices, gather_rows(): other = lax.ppermute(rows, axis, [(i, i ^ step) for i in range(size)])  35.2 us
  transfers between devices with their start and end apart: 20, of which 14 were waited for; matrix products, arithmetic and copies ran while one was open for 10% of the time, Pallas kernels for 7%

profile of v1, /device:TPU:1, one launch (start us, length us, event | category | flops | bytes accessed | tf_op | source)
XLA Modules:
  0.0 1304.7 jit_solution(12385247216375214913)
XLA Ops:
  37.1 10.8 all-to-all-done
  49.2 88.1 %all-gather.5.cloned.1.call-done = bf16[1152,3456]{1,0:T(8,128)(2,1)} async-done(((bf16[144,3456]{1,0:T(8,128)(2,1)}), bf16[1152,3456]{1,0:T(8,128)(2,1)}) %all-gather.5.cloned.1.call-update) | async-done | bytes 7962640 | tf_op jit(solution)/shard_map/all_gather | solution.py:245
  137.3 15.7 %add_convert_fusion.qkv_ref = bf16[1024,3456]{1,0:T(8,128)(2,1)} fusion(bf16[1152,3456]{1,0:T(8,128)(2,1)} %all-gather.5.cloned.1.call-done, f32[3456]{0:T(1024)S(1)} %pad_maximum_fusion.5, bf16[1,1024,1152]{2,1,0:T(8,128)(2,1)} %param.17, f32[1152]{0:T(1024)S(1)} %get-tuple-element.76, f32[1152]{0:T(1024)S(1)} %get-tuple-element.77, ...), kind=kOutput, calls=%fused_computation.13 | convolution fusion | flops 8167882752 | bytes 17431040 | tf_op jit(solution)/shard_map/dot_general | solution.py:254
  153.0 37.0 %attend_forward.1 = (bf16[1024,1152]{1,0:T(8,128)(2,1)S(1)}, f32[16,1024]{1,0:T(8,128)S(1)}) custom-call(s32[16]{0:T(128)S(1)} %bitcast.98, bf16[1024,3456]{1,0:T(8,128)(2,1)} %add_convert_fusion.qkv_ref), custom_call_target="tpu_custom_call" | custom-call | flops 17179869184 | bytes 9437184 | tf_op jit(solution)/shard_map/attend_forward/pallas_call | solution.py:117
  192.1 9.0 fusion.64
  203.9 142.0 %all-gather.9.cloned.1.call-done = bf16[1152,4608]{1,0:T(8,128)(2,1)} async-done(((bf16[144,4608]{1,0:T(8,128)(2,1)}), bf16[1152,4608]{1,0:T(8,128)(2,1)}) %all-gather.9.cloned.1.call-update) | async-done | bytes 10616848 | tf_op jit(solution)/shard_map/all_gather | solution.py:247
  345.9 20.9 %fusion.62 = f32[1024,4608]{1,0:T(8,128)} fusion(bf16[1152,4608]{1,0:T(8,128)(2,1)} %all-gather.9.cloned.1.call-done, f32[1024,1152]{1,0:T(8,128)} %copy-done.7, f32[1152]{0:T(1024)S(1)} %get-tuple-element.74, f32[1152]{0:T(1024)S(1)} %get-tuple-element.75, f32[1024]{0:T(1024)S(1)} %add_rsqrt_fusion, f32[1024]{0:T(1024)S(1)} %broadcast_multiply_fusion.4), kind=kOutput, calls=%fused_computation.162 | convolution fusion | flops 10877534208 | bytes 34227200 | tf_op jit(solution)/shard_map/dot_general | solution.py:260
  366.8 23.5 %convolution_convert_fusion.1 = bf16[4608,1152]{1,0:T(8,128)(2,1)} fusion(bf16[1,1024,1152]{2,1,0:T(8,128)(2,1)S(1)} %copy-done.8, f32[1152]{0:T(1024)S(1)} %get-tuple-element.73, f32[1024,4608]{1,0:T(8,128)} %fusion.62, f32[4608]{0:T(1024)S(1)} %convert_reduce_fusion.2, f32[4608]{0:T(1024)S(1)} %add.232), kind=kOutput, calls=%fused_computation.3 | convolution fusion | flops 10932387840 | bytes 31891968 | tf_op jit(solution)/shard_map/tf,td->fd/dot_general | solution.py:270
  390.3 108.3 %all-gather.11.cloned.1.call-done = bf16[4608,1152]{1,0:T(8,128)(2,1)} async-done(((bf16[576,1152]{1,0:T(8,128)(2,1)}), bf16[4608,1152]{1,0:T(8,128)(2,1)}) %all-gather.11.cloned.1.call-update) | async-done | bytes 10616848 | tf_op jit(solution)/shard_map/all_gather | solution.py:248
  498.6 29.1 %fusion.70 = (bf16[4608]{0:T(1024)(128)(2,1)}, bf16[1024,4608]{1,0:T(8,128)(2,1)S(1)}) fusion(f32[1024,4608]{1,0:T(8,128)} %fusion.62, f32[4608]{0:T(1024)S(1)} %add.232, f32[4608]{0:T(1024)S(1)} %convert_reduce_fusion.2, bf16[4608,1152]{1,0:T(8,128)(2,1)} %all-gather.11.cloned.1.call-done, bf16[1,1024,1152]{2,1,0:T(8,128)(2,1)} %param.22, ...), kind=kOutput, calls=%fused_computation.169 | convolution fusion | flops 10983698432 | bytes 41338368 | tf_op jit(solution)/shard_map/td,fd->tf/dot_general | solution.py:271
  531.3 16.7 %convolution_convert_fusion = bf16[1152,4608]{1,0:T(8,128)(2,1)} fusion(bf16[1024,4608]{1,0:T(8,128)(2,1)S(1)} %get-tuple-element.98, f32[1024,1152]{1,0:T(8,128)} %copy-done.7, f32[1152]{0:T(1024)S(1)} %get-tuple-element.74, f32[1152]{0:T(1024)S(1)} %get-tuple-element.75, f32[1024]{0:T(1024)S(1)} %add_rsqrt_fusion, f32[1024]{0:T(1024)S(1)} %broadcast_multiply_fusion.4), kind=kOutput, calls=%fused_computation.2 | convolution fusion | flops 10882842624 | bytes 24790016 | tf_op jit(solution)/shard_map/td,tf->df/dot_general | solution.py:275
  548.0 18.3 %fusion.71 = f32[1024,1152]{1,0:T(8,128)} fusion(bf16[1024,4608]{1,0:T(8,128)(2,1)} %copy-done.36, bf16[1152,4608]{1,0:T(8,128)(2,1)} %all-gather.9.cloned.1.call-done), kind=kOutput, calls=%fused_computation.170 | convolution fusion | flops 10871635968 | bytes 24772608 | tf_op jit(solution)/shard_map/tf,df->td/dot_general | solution.py:276
  566.3 28.9 %fusion.25 = (bf16[1152]{0:T(1024)(128)(2,1)S(1)}, bf16[1,1024,1152]{2,1,0:T(8,128)(2,1)}, bf16[1152]{0:T(1024)(128)(2,1)S(1)}, f32[1024]{0:T(1024)S(1)}, f32[1024]{0:T(1024)S(1)}, /*index=5*/bf16[1152]{0:T(1024)(128)(2,1)S(1)}) fusion(bf16[1,1024,1152]{2,1,0:T(8,128)(2,1)} %param.22, f32[1024,1152]{1,0:T(8,128)} %copy-done.7, ...), kind=kOutput, calls=%fused_computation.40 | convolution fusion | flops 10942409728 | bytes 43720960 | tf_op jit(solution)/shard_map/dot_general | solution.py:263
  595.3 7.5 fusion.63
  609.0 7.4 convolution_convert_fusion.4.grad_ref
  616.5 60.8 %attend_backward.1 = bf16[1024,3456]{1,0:T(8,128)(2,1)} custom-call(s32[16]{0:T(128)} %bitcast.97, bf16[1024,3456]{1,0:T(8,128)(2,1)} %add_convert_fusion.qkv_ref, bf16[1024,1152]{1,0:T(8,128)(2,1)} %copy-done.2, bf16[1024,1152]{1,0:T(8,128)(2,1)} %convolution_convert_fusion.4.grad_ref, f32[16,1024]{1,0:T(8,128)} %copy-done.4), custom_call_target="tpu_custom_call" | custom-call | flops 42949672960 | bytes 18874368 | tf_op jit(solution)/shard_map/attend_backward/pallas_call | solution.py:143
  677.4 14.3 %convolution_convert_fusion.2 = bf16[1152,3456]{1,0:T(8,128)(2,1)} fusion(bf16[1024,3456]{1,0:T(8,128)(2,1)} %attend_backward.1, bf16[1,1024,1152]{2,1,0:T(8,128)(2,1)S(1)} %copy-done.5, f32[1152]{0:T(1024)S(1)} %copy-done.28, f32[1152]{0:T(1024)S(1)} %copy-done.17, f32[1024]{0:T(1024)S(1)} %copy-done.21, f32[1024]{0:T(1024)S(1)} %copy-done.15), kind=kOutput, calls=%fused_computation.12 | convolution fusion | flops 8164786176 | bytes 17417216 | tf_op jit(solution)/shard_map/td,te->de/dot_general | solution.py:302
  696.8 16.0 %fusion.22 = (bf16[1152]{0:T(1024)(128)(2,1)S(1)}, f32[1024]{0:T(1024)S(1)}, f32[1024]{0:T(1024)S(1)}, bf16[1152]{0:T(1024)(128)(2,1)S(1)}, f32[1024,1152]{1,0:T(8,128)S(1)}) fusion(bf16[1,1024,1152]{2,1,0:T(8,128)(2,1)} %param.17, f32[1024]{0:T(1024)S(1)} %copy-done.21, f32[1024]{0:T(1024)S(1)} %copy-done.15, f32[1152]{0:T(1024)S(1)} %copy-done.17, ...), kind=kOutput, calls=%fused_computation.37 | convolution fusion | flops 8165519360 | bytes 22144000 | tf_op jit(solution)/shard_map/te,de->td/dot_general | solution.py:306
  723.6 9.1 collective-permute-done.4
  733.2 17.7 %collective-permute-done.5 = bf16[4,16128]{1,0:T(4,128)(2,1)S(1)} collective-permute-done((bf16[4,16128]{1,0:T(4,128)(2,1)S(1)}, bf16[4,16128]{1,0:T(4,128)(2,1)S(1)}, u32[]{:S(2)}, u32[]{:S(2)}) %collective-permute-start.5) | collective-permute-done | bytes 129056 | tf_op jit(solution)/shard_map/ppermute | solution.py:169
  758.0 81.5 %reduce-scatter.5.cloned.1.call-done = bf16[144,3456]{1,0:T(8,128)(2,1)} async-done(((bf16[1152,3456]{1,0:T(8,128)(2,1)}), bf16[144,3456]{1,0:T(8,128)(2,1)}) %reduce-scatter.5.cloned.1.call-update) | async-done | bytes 995344 | tf_op jit(solution)/shard_map/reduce_scatter | solution.py:284
  839.5 183.1 %reduce-scatter.9.cloned.1.call-done = bf16[144,4608]{1,0:T(8,128)(2,1)} async-done(((bf16[1152,4608]{1,0:T(8,128)(2,1)}), bf16[144,4608]{1,0:T(8,128)(2,1)}) %reduce-scatter.9.cloned.1.call-update) | async-done | bytes 1327120 | tf_op jit(solution)/shard_map/reduce_scatter | solution.py:284
  1022.6 182.6 %reduce-scatter.11.cloned.1.call-done = bf16[576,1152]{1,0:T(8,128)(2,1)} async-done(((bf16[4608,1152]{1,0:T(8,128)(2,1)}), bf16[576,1152]{1,0:T(8,128)(2,1)}) %reduce-scatter.11.cloned.1.call-update) | async-done | bytes 1327120 | tf_op jit(solution)/shard_map/reduce_scatter | solution.py:284
  1216.3 73.6 %all-reduce.3.cloned.1.call-done = (bf16[144,3456]{1,0:T(8,128)(2,1)}, bf16[144,1152]{1,0:T(8,128)(2,1)}, bf16[144,4608]{1,0:T(8,128)(2,1)}, bf16[576,1152]{1,0:T(8,128)(2,1)}) async-done(((bf16[144,3456]{1,0:T(8,128)(2,1)}, bf16[144,1152]{1,0:T(8,128)(2,1)}, bf16[144,4608]{1,0:T(8,128)(2,1)}, bf16[576,1152]{1,0:T(8,128)(2,1)}), (bf16[144,3456]{1,0:T(8,128)(2,1)}, bf16[144,1152]{1,0:T(8,128)(2,1)}, ...) | async-done | bytes 3981328 | tf_op jit(solution)/shard_map/psum | solution.py:283
  (207 shorter events, 86.7 us)
Async XLA Ops:
  7.2 130.1 %all-gather.5.cloned.1.call-start = ((), (), s32[]{:S(2)}) async-start(), calls=%async_computation.5 | async-start | bytes 8957952 | tf_op jit(solution)/shard_map/all_gather | solution.py:245
  7.9 184.1 %all-gather.7.cloned.1.call-start = ((), (), s32[]{:S(2)}) async-start(), calls=%async_computation.6 | async-start | bytes 2985984 | tf_op jit(solution)/shard_map/all_gather | solution.py:246
  8.7 337.2 %all-gather.9.cloned.1.call-start = ((), (), s32[]{:S(2)}) async-start(), calls=%async_computation.7 | async-start | bytes 11943936 | tf_op jit(solution)/shard_map/all_gather | solution.py:247
  9.4 489.2 %all-gather.11.cloned.1.call-start = ((), (), s32[]{:S(2)}) async-start(), calls=%async_computation.8 | async-start | bytes 11943936 | tf_op jit(solution)/shard_map/all_gather | solution.py:248
  11.3 8.7 collective-permute-start
  20.0 133.0 %copy-start.14 = (f32[1024]{0:T(1024)}, f32[1024]{0:T(1024)S(1)}, u32[]{:S(2)}) copy-start(f32[1024]{0:T(1024)S(1)} %broadcast_multiply_fusion.5) | copy-start | bytes 12292
  20.1 2.4 collective-permute-start.1
  22.7 4.8 collective-permute-start.2
  29.9 17.9 %all-to-all-start = ((f32[8,1,8064]{2,1,0:T(1,128)}), f32[8,1,8064]{2,1,0:T(1,128)S(1)}, u32[]{:S(2)}, u32[]{:S(2)}) async-start(f32[8,1,8064]{2,1,0:T(1,128)} %copy.31), calls=%async_computation | async-start | bytes 516096 | tf_op jit(solution)/shard_map/all_to_all | solution.py:234
  34.0 724.0 %reduce-scatter.7.cloned.1.call-start = ((), (), s32[]{:S(2)}) async-start(), calls=%async_computation.10 | async-start | bytes 2985984 | tf_op jit(solution)/shard_map/reduce_scatter | solution.py:284
  37.0 115.9 %copy-start.20 = (f32[1024]{0:T(1024)}, f32[1024]{0:T(1024)S(1)}, u32[]{:S(2)}) copy-start(f32[1024]{0:T(1024)S(1)} %add_rsqrt_fusion.1) | copy-start | bytes 12292
  49.1 103.8 %copy-start.16 = (f32[1152]{0:T(1024)}, f32[1152]{0:T(1024)S(1)}, u32[]{:S(2)}) copy-start(f32[1152]{0:T(1024)S(1)} %get-tuple-element.77) | copy-start | bytes 13828
  49.2 142.9 %copy-start.18 = (f32[1152]{0:T(1024)}, f32[1152]{0:T(1024)S(1)}, u32[]{:S(2)}) copy-start(f32[1152]{0:T(1024)S(1)} %get-tuple-element.78) | copy-start | bytes 13828
  616.4 223.1 %reduce-scatter.5.cloned.1.call-start = ((), (), s32[]{:S(2)}) async-start(), calls=%async_computation.9 | async-start | bytes 8957952 | tf_op jit(solution)/shard_map/reduce_scatter | solution.py:284
  691.6 330.9 %reduce-scatter.9.cloned.1.call-start = ((), (), s32[]{:S(2)}) async-start(), calls=%async_computation.11 | async-start | bytes 11943936 | tf_op jit(solution)/shard_map/reduce_scatter | solution.py:284
  692.4 512.8 %reduce-scatter.11.cloned.1.call-start = ((), (), s32[]{:S(2)}) async-start(), calls=%async_computation.12 | async-start | bytes 11943936 | tf_op jit(solution)/shard_map/reduce_scatter | solution.py:284
  718.1 3.6 collective-permute-start.3
  718.5 571.3 %all-reduce.3.cloned.1.call-start = ((), (), s32[]{:S(2)}) async-start(), calls=%async_computation.13 | async-start | bytes 7962624 | tf_op jit(solution)/shard_map/psum | solution.py:283
  722.0 10.6 collective-permute-start.4
  722.1 10.9 collective-permute-start.8
  733.0 17.9 %collective-permute-start.5 = (bf16[4,16128]{1,0:T(4,128)(2,1)S(1)}, bf16[4,16128]{1,0:T(4,128)(2,1)S(1)}, u32[]{:S(2)}, u32[]{:S(2)}) collective-permute-start(bf16[4,16128]{1,0:T(4,128)(2,1)S(1)} %pad_maximum_fusion.3), channel_id=1, source_target_pairs={{0,16},{4,20},{8,24},{12,28},{16,0},{20,4},{24,8},{28,12},{1,17},{... | collective-permute-start | bytes 387080 | tf_op jit(solution)/shard_map/ppermute | solution.py:169
  751.2 3.3 collective-permute-start.6
  751.7 2.8 collective-permute-start.9
  755.8 449.5 %collective-permute-start.7 = (bf16[16,16128]{1,0:T(8,128)(2,1)S(1)}, bf16[16,16128]{1,0:T(8,128)(2,1)}, u32[]{:S(2)}, u32[]{:S(2)}) collective-permute-start(bf16[16,16128]{1,0:T(8,128)(2,1)S(1)} %pad_maximum_fusion.1), channel_id=1, source_target_pairs={{0,2},{1,3},{2,0},{3,1},{4,6},{5,7},{6,4},{7,5},{8,10},{9,11},{10,... | collective-permute-start | bytes 1548296 | tf_op jit(solution)/shard_map/ppermute | solution.py:169
  (35 other events, 836.5 us)
Sparse Core Ops, SparseCore 0:
  10.2 127.0 all-gather.4
  139.4 52.3 all-gather.6
  194.0 151.8 all-gather.8
  348.0 150.6 all-gather.10
  616.5 67.7 reduce-scatter.6
  691.8 147.7 reduce-scatter.4
  843.5 178.9 reduce-scatter.8
  1026.2 179.0 reduce-scatter.10
  1208.0 81.7 all-reduce.2

commit v2 on v1

--- a/solution.py
+++ b/solution.py
@@ -32,10 +32,6 @@
     )
 
 
-def gelu_tanh(values):
-    return jax.nn.gelu(values, approximate=True)
-
-
 def head_window(head, head_size, width):
     tile = jnp.minimum((head * head_size) // 128, width // 128 - 2)
     base = pl.multiple_of(tile * 128, 128)
@@ -47,17 +43,21 @@
     return jnp.transpose(jnp.broadcast_to(column, (column.shape[0], 128)))[0:1]
 
 
-def attend_forward_kernel(keep_ref, qkv_ref, out_ref, lse_ref, *, head_size, width, rows):
+def attend_forward_kernel(
+    keep_ref, query_ref, key_ref, value_ref, out_ref, lse_ref, *, head_size, width, rows
+):
+    query_ref, key_ref, value_ref = query_ref.at[0], key_ref.at[0], value_ref.at[0]
     head = pl.program_id(0)
     base, mask = head_window(head, head_size, width)
     scale = head_size**-0.5 * LOG2E
     zero = jnp.zeros((), jnp.bfloat16)
-    keys = qkv_ref[:, pl.ds(width + base, 256)]
-    values = qkv_ref[:, pl.ds(2 * width + base, 256)]
+    window = (slice(None), pl.ds(base, 256))
+    keys = key_ref[window]
+    values = value_ref[window]
     keep = keep_ref[head].astype(jnp.float32)
-    for start in range(0, qkv_ref.shape[0], rows):
+    for start in range(0, query_ref.shape[0], rows):
         block = (pl.ds(start, rows), pl.ds(base, 256))
-        query = jnp.where(mask, qkv_ref[block], zero)
+        query = jnp.where(mask, query_ref[block], zero)
         scores = matmul(query, keys, ROWS_NT)
         top = jnp.max(scores, axis=-1, keepdims=True)
         probs = jnp.exp2((scores - top) * scale)
@@ -69,24 +69,36 @@
 
 
 def attend_backward_kernel(
-    keep_ref, qkv_ref, out_ref, grad_ref, lse_ref, dqkv_ref, *, head_size, width, rows
+    keep_ref,
+    query_ref,
+    key_ref,
+    value_ref,
+    out_ref,
+    grad_ref,
+    lse_ref,
+    grads_ref,
+    *,
+    head_size,
+    width,
+    rows,
 ):
+    query_ref, key_ref, value_ref = query_ref.at[0], key_ref.at[0], value_ref.at[0]
+    dquery_ref, dkey_ref, dvalue_ref = grads_ref.at[0], grads_ref.at[1], grads_ref.at[2]
     head = pl.program_id(0)
     base, mask = head_window(head, head_size, width)
     scale = head_size**-0.5
     zero = jnp.zeros((), jnp.bfloat16)
-    length = qkv_ref.shape[0]
-    key_block = (slice(None), pl.ds(width + base, 256))
-    value_block = (slice(None), pl.ds(2 * width + base, 256))
-    keys = qkv_ref[key_block]
-    values = qkv_ref[value_block]
+    length = query_ref.shape[0]
+    window = (slice(None), pl.ds(base, 256))
+    keys = key_ref[window]
+    values = value_ref[window]
     keys_across = jnp.transpose(keys)
     key_grad = jnp.zeros((length, 256), jnp.float32)
     value_grad = jnp.zeros((length, 256), jnp.float32)
     kept = mask & (keep_ref[head] > 0)
     for start in range(0, length, rows):
         block = (pl.ds(start, rows), pl.ds(base, 256))
-        query = jnp.where(mask, qkv_ref[block], zero)
+        query = jnp.where(mask, query_ref[block], zero)
         grad = jnp.where(kept, grad_ref[block], zero)
         row_dot = as_row(
             jnp.sum(
@@ -99,27 +111,32 @@
         value_grad = value_grad + matmul(probs.astype(jnp.bfloat16), grad, ROWS_NN)
         key_grad = key_grad + matmul(score_grad, query, ROWS_NN)
         query_grad = jnp.transpose(matmul(keys_across, score_grad, ROWS_NN)) * scale
-        dqkv_ref[block] = jnp.where(mask, query_grad.astype(jnp.bfloat16), dqkv_ref[block])
-    dqkv_ref[key_block] = jnp.where(
-        mask, (key_grad * scale).astype(jnp.bfloat16), dqkv_ref[key_block]
-    )
-    dqkv_ref[value_block] = jnp.where(mask, value_grad.astype(jnp.bfloat16), dqkv_ref[value_block])
+        dquery_ref[block] = jnp.where(mask, query_grad.astype(jnp.bfloat16), dquery_ref[block])
+    dkey_ref[window] = jnp.where(mask, (key_grad * scale).astype(jnp.bfloat16), dkey_ref[window])
+    dvalue_ref[window] = jnp.where(mask, value_grad.astype(jnp.bfloat16), dvalue_ref[window])
 
 
 def whole(shape):
     return pl.BlockSpec(shape, lambda *_: (0,) * len(shape), pipeline_mode=pl.Buffered(1))
 
 
+def one_of(index, length, width):
+    return pl.BlockSpec(
+        (1, length, width), lambda head: (index, 0, 0), pipeline_mode=pl.Buffered(1)
+    )
+
+
 def attend_forward(qkv, keep, rows=512):
-    length, triple = qkv.shape
-    width, heads = triple // 3, keep.shape[0]
+    _, length, width = qkv.shape
+    heads = keep.shape[0]
     cells = heads * length * length
     return pl.pallas_call(
         functools.partial(
             attend_forward_kernel, head_size=width // heads, width=width, rows=min(rows, length)
         ),
         grid=(heads,),
-        in_specs=[pl.BlockSpec(memory_space=pltpu.SMEM), whole((length, triple))],
+        in_specs=[pl.BlockSpec(memory_space=pltpu.SMEM)]
+        + [one_of(i, length, width) for i in range(3)],
         out_specs=[
             pl.BlockSpec((length, width), lambda head: (0, 0)),
             pl.BlockSpec((heads, length), lambda head: (0, 0)),
@@ -133,33 +150,645 @@
             flops=cells * 1024, transcendentals=cells, bytes_accessed=length * width * 8
         ),
         name="attend_forward",
-    )(keep, qkv)
+    )(keep, qkv, qkv, qkv)
 
 
 def attend_backward(qkv, out, grad, lse, keep, rows=256):
-    length, triple = qkv.shape
-    width, heads = triple // 3, keep.shape[0]
+    _, length, width = qkv.shape
+    heads = keep.shape[0]
     cells = heads * length * length
     return pl.pallas_call(
         functools.partial(
             attend_backward_kernel, head_size=width // heads, width=width, rows=min(rows, length)
         ),
         grid=(heads,),
-        in_specs=[
-            pl.BlockSpec(memory_space=pltpu.SMEM),
-            whole((length, triple)),
-            whole((length, width)),
-            whole((length, width)),
-            whole((heads, length)),
-        ],
-        out_specs=pl.BlockSpec((length, triple), lambda head: (0, 0)),
-        out_shape=jax.ShapeDtypeStruct((length, triple), jnp.bfloat16),
+        in_specs=[pl.BlockSpec(memory_space=pltpu.SMEM)]
+        + [one_of(i, length, width) for i in range(3)]
+        + [whole((length, width))] * 2
+        + [whole((heads, length))],
+        out_specs=pl.BlockSpec((3, length, width), lambda head: (0, 0, 0)),
+        out_shape=jax.ShapeDtypeStruct((3, length, width), jnp.bfloat16),
         compiler_params=pltpu.CompilerParams(vmem_limit_bytes=56 << 20),
         cost_estimate=pl.CostEstimate(
             flops=cells * 2560, transcendentals=cells, bytes_accessed=length * width * 16
         ),
         name="attend_backward",
-    )(keep, qkv, out, grad, lse)
+    )(keep, qkv, qkv, qkv, out, grad, lse)
+
+
+ROWS_TN = (((0,), (0,)), ((), ()))
+ANY = pl.BlockSpec(memory_space=pl.ANY)
+
+
+def square_copies(place, sets, r, target, sem):
+    part = jnp.bitwise_xor(place[2], r)
+    if len(sets[0]) == 1:
+        return [pltpu.make_async_copy(sets[0][0].at[part], target, sem)]
+    copies, column = [], 0
+    for refs in sets:
+        _, rows, columns = refs[0].shape
+        for x_r in range(2):
+            for z_r in range(4):
+                shard = (place[0] + z_r) % 4 * 2 + (place[1] + x_r) % 2
+                block = (pl.ds(pl.multiple_of(shard * rows, 16), rows), pl.ds(column, columns))
+                source = refs[2 * r + x_r].at[z_r]
+                copies.append(pltpu.make_async_copy(source, target.at[block], sem))
+        column += columns
+    return copies
+
+
+def strip_copies(place, refs, chunk, target, sem):
+    if len(refs) == 1:
+        return [pltpu.make_async_copy(refs[0].at[chunk], target, sem)]
+    rows = refs[0].shape[2]
+    z_r = (chunk + 4 - place[0]) % 4
+    copies = []
+    for core_r in range(2):
+        for y in range(2):
+            part = 2 * y + (place[2] + core_r) % 2
+            for x_r in range(2):
+                start = (place[1] + x_r) % 2 * (4 * rows) + part * rows
+                block = target.at[pl.ds(pl.multiple_of(start, 16), rows)]
+                source = refs[2 * core_r + x_r].at[z_r, y]
+                copies.append(pltpu.make_async_copy(source, block, sem))
+    return copies
+
+
+def square_stores(place, outs, r, source, sem):
+    part = jnp.bitwise_xor(place[2], r)
+    if len(outs) == 1:
+        return [pltpu.make_async_copy(source, outs[0].at[part], sem)]
+    copies, column = [], 0
+    for pair in range(0, len(outs), 2):
+        out = outs[pair + r % 2]
+        rows, columns = out.shape[3:]
+        for shard in range(8):
+            x_r, z_r = (place[1] + shard % 2) % 2, (shard // 2 + 4 - place[0]) % 4
+            block = source.at[pl.ds(shard * rows, rows), pl.ds(column, columns)]
+            copies.append(pltpu.make_async_copy(block, out.at[r // 2, x_r, z_r], sem))
+        column += columns
+    return copies
+
+
+def strip_stores(place, outs, chunk, source, sem):
+    if len(outs) == 1:
+        return [pltpu.make_async_copy(source, outs[0].at[chunk], sem)]
+    rows = outs[0].shape[3]
+    z_r = (chunk + 4 - place[0]) % 4
+    copies = []
+    for r in range(4):
+        part = jnp.bitwise_xor(place[2], r)
+        for x in range(2):
+            block = source.at[pl.ds(pl.multiple_of(x * (4 * rows) + part * rows, 16), rows)]
+            x_r = (place[1] + x) % 2
+            copies.append(pltpu.make_async_copy(block, outs[r % 2].at[r // 2, x_r, z_r], sem))
+    return copies
+
+
+def in_sets(refs, sets):
+    refs, found = list(refs), []
+    for entry in sets:
+        found.append(refs[: len(entry)])
+        refs = refs[len(entry) :]
+    return found
+
+
+def flat(sets):
+    return [array for entry in sets for array in entry]
+
+
+def start_all(copies):
+    for copy in copies:
+        copy.start()
+
+
+def wait_all(copies):
+    for copy in copies:
+        copy.wait()
+
+
+def for_each(step, action):
+    for r in range(4):
+
+        @pl.when(step == r)
+        def _(r=r):
+            action(r)
+
+
+def fetch_squares(place, sets, step, held, sems):
+    @pl.when(step == 0)
+    def _():
+        start_all(square_copies(place, sets, 0, held.at[0], sems.at[0]))
+
+    for_each(
+        step + 1,
+        lambda r: start_all(square_copies(place, sets, r, held.at[r % 2], sems.at[r % 2])),
+    )
+    for_each(
+        step, lambda r: wait_all(square_copies(place, sets, r, held.at[r % 2], sems.at[r % 2]))
+    )
+
+
+def tiles(length, rows=256):
+    return [pl.ds(start, min(rows, length)) for start in range(0, length, min(rows, length))]
+
+
+def prepare_kernel(tokens_ref, cotangent_ref, rows_ref, mod_ref, across_ref, grad_ref, sum_ref):
+    normed, _ = norm_forward(tokens_ref[...].astype(jnp.float32))
+    mod = normed * (1.0 + row_of(rows_ref, SCALE_ATTN)) + row_of(rows_ref, SHIFT_ATTN)
+    mod_ref[...] = mod.astype(jnp.bfloat16)
+    across_ref[...] = jnp.transpose(mod).astype(jnp.bfloat16)
+    grad = (cotangent_ref[...].astype(jnp.float32) * row_of(rows_ref, GATE_MLP)).astype(jnp.bfloat16)
+    grad_ref[...] = grad
+
+    @pl.when(pl.program_id(0) == 0)
+    def _():
+        sum_ref[...] = jnp.zeros_like(sum_ref)
+
+    sum_ref[0:1] += jnp.sum(grad.astype(jnp.float32), axis=0, keepdims=True)
+
+
+def prepare(tokens, cotangent, rows, tile=256):
+    length, width = tokens.shape
+    tile = min(tile, length)
+    by_rows = pl.BlockSpec((tile, width), lambda step: (step, 0))
+    fixed = pl.BlockSpec((8, width), lambda step: (0, 0))
+    return pl.pallas_call(
+        prepare_kernel,
+        grid=(length // tile,),
+        in_specs=[by_rows, by_rows, fixed],
+        out_specs=[by_rows, pl.BlockSpec((width, tile), lambda step: (0, step)), by_rows, fixed],
+        out_shape=[
+            jax.ShapeDtypeStruct((length, width), jnp.bfloat16),
+            jax.ShapeDtypeStruct((width, length), jnp.bfloat16),
+            jax.ShapeDtypeStruct((length, width), jnp.bfloat16),
+            jax.ShapeDtypeStruct((8, width), jnp.float32),
+        ],
+        compiler_params=vmem_params(),
+        cost_estimate=cost(20 * length * width, 10 * length * width),
+        name="prepare",
+    )(tokens, cotangent, rows)
+
+
+def project_kernel(place, mod_ref, bias_ref, *rest, sets):
+    *refs, out_ref, held, sems = rest
+    step = pl.program_id(0)
+    fetch_squares(place, in_sets(refs, sets), step, held, sems)
+    part = jnp.bitwise_xor(place[2], step)
+
+    @pl.when(part < 3)
+    def _():
+        weight = held[step % 2]
+        bias = bias_ref[pl.ds(part, 1)]
+        for tile in tiles(mod_ref.shape[0]):
+            out_ref[0, tile] = (matmul(mod_ref[tile], weight, ROWS_NN) + bias).astype(jnp.bfloat16)
+
+
+def vmem_params(mebibytes=56):
+    return pltpu.CompilerParams(
+        vmem_limit_bytes=mebibytes << 20, dimension_semantics=("arbitrary",)
+    )
+
+
+def cost(flops, moved):
+    return pl.CostEstimate(flops=int(flops), transcendentals=0, bytes_accessed=int(moved))
+
+
+def project(place, mod, bias, squares):
+    length, width = mod.shape
+    return pl.pallas_call(
+        functools.partial(project_kernel, sets=squares),
+        grid_spec=pltpu.PrefetchScalarGridSpec(
+            num_scalar_prefetch=1,
+            grid=(4,),
+            in_specs=[
+                pl.BlockSpec((length, width), lambda step, place: (0, 0)),
+                pl.BlockSpec(bias.shape, lambda step, place: (0, 0)),
+            ]
+            + [ANY] * len(flat(squares)),
+            out_specs=pl.BlockSpec(
+                (1, length, width), lambda step, place: (jnp.bitwise_xor(place[2], step), 0, 0)
+            ),
+            scratch_shapes=[
+                pltpu.VMEM((2, width, width), jnp.bfloat16),
+                pltpu.SemaphoreType.DMA((2,)),
+            ],
+        ),
+        out_shape=jax.ShapeDtypeStruct((4, length, width), jnp.bfloat16),
+        compiler_params=vmem_params(),
+        cost_estimate=cost(6 * length * width * width, 14 * length * width),
+        name="project",
+    )(place, mod, bias, *flat(squares))
+
+
+def fetch_part(place, sets, wanted, target, sem):
+    part = jnp.bitwise_xor(place[2], wanted)
+    for_each(part, lambda r: start_all(square_copies(place, sets, r, target, sem)))
+    for_each(part, lambda r: wait_all(square_copies(place, sets, r, target, sem)))
+
+
+def row_of(rows_ref, index):
+    return rows_ref[index : index + 1]
+
+
+SHIFT_ATTN, SCALE_ATTN, GATE_ATTN, SHIFT_MLP, SCALE_MLP, GATE_MLP, OUT_BIAS, DOWN_BIAS = range(8)
+
+
+def after_attention_kernel(place, low_ref, tokens_ref, rows_ref, *rest, sets):
+    *refs, branch_ref, middle_ref, mod_ref, across_ref, weight, sem = rest
+
+    @pl.when(pl.program_id(0) == 0)
+    def _():
+        fetch_part(place, in_sets(refs, sets), 3, weight, sem)
+
+    branch = matmul(low_ref[...], weight[...], ROWS_NN) + row_of(rows_ref, OUT_BIAS)
+    middle = tokens_ref[...].astype(jnp.float32) + row_of(rows_ref, GATE_ATTN) * branch
+    normed, _ = norm_forward(middle)
+    mod = normed * (1.0 + row_of(rows_ref, SCALE_MLP)) + row_of(rows_ref, SHIFT_MLP)
+    branch_ref[...] = branch
+    middle_ref[...] = middle
+    mod_ref[...] = mod.astype(jnp.bfloat16)
+    across_ref[...] = jnp.transpose(mod).astype(jnp.bfloat16)
+
+
+def after_attention(place, low, tokens, rows, squares, tile=256):
+    length, width = low.shape
+    tile = min(tile, length)
+    by_rows = pl.BlockSpec((tile, width), lambda step, place: (step, 0))
+    return pl.pallas_call(
+        functools.partial(after_attention_kernel, sets=squares),
+        grid_spec=pltpu.PrefetchScalarGridSpec(
+            num_scalar_prefetch=1,
+            grid=(length // tile,),
+            in_specs=[by_rows, by_rows, pl.BlockSpec(rows.shape, lambda step, place: (0, 0))]
+            + [ANY] * len(flat(squares)),
+            out_specs=[by_rows] * 3 + [pl.BlockSpec((width, tile), lambda step, place: (0, step))],
+            scratch_shapes=[pltpu.VMEM((width, width), jnp.bfloat16), pltpu.SemaphoreType.DMA],
+        ),
+        out_shape=[
+            jax.ShapeDtypeStruct((length, width), jnp.float32),
+            jax.ShapeDtypeStruct((length, width), jnp.float32),
+            jax.ShapeDtypeStruct((length, width), jnp.bfloat16),
+            jax.ShapeDtypeStruct((width, length), jnp.bfloat16),
+        ],
+        compiler_params=vmem_params(),
+        cost_estimate=cost(2 * length * width * width, 18 * length * width),
+        name="after_attention",
+    )(place, low, tokens, rows, *flat(squares))
+
+
+ROOT = 0.7978845608028654
+
+
+def gelu_and_slope(values):
+    square = values * values
+    bend = jnp.tanh(values * (ROOT + (ROOT * 0.044715) * square))
+    half = 0.5 + 0.5 * bend
+    slope = half + (0.5 * values) * (1.0 - bend * bend) * (ROOT + (3 * 0.044715 * ROOT) * square)
+    return values * half, slope
+
+
+def mlp_kernel(place, mod_ref, across_ref, grad_ref, bias_ref, keep_ref, *rest, ups, downs):
+    count = len(flat(ups)) + downs
+    refs, rest = rest[:count], rest[count:]
+    up_sets, down_refs = in_sets(refs, ups), refs[-downs:]
+    branch_ref, dmod_ref, dbias_ref = rest[:3]
+    *stores, act, dpre, up, down, up_out, down_out, in_sems, out_sems = rest[3:]
+    up_stores, down_stores = stores[: len(stores) // 2], stores[len(stores) // 2 :]
+    step = pl.program_id(0)
+    length = mod_ref.shape[0]
+
+    def chunk_of(r):
+        return jnp.bitwise_xor(place[2], r)
+
+    def fetch(r):
+        slot = r % 2
+        return square_copies(place, up_sets, r, up.at[slot], in_sems.at[slot, 0]) + strip_copies(
+            place, down_refs, chunk_of(r), down.at[slot], in_sems.at[slot, 1]
+        )
+
+    @pl.when(step == 0)
+    def _():
+        start_all(fetch(0))
+        branch_ref[...] = jnp.zeros_like(branch_ref)
+        dmod_ref[...] = jnp.zeros_like(dmod_ref)
+
+    for_each(step + 1, lambda r: start_all(fetch(r)))
+    for_each(step, lambda r: wait_all(fetch(r)))
+    chunk = chunk_of(step)
+    slot = step % 2
+    bias = bias_ref[pl.ds(chunk, 1)]
+    keep = keep_ref[pl.ds(chunk, 1)]
+    total = jnp.zeros_like(bias)
+    for tile in tiles(length):
+        gelu, slope = gelu_and_slope(matmul(mod_ref[tile], up[slot], ROWS_NN) + bias)
+        act[tile] = (gelu * keep).astype(jnp.bfloat16)
+        back = matmul(grad_ref[tile], down[slot], ROWS_NT)
+        low = (slope * keep * back).astype(jnp.bfloat16)
+        dpre[tile] = low
+        total = total + jnp.sum(low.astype(jnp.float32), axis=0, keepdims=True)
+        branch_ref[tile] += matmul(act[tile], down[slot], ROWS_NN)
+        dmod_ref[tile] += matmul(low, up[slot], ROWS_NT)
+    dbias_ref[pl.ds(chunk, 1)] = total
+
+    def leave(r):
+        return square_stores(place, up_stores, r, up_out, out_sems.at[0]), strip_stores(
+            place, down_stores, chunk_of(r), down_out, out_sems.at[1]
+        )
+
+    for_each(step - 1, lambda r: wait_all(leave(r)[0]))
+    up_out[...] = matmul(across_ref[...], dpre[...], ROWS_NN).astype(jnp.bfloat16)
+    for_each(step, lambda r: start_all(leave(r)[0]))
+    for_each(step - 1, lambda r: wait_all(leave(r)[1]))
+    down_out[...] = matmul(act[...], grad_ref[...], ROWS_TN).astype(jnp.bfloat16)
+    for_each(step, lambda r: start_all(leave(r)[1]))
+
+    @pl.when(step == 3)
+    def _():
+        wait_all(leave(3)[0])
+        wait_all(leave(3)[1])
+
+
+def gradient_shapes(paired, rows, columns):
+    if paired:
+        return [
+            jax.ShapeDtypeStruct((2, 2, 4, rows, count), jnp.bfloat16)
+            for count in columns
+            for _ in range(2)
+        ]
+    return [jax.ShapeDtypeStruct((4, sum(columns), sum(columns)), jnp.bfloat16)]
+
+
+def mlp(place, mod, across, grad, bias, keep, ups, downs, block_rows):
+    length, width = mod.shape
+    stores = gradient_shapes(len(downs) > 1, block_rows, [width])
+    quarter = jax.ShapeDtypeStruct((4, width), jnp.float32)
+    table = pl.BlockSpec((4, width), lambda step, place: (0, 0))
+    held = pl.BlockSpec((length, width), lambda step, place: (0, 0), pipeline_mode=pl.Buffered(1))
+    square = pltpu.VMEM((width, width), jnp.bfloat16)
+    pair = pltpu.VMEM((2, width, width), jnp.bfloat16)
+    tall = pltpu.VMEM((length, width), jnp.bfloat16)
+    wide = pl.BlockSpec((length, width), lambda step, place: (0, 0))
+    return pl.pallas_call(
+        functools.partial(mlp_kernel, ups=ups, downs=len(downs)),
+        grid_spec=pltpu.PrefetchScalarGridSpec(
+            num_scalar_prefetch=1,
+            grid=(4,),
+            in_specs=[
+                held,
+                pl.BlockSpec((width, length), lambda step, place: (0, 0), pipeline_mode=pl.Buffered(1)),
+                held,
+                table,
+                table,
+            ]
+            + [ANY] * (len(flat(ups)) + len(downs)),
+            out_specs=[wide, wide, table] + [ANY] * (2 * len(stores)),
+            scratch_shapes=[
+                tall,
+                tall,
+                pair,
+                pair,
+                square,
+                square,
+                pltpu.SemaphoreType.DMA((2, 2)),
+                pltpu.SemaphoreType.DMA((2,)),
+            ],
+        ),
+        out_shape=[jax.ShapeDtypeStruct((length, width), jnp.float32)] * 2
+        + [quarter]
+        + stores
+        + stores,
+        compiler_params=vmem_params(60),
+        cost_estimate=cost(48 * length * width * width, 32 * width * width),
+        name="mlp",
+    )(place, mod, across, grad, bias, keep, *flat(ups), *downs)
+
+
+def after_mlp_kernel(
+    place, mlp_ref, dmod_ref, middle_ref, branch_ref, cotangent_ref, low_ref, rows_ref, *rest, sets
+):
+    *refs, out_ref, dmiddle_ref, dlow_ref, sums_ref, dweight_ref, weight, dbranch, staged, sems = rest
+    step = pl.program_id(0)
+    tile = out_ref.shape[0]
+
+    @pl.when(step == 0)
+    def _():
+        fetch_part(place, in_sets(refs, sets), 3, weight, sems.at[0])
+        sums_ref[...] = jnp.zeros_like(sums_ref)
+
+    middle = middle_ref[...]
+    grad = cotangent_ref[...].astype(jnp.float32)
+    mlp_branch = mlp_ref[...] + row_of(rows_ref, DOWN_BIAS)
+    out_ref[...] = (middle + row_of(rows_ref, GATE_MLP) * mlp_branch).astype(jnp.bfloat16)
+    normed, inverse = norm_forward(middle)
+    dmod = dmod_ref[...]
+    dmiddle = grad + norm_backward(dmod * (1.0 + row_of(rows_ref, SCALE_MLP)), normed, inverse)
+    dmiddle_ref[...] = dmiddle
+    low = (dmiddle * row_of(rows_ref, GATE_ATTN)).astype(jnp.bfloat16)
+    dbranch[pl.ds(pl.multiple_of(step * tile, tile), tile)] = low
+    dlow_ref[...] = matmul(low, weight[...], ROWS_NT).astype(jnp.bfloat16)
+
+    def add(index, values):
+        sums_ref[index : index + 1] += jnp.sum(values, axis=0, keepdims=True)
+
+    add(0, grad * mlp_branch)
+    add(1, dmod * normed)
+    add(2, dmod)
+    add(3, dmiddle * branch_ref[...])
+    add(4, low.astype(jnp.float32))
+
+    @pl.when(step == pl.num_programs(0) - 1)
+    def _():
+        staged[...] = matmul(low_ref[...], dbranch[...], ROWS_TN).astype(jnp.bfloat16)
+        if len(dweight_ref.shape) == 2:
+            copies = [pltpu.make_async_copy(staged, dweight_ref, sems.at[1])]
+        else:
+            rows = dweight_ref.shape[2]
+            copies = []
+            for shard in range(8):
+                x_r, z_r = (place[1] + shard % 2) % 2, (shard // 2 + 4 - place[0]) % 4
+                block = staged.at[pl.ds(shard * rows, rows)]
+                copies.append(pltpu.make_async_copy(block, dweight_ref.at[x_r, z_r], sems.at[1]))
+        start_all(copies)
+        wait_all(copies)
+
+
+def after_mlp(place, branch_mlp, dmod, middle, branch, cotangent, low, rows, squares, block_rows, tile=256):
+    length, width = low.shape
+    tile = min(tile, length)
+    by_rows = pl.BlockSpec((tile, width), lambda step, place: (step, 0))
+    fixed = lambda shape: pl.BlockSpec(shape, lambda step, place: (0, 0))
+    wgrad = (2, 4, block_rows, width) if len(squares[0]) > 1 else (width, width)
+    return pl.pallas_call(
+        functools.partial(after_mlp_kernel, sets=squares),
+        grid_spec=pltpu.PrefetchScalarGridSpec(
+            num_scalar_prefetch=1,
+            grid=(length // tile,),
+            in_specs=[by_rows] * 5 + [fixed((length, width)), fixed(rows.shape)] + [ANY] * len(flat(squares)),
+            out_specs=[by_rows] * 3 + [fixed((8, width)), ANY],
+            scratch_shapes=[
+                pltpu.VMEM((width, width), jnp.bfloat16),
+                pltpu.VMEM((length, width), jnp.bfloat16),
+                pltpu.VMEM((width, width), jnp.bfloat16),
+                pltpu.SemaphoreType.DMA((2,)),
+            ],
+        ),
+        out_shape=[
+            jax.ShapeDtypeStruct((length, width), jnp.bfloat16),
+            jax.ShapeDtypeStruct((length, width), jnp.float32),
+            jax.ShapeDtypeStruct((length, width), jnp.bfloat16),
+            jax.ShapeDtypeStruct((8, width), jnp.float32),
+            jax.ShapeDtypeStruct(wgrad, jnp.bfloat16),
+        ],
+        compiler_params=vmem_params(),
+        cost_estimate=cost(4 * length * width * width, 30 * length * width),
+        name="after_mlp",
+    )(place, branch_mlp, dmod, middle, branch, cotangent, low, rows, *flat(squares))
+
+
+def square_grads_kernel(place, across_ref, grads_ref, out_grad_ref, *rest):
+    *stores, sums_ref, staged, sems = rest
+    step = pl.program_id(0)
+    part = jnp.bitwise_xor(place[2], step)
+
+    def leave(r):
+        return square_stores(place, stores, r, staged.at[r % 2], sems.at[r % 2])
+
+    def pass_on(r):
+        if len(stores) == 1:
+            return [pltpu.make_async_copy(out_grad_ref, stores[0].at[3], sems.at[r % 2])]
+        copies, column = [], 0
+        for pair in range(0, len(stores), 2):
+            out = stores[pair + r % 2]
+            columns = out.shape[4]
+            source = out_grad_ref.at[:, :, :, pl.ds(column, columns)]
+            copies.append(pltpu.make_async_copy(source, out.at[r // 2], sems.at[r % 2]))
+            column += columns
+        return copies
+
+    def wait(r):
+        wait_all(pass_on(r))
+
+    for_each(step - 2, wait)
+
+    @pl.when(part < 3)
+    def _():
+        grads = grads_ref[0]
+        staged[step % 2] = matmul(across_ref[...], grads, ROWS_NN).astype(jnp.bfloat16)
+        sums_ref[pl.ds(part, 1)] = jnp.sum(grads.astype(jnp.float32), axis=0, keepdims=True)
+        for_each(step, lambda r: start_all(leave(r)))
+
+    @pl.when(part == 3)
+    def _():
+        for_each(step, lambda r: start_all(pass_on(r)))
+
+    @pl.when(step == 3)
+    def _():
+        wait(2)
+        wait(3)
+
+
+def square_grads(place, across, grads, out_grad, block_rows, columns):
+    width, length = across.shape
+    paired = len(out_grad.shape) > 2
+    stores = gradient_shapes(paired, block_rows, columns)
+    return pl.pallas_call(
+        square_grads_kernel,
+        grid_spec=pltpu.PrefetchScalarGridSpec(
+            num_scalar_prefetch=1,
+            grid=(4,),
+            in_specs=[
+                pl.BlockSpec((width, length), lambda step, place: (0, 0)),
+                pl.BlockSpec(
+                    (1, length, width),
+                    lambda step, place: (jnp.minimum(jnp.bitwise_xor(place[2], step), 2), 0, 0),
+                ),
+                pl.BlockSpec(
+                    out_grad.shape,
+                    lambda step, place: (0,) * len(out_grad.shape),
+                    pipeline_mode=pl.Buffered(1),
+                ),
+            ],
+            out_specs=[ANY] * len(stores) + [pl.BlockSpec((4, width), lambda step, place: (0, 0))],
+            scratch_shapes=[
+                pltpu.VMEM((2, width, width), jnp.bfloat16),
+                pltpu.SemaphoreType.DMA((2,)),
+            ],
+        ),
+        out_shape=stores + [jax.ShapeDtypeStruct((4, width), jnp.float32)],
+        compiler_params=vmem_params(),
+        cost_estimate=cost(6 * length * width * width, 16 * length * width),
+        name="square_grads",
+    )(place, across, grads, out_grad)
+
+
+def tokens_back_kernel(place, grads_ref, tokens_ref, dmiddle_ref, rows_ref, *rest, sets):
+    *refs, out_ref, sums_ref, dmod, held, sems = rest
+    step = pl.program_id(0)
+    fetch_squares(place, in_sets(refs, sets), step, held, sems)
+    part = jnp.bitwise_xor(place[2], step)
+    length = tokens_ref.shape[0]
+
+    @pl.when(step == 0)
+    def _():
+        dmod[...] = jnp.zeros_like(dmod)
+
+    @pl.when(part < 3)
+    def _():
+        for tile in tiles(length):
+            dmod[tile] += matmul(grads_ref[0, tile], held[step % 2], ROWS_NT)
+
+    @pl.when(step == 3)
+    def _():
+        shift = jnp.zeros((1, dmod.shape[1]), jnp.float32)
+        scale = shift
+        for tile in tiles(length):
+            back = dmod[tile]
+            normed, inverse = norm_forward(tokens_ref[tile].astype(jnp.float32))
+            scale = scale + jnp.sum(back * normed, axis=0, keepdims=True)
+            shift = shift + jnp.sum(back, axis=0, keepdims=True)
+            back = norm_backward(back * (1.0 + row_of(rows_ref, SCALE_ATTN)), normed, inverse)
+            out_ref[tile] = (dmiddle_ref[tile] + back).astype(jnp.bfloat16)
+        sums_ref[0:1] = shift
+        sums_ref[1:2] = scale
+
+
+def tokens_back(place, grads, tokens, dmiddle, rows, squares):
+    length, width = tokens.shape
+    held = pl.BlockSpec((length, width), lambda step, place: (0, 0), pipeline_mode=pl.Buffered(1))
+    return pl.pallas_call(
+        functools.partial(tokens_back_kernel, sets=squares),
+        grid_spec=pltpu.PrefetchScalarGridSpec(
+            num_scalar_prefetch=1,
+            grid=(4,),
+            in_specs=[
+                pl.BlockSpec(
+                    (1, length, width),
+                    lambda step, place: (jnp.minimum(jnp.bitwise_xor(place[2], step), 2), 0, 0),
+                ),
+                held,
+                held,
+                pl.BlockSpec(rows.shape, lambda step, place: (0, 0)),
+            ]
+            + [ANY] * len(flat(squares)),
+            out_specs=[
+                pl.BlockSpec((length, width), lambda step, place: (0, 0)),
+                pl.BlockSpec((8, width), lambda step, place: (0, 0)),
+            ],
+            scratch_shapes=[
+                pltpu.VMEM((length, width), jnp.float32),
+                pltpu.VMEM((2, width, width), jnp.bfloat16),
+                pltpu.SemaphoreType.DMA((2,)),
+            ],
+        ),
+        out_shape=[
+            jax.ShapeDtypeStruct((length, width), jnp.bfloat16),
+            jax.ShapeDtypeStruct((8, width), jnp.float32),
+        ],
+        compiler_params=vmem_params(),
+        cost_estimate=cost(6 * length * width * width, 20 * length * width),
+        name="tokens_back",
+    )(place, grads, tokens, dmiddle, rows, *flat(squares))
 
 
 def gather_rows(rows, axis, size):
@@ -171,6 +800,79 @@
         rows = jnp.concatenate([jnp.where(high, other, rows), jnp.where(high, rows, other)], axis=0)
         step *= 2
     return rows
+
+
+def swap(value, axis, size, step):
+    return lax.ppermute(value, axis, [(i, i ^ step) for i in range(size)])
+
+
+def both(value, axis, size, step, dim):
+    other = swap(value, axis, size, step)
+    first = lax.axis_index(axis) // step % 2 == 0
+    return jnp.stack([jnp.where(first, value, other), jnp.where(first, other, value)], axis=dim)
+
+
+def after(value, *others):
+    return lax.optimization_barrier((value, others))[0]
+
+
+def add(*terms):
+    return sum(term.astype(jnp.float32) for term in terms).astype(jnp.bfloat16)
+
+
+class Pairwise:
+    def __init__(self, shards, group):
+        self.shards, self.group = shards, group
+
+    def partner(self, value, kind):
+        if kind == "x":
+            return swap(value, "fsdp", self.shards, 1)
+        return swap(value, "dp", self.group, 2 if kind == "y" else 1)
+
+    def ahead(self, value, count):
+        pairs = [((target // 2 + count) % 4 * 2 + target % 2, target) for target in range(8)]
+        return lax.ppermute(value, "fsdp", pairs)
+
+    def along_z(self, block):
+        return jnp.stack([block] + [self.ahead(block, count) for count in (1, 2, 3)])
+
+    def widen(self, blocks, kind):
+        return blocks | {key + kind: self.partner(value, kind) for key, value in blocks.items()}
+
+    def listed(self, blocks, kinds):
+        found = {"".join(sorted(key)): value for key, value in blocks.items()}
+        names = [""]
+        for kind in kinds:
+            names = [name + more for name in names for more in ("", kind)]
+        return [found["".join(sorted(name))] for name in names]
+
+    def first_sum(self, kept, other, kind):
+        dim = 0 if kind == "y" else 1
+        stay, go = [
+            [lax.index_in_dim(half, i, dim, keepdims=False) for half in (kept, other)] for i in (0, 1)
+        ]
+        return add(*go), stay
+
+    def second_sum(self, stay, back):
+        return add(stay[0][1], stay[1][1], back[1]), add(stay[0][0], stay[1][0], back[0])
+
+    def send_z(self, mine):
+        return [self.ahead(mine[count], 4 - count) for count in (1, 2, 3)]
+
+    def to_group(self, part):
+        parts = both(both(part, "dp", self.group, 2, 0), "dp", self.group, 1, 1)
+        return parts.reshape(4, *part.shape)
+
+
+def reduce_all(grad):
+    shard = lax.psum_scatter(grad, "fsdp", scatter_dimension=0, tiled=True)
+    return lax.psum(shard, "dp").astype(jnp.float32)
+
+
+def reduce_columns(parts):
+    _, rows, width = parts.shape
+    shard = reduce_all(parts.swapaxes(0, 1).reshape(rows, 4 * width))
+    return [shard[:, i * width : (i + 1) * width] for i in range(4)]
 
 
 def conditioning(times, labels, table, shard, width):
@@ -217,6 +919,7 @@
     columns = width // shard_count
     group_count = image_count // shard_count
     shard = lax.axis_index("fsdp")
+    member = lax.axis_index("dp")
     bf16, f32 = jnp.bfloat16, jnp.float32
 
     facts = gather_rows(jnp.stack([timesteps, labels], axis=1), "fsdp", shard_count)
@@ -242,73 +945,130 @@
     up_bias_full = small[:, 3 * columns : up_end].reshape(-1)
     down_bias_full = small[:, up_end:].reshape(-1)
 
-    qkv_full = lax.all_gather(qkv_weight, "fsdp", axis=0, tiled=True)
-    out_full = lax.all_gather(out_weight, "fsdp", axis=0, tiled=True)
-    up_full = lax.all_gather(up_weight, "fsdp", axis=0, tiled=True)
-    down_full = lax.all_gather(down_weight, "fsdp", axis=0, tiled=True)
-
-    inputs = tokens[0].astype(f32)
-    normed_one, inverse_one = norm_forward(inputs)
-    mod_one = (normed_one * (1.0 + scale_attn) + shift_attn).astype(bf16)
-    qkv_bias = jnp.concatenate([query_bias, jnp.zeros((width,), f32), value_bias])
-    qkv = (jnp.dot(mod_one, qkv_full, preferred_element_type=f32) + qkv_bias).astype(bf16)
+    place = jnp.stack([shard // 2, shard % 2, member]).astype(jnp.int32)
+    paired = shard_count == 8 and group_count == 4 and columns % 16 == 0
+    four = jnp.concatenate([qkv_weight, out_weight], axis=1)
+    rows = jnp.concatenate([ada_rows[:, 0], out_bias_full[None], down_bias_full[None]])
+    qkv_bias = jnp.stack([query_bias, jnp.zeros((width,), f32), value_bias, out_bias_full])
+    net = Pairwise(shard_count, group_count)
+    splits = [width // 2 // 128 * 128]
+    splits.append(width - splits[0])
+
+    mod_one, mod_across, branch_grad, down_bias_g = prepare(tokens[0], cotangent[0], rows)
+    if paired:
+        mine = lax.dynamic_slice_in_dim(four, member * width, width, axis=1)
+        first = {"": net.along_z(mine[:, : splits[0]])}
+        second = {"": net.along_z(mine[:, splits[0] :])}
+        mine = lax.dynamic_slice_in_dim(up_weight, member * width, width, axis=1)
+        up = {"": net.along_z(after(mine, first, second))}
+        mine = down_weight.reshape(2, 2, columns, width)
+        mine = jnp.where(member % 2 == 0, mine[:, 0], mine[:, 1])
+        down = {"": net.along_z(after(mine, up))}
+        first = net.widen(first, "x")
+        second = net.widen(second, "x")
+        first = net.widen(first, "y")
+        up = net.widen(after(up, second), "x")
+        second = net.widen(after(second, first), "y")
+        first = net.widen(first, "c")
+        second = net.widen(second, "c")
+        up = net.widen(after(up, second), "y")
+        down = net.widen(after(down, up), "x")
+        squares = [net.listed(blocks, "ycx") for blocks in (first, second)]
+    else:
+        parts = lax.all_gather(four, "fsdp", axis=0, tiled=True)
+        squares = [[parts.reshape(width, 4, width).swapaxes(0, 1)]]
+    qkv = project(place, mod_one, qkv_bias, squares)
     attn_low, lse = attend_forward(qkv, head_keep[0])
-    attn_branch = jnp.dot(attn_low, out_full, preferred_element_type=f32) + out_bias_full
-    middle = inputs + gate_attn * attn_branch
-    normed_two, inverse_two = norm_forward(middle)
-    mod_two = (normed_two * (1.0 + scale_mlp) + shift_mlp).astype(bf16)
-    pre_act = jnp.dot(mod_two, up_full, preferred_element_type=f32) + up_bias_full
-    chan_mask = chan_keep.astype(f32)
-    act_low = (gelu_tanh(pre_act) * chan_mask).astype(bf16)
-    mlp_branch = jnp.dot(act_low, down_full, preferred_element_type=f32) + down_bias_full
-    block_out = (middle + gate_mlp * mlp_branch).astype(bf16)
-
-    out_grad = cotangent[0].astype(f32)
-    gate_mlp_grad = jnp.sum(out_grad * mlp_branch, axis=0)
-    branch_grad = (out_grad * gate_mlp).astype(bf16)
-    down_bias_g = jnp.sum(branch_grad.astype(f32), axis=0)
-    down_weight_g = jnp.einsum("tf,td->fd", act_low, branch_grad, preferred_element_type=f32)
-    act_grad = jnp.einsum("td,fd->tf", branch_grad, down_full, preferred_element_type=f32)
-    _, gelu_pull = jax.vjp(gelu_tanh, pre_act)
-    pre_grad = gelu_pull(act_grad * chan_mask)[0].astype(bf16)
-    up_bias_g = jnp.sum(pre_grad.astype(f32), axis=0)
-    up_weight_g = jnp.einsum("td,tf->df", mod_two, pre_grad, preferred_element_type=f32)
-    mod_two_grad = jnp.einsum("tf,df->td", pre_grad, up_full, preferred_element_type=f32)
-    mlp_grads = lax.optimization_barrier(
-        (down_weight_g.astype(bf16), up_weight_g.astype(bf16), mod_two_grad)
-    )
-    down_weight_g, up_weight_g, mod_two_grad = mlp_grads
-
-    def reduce(grad):
-        return lax.psum(
-            lax.psum_scatter(grad, "fsdp", scatter_dimension=0, tiled=True), "dp"
-        ).astype(f32)
-
-    down_shard = reduce(down_weight_g)
-    up_shard = reduce(up_weight_g)
-    scale_mlp_grad = jnp.sum(mod_two_grad * normed_two, axis=0)
-    shift_mlp_grad = jnp.sum(mod_two_grad, axis=0)
-    middle_grad = out_grad + norm_backward(
-        mod_two_grad * (1.0 + scale_mlp), normed_two, inverse_two
-    )
-    gate_attn_grad = jnp.sum(middle_grad * attn_branch, axis=0)
-    attn_grad = (middle_grad * gate_attn).astype(bf16)
-    out_bias_g = jnp.sum(attn_grad.astype(f32), axis=0)
-    out_weight_g = jnp.einsum("td,te->de", attn_low, attn_grad, preferred_element_type=f32)
-    low_grad = jnp.einsum("te,de->td", attn_grad, out_full, preferred_element_type=f32).astype(bf16)
-    out_weight_g, low_grad = lax.optimization_barrier((out_weight_g.astype(bf16), low_grad))
-    out_shard = reduce(out_weight_g)
-    qkv_grad = attend_backward(qkv, attn_low, low_grad, lse, head_keep[0])
-    qkv_weight_g = jnp.einsum("td,te->de", mod_one, qkv_grad, preferred_element_type=f32)
-    qkv_weight_g, qkv_grad = lax.optimization_barrier((qkv_weight_g.astype(bf16), qkv_grad))
-    qkv_shard = reduce(qkv_weight_g)
-    bias_sums = jnp.sum(qkv_grad.astype(f32), axis=0)
-    mod_one_grad = jnp.einsum("te,de->td", qkv_grad, qkv_full, preferred_element_type=f32)
-    scale_attn_grad = jnp.sum(mod_one_grad * normed_one, axis=0)
-    shift_attn_grad = jnp.sum(mod_one_grad, axis=0)
-    tokens_grad = (
-        middle_grad + norm_backward(mod_one_grad * (1.0 + scale_attn), normed_one, inverse_one)
-    ).astype(bf16)
+    if paired:
+        attn_low, up, down = lax.optimization_barrier((attn_low, up, down))
+        ups = [net.listed(net.widen(up, "c"), "ycx")]
+        downs = net.listed(net.widen(down, "c"), "cx")
+    else:
+        parts = lax.all_gather(up_weight, "fsdp", axis=0, tiled=True)
+        ups = [[parts.reshape(width, 4, width).swapaxes(0, 1)]]
+        parts = lax.all_gather(down_weight, "fsdp", axis=0, tiled=True)
+        downs = [parts.reshape(4, width, width)]
+    attn_branch, middle, mod_two, mod_two_across = after_attention(
+        place, attn_low, tokens[0], rows, squares
+    )
+    branch_mlp, mod_two_grad, up_bias_g, *stores = mlp(
+        place,
+        mod_two,
+        mod_two_across,
+        branch_grad,
+        up_bias_full.reshape(4, width),
+        chan_keep.astype(f32).reshape(4, width),
+        ups,
+        downs,
+        columns,
+    )
+    up_bias_g = up_bias_g.reshape(-1)
+    if paired:
+        up_kept, up_sent, down_kept, down_sent = stores
+        up_other, down_other = net.partner(up_sent, "c"), net.partner(down_sent, "c")
+    else:
+        up_shard = jnp.concatenate(reduce_columns(stores[0]), axis=1)
+        down_shard = reduce_all(stores[1].reshape(hidden, width))
+    block_out, middle_grad, low_grad, sums, out_weight_g = after_mlp(
+        place,
+        branch_mlp,
+        mod_two_grad,
+        middle,
+        attn_branch,
+        cotangent[0],
+        attn_low,
+        rows,
+        squares,
+        columns,
+    )
+    gate_mlp_grad, scale_mlp_grad, shift_mlp_grad, gate_attn_grad, out_bias_g = [
+        sums[i] for i in range(5)
+    ]
+    if paired:
+        low_grad, up_other, down_other = lax.optimization_barrier((low_grad, up_other, down_other))
+        up_go, up_stay = net.first_sum(up_kept, up_other, "x")
+        down_go, down_stay = net.first_sum(down_kept, down_other, "y")
+        low_grad, up_go, down_go = lax.optimization_barrier((low_grad, up_go, down_go))
+        up_back, down_back = net.partner(up_go, "x"), net.partner(down_go, "y")
+    grads = attend_backward(qkv, attn_low, low_grad, lse, head_keep[0])
+    if paired:
+        grads, up_back, down_back = lax.optimization_barrier((grads, up_back, down_back))
+        up_go, up_stay = net.second_sum(up_stay, up_back)
+        down_go, down_stay = net.second_sum(down_stay, down_back)
+        grads, up_go, down_go = lax.optimization_barrier((grads, up_go, down_go))
+        up_back, down_back = net.partner(up_go, "y"), net.partner(down_go, "x")
+    *stores, bias_sums = square_grads(place, mod_across, grads, out_weight_g, columns, splits)
+    query_sum, value_sum = bias_sums[0], bias_sums[2]
+    if paired:
+        grads, stores = lax.optimization_barrier((grads, stores))
+        others = [net.partner(sent, "c") for sent in stores[1::2]]
+    tokens_grad, sums = tokens_back(place, grads, tokens[0], middle_grad, rows, squares)
+    shift_attn_grad, scale_attn_grad = sums[0], sums[1]
+    if paired:
+        tokens_grad, up_back, down_back, others = lax.optimization_barrier(
+            (tokens_grad, up_back, down_back, others)
+        )
+        goes, stays = zip(
+            *[net.first_sum(stores[2 * i], others[i], kind) for i, kind in enumerate("yx")]
+        )
+        backs = [net.partner(go, kind) for go, kind in zip(goes, "yx")]
+        up_mine, down_mine = add(up_stay, up_back), add(down_stay, down_back)
+        up_terms, down_terms = net.send_z(up_mine), net.send_z(down_mine)
+        backs, up_terms, down_terms = lax.optimization_barrier((backs, up_terms, down_terms))
+        goes, stays = zip(*[net.second_sum(stay, back) for stay, back in zip(stays, backs)])
+        backs = [net.partner(go, kind) for go, kind in zip(goes, "xy")]
+        part = jnp.stack([add(up_mine[0], *up_terms), add(down_mine[0], *down_terms)])
+        parts = net.to_group(part)
+        up_shard = jnp.concatenate([parts[i, 0] for i in range(4)], axis=1).astype(f32)
+        down_shard = parts[:, 1].reshape(down_weight.shape).astype(f32)
+        mine = [add(stay, back) for stay, back in zip(stays, backs)]
+        terms = [net.send_z(value) for value in mine]
+        part = [add(value[0], *more) for value, more in zip(mine, terms)]
+        parts = net.to_group(jnp.concatenate(part, axis=1)).astype(f32)
+        query_g, key_g, value_g, out_shard = parts
+    else:
+        query_g, key_g, value_g, out_shard = reduce_columns(stores[0])
+    qkv_shard = jnp.concatenate([query_g, key_g, value_g], axis=1)
 
     row = jnp.concatenate(
         [
@@ -318,11 +1078,11 @@
             shift_mlp_grad,
             scale_mlp_grad,
             gate_mlp_grad,
-            bias_sums[:width],
-            bias_sums[2 * width :],
+            query_sum,
+            value_sum,
             out_bias_g,
             up_bias_g,
-            down_bias_g,
+            down_bias_g[0],
         ]
     ).astype(bf16)[None]
     rows = gather_rows(gather_rows(row, "fsdp", shard_count), "dp", group_count)

time: 1310 us -> 718 us (0.55)
  waiting for transfers between devices: 908 us -> 218 us
  matrix products: 212 us -> 6.6 us
  Pallas kernels: 97.8 us -> 299 us
  starting transfers between devices: 15.7 us -> 104 us
  other arithmetic: 35.9 us -> 53.7 us
    reduce_scatter x4 -> x0, waiting for transfers between devices: 447 us -> none  [reduce(): lax.psum_scatter(grad, 'fsdp', scatter_dimension=0, tiled=True)]
    all_gather x4 -> x0, waiting for transfers between devices: 338 us -> none  [the longest x1 142 us: body(): up_full = lax.all_gather(up_weight, 'fsdp', axis=0, tiled=True)]
    dot_general x12 -> x0, matrix products: 205 us -> none  [the longest x1 29.1 us: body(): jnp.einsum('td,fd->tf', branch_grad, down_full, preferred_element_type=f32)]
    pallas_call x0 -> x7, Pallas kernels: none -> 204 us  [the longest x1 100 us: mlp(): pl.pallas_call(functools.partial(mlp_kernel, ups=ups, downs=len(downs)),...]
    ppermute x0 -> x64, waiting for transfers between devices: none -> 192 us  [the longest x24 126 us: ahead(): return lax.ppermute(value, 'fsdp', pairs)]
    ppermute x0 -> x64, starting transfers between devices: none -> 88.6 us  [the longest x40 48.7 us: swap(): return lax.ppermute(value, axis, [(i, i ^ step) for i in range(size)])]
    psum x1 -> x0, waiting for transfers between devices: 73.6 us -> none  [reduce(): lax.psum(lax.psum_scatter(grad, 'fsdp', scatter_dimension=0, tiled=True),...]
    convert_element_type x5 -> x17, other arithmetic: 8.86 us -> 34 us  [the longest x13 30.2 us: add(): sum((term.astype(jnp.float32) for term in terms)).astype(jnp.bfloat16)]
  transfers between devices with their start and end apart: 20 -> 75, of which waited for: 14 -> 24; matrix products, arithmetic and copies ran while one was open for 10% -> 7% of each run, Pallas kernels for 7% -> 22%
where the time goes in v2:
time: 718 us; the launch traced here: 710 us
  Pallas kernels  299 us (42%)
  waiting for transfers between devices  218 us (30%)
  starting transfers between devices  104 us (14%)
  other arithmetic  53.7 us (7%)
  local copies, waits for them, and re-layouts  25.7 us (4%)
    ppermute x24, waiting for transfers between devices, ahead(): return lax.ppermute(value, 'fsdp', pairs)  126 us
    pallas_call x1, Pallas kernels, mlp(): pl.pallas_call(functools.partial(mlp_kernel, ups=ups, downs=len(downs)),...  100 us
    ppermute x40, waiting for transfers between devices, swap(): return lax.ppermute(value, axis, [(i, i ^ step) for i in range(size)])  66.1 us
    pallas_call x1, Pallas kernels, attend_backward(): pl.pallas_call(functools.partial(attend_backward_kernel, head_size=width...  57.6 us
    ppermute x40, starting transfers between devices, swap(): return lax.ppermute(value, axis, [(i, i ^ step) for i in range(size)])  48.7 us
    ppermute x24, starting transfers between devices, ahead(): return lax.ppermute(value, 'fsdp', pairs)  40 us
    pallas_call x1, Pallas kernels, attend_forward(): pl.pallas_call(functools.partial(attend_forward_kernel, head_size=width /...  37.1 us
    convert_element_type x13, other arithmetic, add(): sum((term.astype(jnp.float32) for term in terms)).astype(jnp.bfloat16)  30.2 us
  transfers between devices with their start and end apart: 75, of which 24 were waited for; matrix products, arithmetic and copies ran while one was open for 7% of the time, Pallas kernels for 22%

profile of v2, /device:TPU:1, one launch (start us, length us, event | category | flops | bytes accessed | tf_op | source)
XLA Modules:
  0.0 710.4 jit_solution(5632379771508757739)
XLA Ops:
  8.8 9.7 %collective-permute-done.4 = bf16[144,512]{1,0:T(8,128)(2,1)S(1)} collective-permute-done((bf16[144,512]{1,0:T(8,128)(2,1)S(1)}, bf16[144,512]{1,0:T(8,128)(2,1)S(1)}, u32[]{:S(2)}, u32[]{:S(2)}) %collective-permute-start.4) | collective-permute-done | bytes 147488 | tf_op jit(solution)/shard_map/ppermute | solution.py:834
  25.0 12.5 %collective-permute-done.14 = bf16[144,640]{1,0:T(8,128)(2,1)S(1)} collective-permute-done((bf16[144,640]{1,0:T(8,128)(2,1)S(1)}, bf16[144,640]{1,0:T(8,128)(2,1)S(1)}, u32[]{:S(2)}, u32[]{:S(2)}) %collective-permute-start.14) | collective-permute-done | bytes 184352 | tf_op jit(solution)/shard_map/ppermute | solution.py:834
  48.1 7.4 %collective-permute-done.16.rest_9_ = bf16[4,144,640]{2,1,0:T(8,128)(2,1)} collective-permute-done((bf16[4,144,640]{2,1,0:T(8,128)(2,1)S(1)}, bf16[4,144,640]{2,1,0:T(8,128)(2,1)}, u32[]{:S(2)}, u32[]{:S(2)}) %collective-permute-start.16) | collective-permute-done | bytes 737312 | tf_op jit(solution)/shard_map/ppermute | solution.py:806
  57.2 17.7 %collective-permute-done.24 = bf16[144,1152]{1,0:T(8,128)(2,1)S(1)} collective-permute-done((bf16[144,1152]{1,0:T(8,128)(2,1)S(1)}, bf16[144,1152]{1,0:T(8,128)(2,1)S(1)}, u32[]{:S(2)}, u32[]{:S(2)}) %collective-permute-start.24) | collective-permute-done | bytes 331808 | tf_op jit(solution)/shard_map/ppermute | solution.py:834
  93.0 12.4 %collective-permute-done.26.rest_1_ = bf16[4,144,1152]{2,1,0:T(8,128)(2,1)} collective-permute-done((bf16[4,144,1152]{2,1,0:T(8,128)(2,1)}, bf16[4,144,1152]{2,1,0:T(8,128)(2,1)}, u32[]{:S(2)}, u32[]{:S(2)}) %collective-permute-start.26) | collective-permute-done | bytes 1327136 | tf_op jit(solution)/shard_map/ppermute | solution.py:806
  129.0 7.0 prepare.1
  139.4 38.6 %collective-permute-done.30 = bf16[2,144,1152]{2,1,0:T(8,128)(2,1)} collective-permute-done((bf16[2,144,1152]{2,1,0:T(8,128)(2,1)S(1)}, bf16[2,144,1152]{2,1,0:T(8,128)(2,1)}, u32[]{:S(2)}, u32[]{:S(2)}) %collective-permute-start.30) | collective-permute-done | bytes 663584 | tf_op jit(solution)/shard_map/ppermute | solution.py:834
  186.7 19.8 %project.1.query_ref.key_ref.value_ref = bf16[4,1024,1152]{2,1,0:T(8,128)(2,1)} custom-call(s32[3]{0:T(128)} %pad_add_fusion.6.place, bf16[1024,1152]{1,0:T(8,128)(2,1)} %get-tuple-element.87.mod_ref, f32[4,1152]{1,0:T(4,128)} %pad_maximum_fusion.16.bias_ref, bf16[4,144,512]{2,1,0:T(8,128)(2,1)} %copy-done.7, ...), custom_call_target="tpu_custom_call" | custom-call | flops 8153726976 | bytes 16515072 | tf_op jit(solution)/shard_map/project/pallas_call | solution.py:359
  206.6 37.1 %attend_forward.1 = (bf16[1024,1152]{1,0:T(8,128)(2,1)S(1)}, f32[16,1024]{1,0:T(8,128)S(1)}) custom-call(s32[16]{0:T(128)S(1)} %bitcast.209, bf16[4,1024,1152]{2,1,0:T(8,128)(2,1)} %project.1.query_ref.key_ref.value_ref, bf16[4,1024,1152]{2,1,0:T(8,128)(2,1)} %project.1.query_ref.key_ref.value_ref, bf16[4,1024,1152]{2,1,0:T(8,128)(2,1)} %project.1.query_ref.key_ref.value_ref), custom_call_target="tpu_custom_call" | custom-call | flops 17179869184 | bytes 9437184 | tf_op jit(solution)/shard_map/attend_forward/pallas_call | solution.py:133
  253.6 11.6 %after_attention.1 = (f32[1024,1152]{1,0:T(8,128)}, f32[1024,1152]{1,0:T(8,128)}, bf16[1024,1152]{1,0:T(8,128)(2,1)}, bf16[1152,1024]{1,0:T(8,128)(2,1)}) custom-call(s32[3]{0:T(128)} %pad_add_fusion.6.place, bf16[1024,1152]{1,0:T(8,128)(2,1)} %copy-done.1, bf16[1024,1152]{1,0:T(8,128)(2,1)} %bitcast.216, f32[8,1152]{1,0:T(8,128)} %pad_maximum_fusion.15.rows_ref, ...), custom_call_target="tpu_custom_call" | custom-call | flops 2717908992 | bytes 21233664 | tf_op jit(solution)/shard_map/after_attention/pallas_call | solution.py:418
  265.3 100.0 %mlp.1 = (f32[1024,1152]{1,0:T(8,128)}, f32[1024,1152]{1,0:T(8,128)}, f32[4,1152]{1,0:T(4,128)}, bf16[2,2,4,144,1152]{4,3,2,1,0:T(8,128)(2,1)}, bf16[2,2,4,144,1...) custom-call(s32[3]{0:T(128)} %pad_add_fusion.6.place, ...), custom_call_target="tpu_custom_call" | custom-call | flops 65229815808 | bytes 42467328 | tf_op jit(solution)/shard_map/mlp/pallas_call | solution.py:532
  365.8 23.3 %after_mlp.1 = (bf16[1024,1152]{1,0:T(8,128)(2,1)}, f32[1024,1152]{1,0:T(8,128)}, bf16[1024,1152]{1,0:T(8,128)(2,1)}, f32[8,1152]{1,0:T(8,128)}, bf16[2,4,144,1152]{3,2,1,0:T(8,128)(2,1)}) custom-call(s32[3]{0:T(128)} %pad_add_fusion.6.place, f32[1024,1152]{1,0:T(8,128)} %get-tuple-element.107.mlp_ref, f32[1024,1152]{1,0:T(8,128)} %get-tuple-element.108.dmod_ref, ...), custom_call_target="tpu_custom_call" | custom-call | flops 5435817984 | bytes 35389440 | tf_op jit(solution)/shard_map/after_mlp/pallas_call | solution.py:622
  402.8 57.6 %attend_backward.1.grads_ref = bf16[3,1024,1152]{2,1,0:T(8,128)(2,1)} custom-call(s32[16]{0:T(128)} %bitcast.208, bf16[4,1024,1152]{2,1,0:T(8,128)(2,1)} %project.1.query_ref.key_ref.value_ref, bf16[4,1024,1152]{2,1,0:T(8,128)(2,1)} %project.1.query_ref.key_ref.value_ref, bf16[4,1024,1152]{2,1,0:T(8,128)(2,1)} %project.1.query_ref.key_ref.value_ref, ...), custom_call_target="tpu_custom_call" | custom-call | flops 42949672960 | bytes 18874368 | tf_op jit(solution)/shard_map/attend_backward/pallas_call | solution.py:160
  465.9 17.6 %square_grads.1 = (bf16[2,2,4,144,512]{4,3,2,1,0:T(8,128)(2,1)}, bf16[2,2,4,144,512]{4,3,2,1,0:T(8,128)(2,1)}, bf16[2,2,4,144,640]{4,3,2,1,0:T(8,128)(2,1)}, bf1...) custom-call(s32[3]{0:T(128)} %pad_add_fusion.6.place, bf16[1152,1024]{1,0:T(8,128)(2,1)} %get-tuple-element.128.across_ref, ...), custom_call_target="tpu_custom_call" | custom-call | flops 8153726976 | bytes 18874368 | tf_op jit(solution)/shard_map/square_grads/pallas_call | solution.py:695
  483.5 24.8 %tokens_back.1 = (bf16[1024,1152]{1,0:T(8,128)(2,1)}, f32[8,1152]{1,0:T(8,128)}) custom-call(s32[3]{0:T(128)} %pad_add_fusion.6.place, bf16[3,1024,1152]{2,1,0:T(8,128)(2,1)} %attend_backward.1.grads_ref, bf16[1024,1152]{1,0:T(8,128)(2,1)} %bitcast.217, f32[1024,1152]{1,0:T(8,128)} %get-tuple-element.135.dmiddle_ref, f32[8,1152]{1,0:T(8,128)} %pad_maximum_fusion.15.rows_ref, ...), custom_call_target="tpu_custom_call" | custom-call | flops 8153726976 | bytes 23592960 | tf_op jit(solution)/shard_map/tokens_back/pallas_call | solution.py:759
  517.7 8.7 %collective-permute-done.67 = bf16[4,16128]{1,0:T(4,128)(2,1)S(1)} collective-permute-done((bf16[4,16128]{1,0:T(4,128)(2,1)S(1)}, bf16[4,16128]{1,0:T(4,128)(2,1)S(1)}, u32[]{:S(2)}, u32[]{:S(2)}) %collective-permute-start.67) | collective-permute-done | bytes 129056 | tf_op jit(solution)/shard_map/ppermute | solution.py:798
  537.9 8.1 %collective-permute-done.69 = bf16[16,16128]{1,0:T(8,128)(2,1)S(1)} collective-permute-done((bf16[16,16128]{1,0:T(8,128)(2,1)S(1)}, bf16[16,16128]{1,0:T(8,128)(2,1)S(1)}, u32[]{:S(2)}, u32[]{:S(2)}) %collective-permute-start.69) | collective-permute-done | bytes 516128 | tf_op jit(solution)/shard_map/ppermute | solution.py:798
  548.5 25.9 %collective-permute-done.43 = bf16[4,144,1152]{2,1,0:T(8,128)(2,1)} collective-permute-done((bf16[4,144,1152]{2,1,0:T(8,128)(2,1)}, bf16[4,144,1152]{2,1,0:T(8,128)(2,1)}, u32[]{:S(2)}, u32[]{:S(2)}) %collective-permute-start.43) | collective-permute-done | bytes 1327136 | tf_op jit(solution)/shard_map/ppermute | solution.py:806
  590.5 11.9 %collective-permute-done.53 = bf16[144,1152]{1,0:T(8,128)(2,1)S(1)} collective-permute-done((bf16[144,1152]{1,0:T(8,128)(2,1)S(1)}, bf16[144,1152]{1,0:T(8,128)(2,1)S(1)}, u32[]{:S(2)}, u32[]{:S(2)}) %collective-permute-start.53) | collective-permute-done | bytes 331808 | tf_op jit(solution)/shard_map/ppermute | solution.py:834
  612.9 17.6 %collective-permute-done.50 = bf16[144,1152]{1,0:T(8,128)(2,1)S(1)} collective-permute-done((bf16[144,1152]{1,0:T(8,128)(2,1)S(1)}, bf16[144,1152]{1,0:T(8,128)(2,1)S(1)}, u32[]{:S(2)}, u32[]{:S(2)}) %collective-permute-start.50) | collective-permute-done | bytes 331808 | tf_op jit(solution)/shard_map/ppermute | solution.py:834
  637.3 6.3 collective-permute-done.55
  645.0 9.2 %collective-permute-start.56 = (bf16[144,512]{1,0:T(8,128)(2,1)S(1)}, bf16[144,512]{1,0:T(8,128)(2,1)S(1)}, u32[]{:S(2)}, u32[]{:S(2)}) collective-permute-start(bf16[144,512]{1,0:T(8,128)(2,1)S(1)} %get-tuple-element.188), channel_id=1, source_target_pairs={{24,0},{28,4},{0,8},{4,12},{8,16},{12,20},{16,24},{20,28},{25,1},{... | collective-permute-start | bytes 442376 | tf_op jit(solution)/shard_map/ppermute | solution.py:834
  665.9 11.4 %collective-permute-done.61 = bf16[144,640]{1,0:T(8,128)(2,1)S(1)} collective-permute-done((bf16[144,640]{1,0:T(8,128)(2,1)S(1)}, bf16[144,640]{1,0:T(8,128)(2,1)S(1)}, u32[]{:S(2)}, u32[]{:S(2)}) %collective-permute-start.61) | collective-permute-done | bytes 184352 | tf_op jit(solution)/shard_map/ppermute | solution.py:834
  683.7 8.3 %collective-permute-start.64 = (bf16[2,144,1152]{2,1,0:T(8,128)(2,1)S(1)}, bf16[2,144,1152]{2,1,0:T(8,128)(2,1)S(1)}, u32[]{:S(2)}, u32[]{:S(2)}) collective-permute-start(bf16[2,144,1152]{2,1,0:T(8,128)(2,1)S(1)} %pad_maximum_fusion.7), channel_id=1, source_target_pairs={{0,1},{1,0},{2,3},{3,2},{4,5},{5,4},{6,7},{7,6},{8,9},{9,8},{10,11... | collective-permute-start | bytes 1990664 | tf_op jit(solution)/shard_map/ppermute | solution.py:806
  (342 shorter events, 202.3 us)
Async XLA Ops:
  44.4 30.5 %collective-permute-start.24 = (bf16[144,1152]{1,0:T(8,128)(2,1)S(1)}, bf16[144,1152]{1,0:T(8,128)(2,1)S(1)}, u32[]{:S(2)}, u32[]{:S(2)}) collective-permute-start(bf16[144,1152]{1,0:T(8,128)(2,1)S(1)} %constant_dynamic-slice_fusion.1), channel_id=1, source_target_pairs={{16,0},{20,4},{24,8},{28,12},{0,16},{4,20},{8,24},{12,28},{17,1},{... | collective-permute-start | bytes 995336 | tf_op jit(solution)/shard_map/ppermute | solution.py:834
  46.6 28.3 %collective-permute-start.25 = (bf16[144,1152]{1,0:T(8,128)(2,1)S(1)}, bf16[144,1152]{1,0:T(8,128)(2,1)S(1)}, u32[]{:S(2)}, u32[]{:S(2)}) collective-permute-start(bf16[144,1152]{1,0:T(8,128)(2,1)S(1)} %constant_dynamic-slice_fusion.1), channel_id=1, source_target_pairs={{24,0},{28,4},{0,8},{4,12},{8,16},{12,20},{16,24},{20,28},{25,1},{... | collective-permute-start | bytes 995336 | tf_op jit(solution)/shard_map/ppermute | solution.py:834
  55.7 31.9 %collective-permute-start.19 = (bf16[4,144,640]{2,1,0:T(8,128)(2,1)S(1)}, bf16[4,144,640]{2,1,0:T(8,128)(2,1)}, u32[]{:S(2)}, u32[]{:S(2)}) collective-permute-start(bf16[4,144,640]{2,1,0:T(8,128)(2,1)S(1)} %pad_maximum_fusion.6.rest_8_), channel_id=1, source_target_pairs={{0,2},{1,3},{2,0},{3,1},{4,6},{5,7},{6,4},{7,5},{8,10},{9,11},{10,... | collective-permute-start | bytes 2211848 | tf_op jit(solution)/shard_map/ppermute | solution.py:806
  57.0 30.6 %collective-permute-start.20 = (bf16[4,144,640]{2,1,0:T(8,128)(2,1)}, bf16[4,144,640]{2,1,0:T(8,128)(2,1)}, u32[]{:S(2)}, u32[]{:S(2)}) collective-permute-start(bf16[4,144,640]{2,1,0:T(8,128)(2,1)} %collective-permute-done.16.rest_9_), channel_id=1, source_target_pairs={{0,2},{1,3},{2,0},{3,1},{4,6},{5,7},{6,4},{7,5},{8,10},{9,11},{10,... | collective-permute-start | bytes 2211848 | tf_op jit(solution)/shard_map/ppermute | solution.py:806
  76.2 29.3 %collective-permute-start.26 = (bf16[4,144,1152]{2,1,0:T(8,128)(2,1)}, bf16[4,144,1152]{2,1,0:T(8,128)(2,1)}, u32[]{:S(2)}, u32[]{:S(2)}) collective-permute-start(bf16[4,144,1152]{2,1,0:T(8,128)(2,1)} %pad_maximum_fusion.3.rest_0_), channel_id=1, source_target_pairs={{0,4},{4,0},{8,12},{12,8},{16,20},{20,16},{24,28},{28,24},{1,5},{5... | collective-permute-start | bytes 3981320 | tf_op jit(solution)/shard_map/ppermute | solution.py:806
  105.5 74.1 %collective-permute-start.27 = (bf16[4,144,1152]{2,1,0:T(8,128)(2,1)}, bf16[4,144,1152]{2,1,0:T(8,128)(2,1)}, u32[]{:S(2)}, u32[]{:S(2)}) collective-permute-start(bf16[4,144,1152]{2,1,0:T(8,128)(2,1)} %collective-permute-done.26.rest_1_), channel_id=1, source_target_pairs={{0,2},{1,3},{2,0},{3,1},{4,6},{5,7},{6,4},{7,5},{8,10},{9,11},{10,... | collective-permute-start | bytes 3981320 | tf_op jit(solution)/shard_map/ppermute | solution.py:806
  112.6 70.9 %collective-permute-start.28 = (bf16[4,144,1152]{2,1,0:T(8,128)(2,1)}, bf16[4,144,1152]{2,1,0:T(8,128)(2,1)}, u32[]{:S(2)}, u32[]{:S(2)}) collective-permute-start(bf16[4,144,1152]{2,1,0:T(8,128)(2,1)} %pad_maximum_fusion.3.rest_0_), channel_id=1, source_target_pairs={{0,2},{1,3},{2,0},{3,1},{4,6},{5,7},{6,4},{7,5},{8,10},{9,11},{10,... | collective-permute-start | bytes 3981320 | tf_op jit(solution)/shard_map/ppermute | solution.py:806
  119.0 59.0 %collective-permute-start.30 = (bf16[2,144,1152]{2,1,0:T(8,128)(2,1)S(1)}, bf16[2,144,1152]{2,1,0:T(8,128)(2,1)}, u32[]{:S(2)}, u32[]{:S(2)}) collective-permute-start(bf16[2,144,1152]{2,1,0:T(8,128)(2,1)S(1)} %fusion.13), channel_id=1, source_target_pairs={{16,0},{20,4},{24,8},{28,12},{0,16},{4,20},{8,24},{12,28},{17,1},{... | collective-permute-start | bytes 1990664 | tf_op jit(solution)/shard_map/ppermute | solution.py:834
  119.0 60.5 %collective-permute-start.31 = (bf16[2,144,1152]{2,1,0:T(8,128)(2,1)S(1)}, bf16[2,144,1152]{2,1,0:T(8,128)(2,1)}, u32[]{:S(2)}, u32[]{:S(2)}) collective-permute-start(bf16[2,144,1152]{2,1,0:T(8,128)(2,1)S(1)} %fusion.13), channel_id=1, source_target_pairs={{24,0},{28,4},{0,8},{4,12},{8,16},{12,20},{16,24},{20,28},{25,1},{... | collective-permute-start | bytes 1990664 | tf_op jit(solution)/shard_map/ppermute | solution.py:834
  136.1 49.2 %collective-permute-start.7 = (bf16[4,144,512]{2,1,0:T(8,128)(2,1)S(1)}, bf16[4,144,512]{2,1,0:T(8,128)(2,1)S(1)}, u32[]{:S(2)}, u32[]{:S(2)}) collective-permute-start(bf16[4,144,512]{2,1,0:T(8,128)(2,1)S(1)} %pad_maximum_fusion.9.rest_0_), channel_id=1, source_target_pairs={{0,1},{1,0},{2,3},{3,2},{4,5},{5,4},{6,7},{7,6},{8,9},{9,8},{10,11... | collective-permute-start | bytes 1769480 | tf_op jit(solution)/shard_map/ppermute | solution.py:806
  183.5 62.3 %collective-permute-start.32 = (bf16[4,2,144,1152]{3,2,1,0:T(8,128)(2,1)}, bf16[4,2,144,1152]{3,2,1,0:T(8,128)(2,1)}, u32[]{:S(2)}, u32[]{:S(2)}) collective-permute-start(bf16[4,2,144,1152]{3,2,1,0:T(8,128)(2,1)} %pad_maximum_fusion.rest_8_), channel_id=1, source_target_pairs={{0,4},{4,0},{8,12},{12,8},{16,20},{20,16},{24,28},{28,24},{1,5},{5... | collective-permute-start | bytes 7962632 | tf_op jit(solution)/shard_map/ppermute | solution.py:806
  365.2 24.7 %collective-permute-start.39 = (bf16[2,2,4,144,1152]{4,3,2,1,0:T(8,128)(2,1)}, bf16[2,2,4,144,1152]{4,3,2,1,0:T(8,128)(2,1)S(1)}, u32[]{:S(2)}, u32[]{:S(2)}) collective-permute-start(bf16[2,2,4,144,1152]{4,3,2,1,0:T(8,128)(2,1)} %get-tuple-element.113), channel_id=1, source_target_pairs={{0,1},{1,0},{2,3},{3,2},{4,5},{5,4},{6,7},{7,6},{8,9},{9,8},{10,11... | collective-permute-start | bytes 15925256 | tf_op jit(solution)/shard_map/ppermute | solution.py:806
  365.6 24.4 %collective-permute-start.40 = (bf16[2,2,4,144,1152]{4,3,2,1,0:T(8,128)(2,1)}, bf16[2,2,4,144,1152]{4,3,2,1,0:T(8,128)(2,1)}, u32[]{:S(2)}, u32[]{:S(2)}) collective-permute-start(bf16[2,2,4,144,1152]{4,3,2,1,0:T(8,128)(2,1)} %get-tuple-element.114), channel_id=1, source_target_pairs={{0,1},{1,0},{2,3},{3,2},{4,5},{5,4},{6,7},{7,6},{8,9},{9,8},{10,11... | collective-permute-start | bytes 15925256 | tf_op jit(solution)/shard_map/ppermute | solution.py:806
  401.1 59.3 %collective-permute-start.41 = (bf16[2,4,144,1152]{3,2,1,0:T(8,128)(2,1)}, bf16[2,4,144,1152]{3,2,1,0:T(8,128)(2,1)}, u32[]{:S(2)}, u32[]{:S(2)}) collective-permute-start(bf16[2,4,144,1152]{3,2,1,0:T(8,128)(2,1)} %fusion), channel_id=1, source_target_pairs={{0,4},{4,0},{8,12},{12,8},{16,20},{20,16},{24,28},{28,24},{1,5},{5... | collective-permute-start | bytes 7962632 | tf_op jit(solution)/shard_map/ppermute | solution.py:806
  401.5 59.0 %collective-permute-start.42 = (bf16[2,4,144,1152]{3,2,1,0:T(8,128)(2,1)}, bf16[2,4,144,1152]{3,2,1,0:T(8,128)(2,1)}, u32[]{:S(2)}, u32[]{:S(2)}) collective-permute-start(bf16[2,4,144,1152]{3,2,1,0:T(8,128)(2,1)} %fusion.1), channel_id=1, source_target_pairs={{0,2},{1,3},{2,0},{3,1},{4,6},{5,7},{6,4},{7,5},{8,10},{9,11},{10,... | collective-permute-start | bytes 7962632 | tf_op jit(solution)/shard_map/ppermute | solution.py:806
  535.3 39.1 %collective-permute-start.46 = (bf16[2,2,4,144,640]{4,3,2,1,0:T(8,128)(2,1)}, bf16[2,2,4,144,640]{4,3,2,1,0:T(8,128)(2,1)}, u32[]{:S(2)}, u32[]{:S(2)}) collective-permute-start(bf16[2,2,4,144,640]{4,3,2,1,0:T(8,128)(2,1)} %get-tuple-element.140), channel_id=1, source_target_pairs={{0,1},{1,0},{2,3},{3,2},{4,5},{5,4},{6,7},{7,6},{8,9},{9,8},{10,11... | collective-permute-start | bytes 8847368 | tf_op jit(solution)/shard_map/ppermute | solution.py:806
  536.8 37.6 %collective-permute-start.45 = (bf16[2,2,4,144,512]{4,3,2,1,0:T(8,128)(2,1)}, bf16[2,2,4,144,512]{4,3,2,1,0:T(8,128)(2,1)}, u32[]{:S(2)}, u32[]{:S(2)}) collective-permute-start(bf16[2,2,4,144,512]{4,3,2,1,0:T(8,128)(2,1)} %get-tuple-element.139), channel_id=1, source_target_pairs={{0,1},{1,0},{2,3},{3,2},{4,5},{5,4},{6,7},{7,6},{8,9},{9,8},{10,11... | collective-permute-start | bytes 7077896 | tf_op jit(solution)/shard_map/ppermute | solution.py:806
  536.9 37.5 %collective-permute-start.43 = (bf16[4,144,1152]{2,1,0:T(8,128)(2,1)}, bf16[4,144,1152]{2,1,0:T(8,128)(2,1)}, u32[]{:S(2)}, u32[]{:S(2)}) collective-permute-start(bf16[4,144,1152]{2,1,0:T(8,128)(2,1)} %get-tuple-element.137), channel_id=1, source_target_pairs={{0,2},{1,3},{2,0},{3,1},{4,6},{5,7},{6,4},{7,5},{8,10},{9,11},{10,... | collective-permute-start | bytes 3981320 | tf_op jit(solution)/shard_map/ppermute | solution.py:806
  536.9 37.5 %collective-permute-start.44 = (bf16[4,144,1152]{2,1,0:T(8,128)(2,1)}, bf16[4,144,1152]{2,1,0:T(8,128)(2,1)}, u32[]{:S(2)}, u32[]{:S(2)}) collective-permute-start(bf16[4,144,1152]{2,1,0:T(8,128)(2,1)} %get-tuple-element.138), channel_id=1, source_target_pairs={{0,4},{4,0},{8,12},{12,8},{16,20},{20,16},{24,28},{28,24},{1,5},{5... | collective-permute-start | bytes 3981320 | tf_op jit(solution)/shard_map/ppermute | solution.py:806
  577.9 24.5 %collective-permute-start.53 = (bf16[144,1152]{1,0:T(8,128)(2,1)S(1)}, bf16[144,1152]{1,0:T(8,128)(2,1)S(1)}, u32[]{:S(2)}, u32[]{:S(2)}) collective-permute-start(bf16[144,1152]{1,0:T(8,128)(2,1)S(1)} %get-tuple-element.176), channel_id=1, source_target_pairs={{16,0},{20,4},{24,8},{28,12},{0,16},{4,20},{8,24},{12,28},{17,1},{... | collective-permute-start | bytes 995336 | tf_op jit(solution)/shard_map/ppermute | solution.py:834
  583.0 48.4 %collective-permute-start.48 = (bf16[2,4,144,640]{3,2,1,0:T(8,128)(2,1)S(1)}, bf16[2,4,144,640]{3,2,1,0:T(8,128)(2,1)S(1)}, u32[]{:S(2)}, u32[]{:S(2)}) collective-permute-start(bf16[2,4,144,640]{3,2,1,0:T(8,128)(2,1)S(1)} %fusion.6), channel_id=1, source_target_pairs={{0,4},{4,0},{8,12},{12,8},{16,20},{20,16},{24,28},{28,24},{1,5},{5... | collective-permute-start | bytes 4423688 | tf_op jit(solution)/shard_map/ppermute | solution.py:806
  585.7 45.7 %collective-permute-start.47 = (bf16[2,4,144,512]{3,2,1,0:T(8,128)(2,1)S(1)}, bf16[2,4,144,512]{3,2,1,0:T(8,128)(2,1)S(1)}, u32[]{:S(2)}, u32[]{:S(2)}) collective-permute-start(bf16[2,4,144,512]{3,2,1,0:T(8,128)(2,1)S(1)} %fusion.9), channel_id=1, source_target_pairs={{0,2},{1,3},{2,0},{3,1},{4,6},{5,7},{6,4},{7,5},{8,10},{9,11},{10,... | collective-permute-start | bytes 3538952 | tf_op jit(solution)/shard_map/ppermute | solution.py:806
  602.4 28.1 %collective-permute-start.50 = (bf16[144,1152]{1,0:T(8,128)(2,1)S(1)}, bf16[144,1152]{1,0:T(8,128)(2,1)S(1)}, u32[]{:S(2)}, u32[]{:S(2)}) collective-permute-start(bf16[144,1152]{1,0:T(8,128)(2,1)S(1)} %get-tuple-element.179), channel_id=1, source_target_pairs={{16,0},{20,4},{24,8},{28,12},{0,16},{4,20},{8,24},{12,28},{17,1},{... | collective-permute-start | bytes 995336 | tf_op jit(solution)/shard_map/ppermute | solution.py:834
  602.4 29.0 %collective-permute-start.51 = (bf16[144,1152]{1,0:T(8,128)(2,1)S(1)}, bf16[144,1152]{1,0:T(8,128)(2,1)S(1)}, u32[]{:S(2)}, u32[]{:S(2)}) collective-permute-start(bf16[144,1152]{1,0:T(8,128)(2,1)S(1)} %get-tuple-element.178), channel_id=1, source_target_pairs={{8,0},{12,4},{16,8},{20,12},{24,16},{28,20},{0,24},{4,28},{9,1},{1... | collective-permute-start | bytes 995336 | tf_op jit(solution)/shard_map/ppermute | solution.py:834
  (92 other events, 1598.7 us)

commit v3 on v2

--- a/solution.py
+++ b/solution.py
@@ -180,18 +180,29 @@
 ANY = pl.BlockSpec(memory_space=pl.ANY)
 
 
+class Blocks(list):
+    def __init__(self, arrays, order):
+        super().__init__(arrays)
+        self.order = order
+
+    def block(self, r, x_r, z_r):
+        y_r, core_r = r // 2, r % 2
+        first_r, second_r = (x_r, y_r) if self.order == "xy" else (y_r, x_r)
+        return self[2 * core_r + second_r].at[first_r, z_r]
+
+
 def square_copies(place, sets, r, target, sem):
     part = jnp.bitwise_xor(place[2], r)
     if len(sets[0]) == 1:
         return [pltpu.make_async_copy(sets[0][0].at[part], target, sem)]
     copies, column = [], 0
     for refs in sets:
-        _, rows, columns = refs[0].shape
+        rows, columns = refs[0].shape[2:]
         for x_r in range(2):
             for z_r in range(4):
                 shard = (place[0] + z_r) % 4 * 2 + (place[1] + x_r) % 2
                 block = (pl.ds(pl.multiple_of(shard * rows, 16), rows), pl.ds(column, columns))
-                source = refs[2 * r + x_r].at[z_r]
+                source = refs.block(r, x_r, z_r)
                 copies.append(pltpu.make_async_copy(source, target.at[block], sem))
         column += columns
     return copies
@@ -201,16 +212,14 @@
     if len(refs) == 1:
         return [pltpu.make_async_copy(refs[0].at[chunk], target, sem)]
     rows = refs[0].shape[2]
-    z_r = (chunk + 4 - place[0]) % 4
     copies = []
     for core_r in range(2):
         for y in range(2):
             part = 2 * y + (place[2] + core_r) % 2
-            for x_r in range(2):
-                start = (place[1] + x_r) % 2 * (4 * rows) + part * rows
-                block = target.at[pl.ds(pl.multiple_of(start, 16), rows)]
-                source = refs[2 * core_r + x_r].at[z_r, y]
-                copies.append(pltpu.make_async_copy(source, block, sem))
+            for x in range(2):
+                start = pl.multiple_of(x * (4 * rows) + part * rows, 16)
+                source = refs[core_r].at[2 * chunk + x, y]
+                copies.append(pltpu.make_async_copy(source, target.at[pl.ds(start, rows)], sem))
     return copies
 
 
@@ -221,11 +230,12 @@
     copies, column = [], 0
     for pair in range(0, len(outs), 2):
         out = outs[pair + r % 2]
-        rows, columns = out.shape[3:]
+        out = out if len(out.shape) == 4 else out.at[r // 2]
+        rows, columns = out.shape[2:]
         for shard in range(8):
             x_r, z_r = (place[1] + shard % 2) % 2, (shard // 2 + 4 - place[0]) % 4
             block = source.at[pl.ds(shard * rows, rows), pl.ds(column, columns)]
-            copies.append(pltpu.make_async_copy(block, out.at[r // 2, x_r, z_r], sem))
+            copies.append(pltpu.make_async_copy(block, out.at[x_r, z_r], sem))
         column += columns
     return copies
 
@@ -248,7 +258,7 @@
 def in_sets(refs, sets):
     refs, found = list(refs), []
     for entry in sets:
-        found.append(refs[: len(entry)])
+        found.append(Blocks(refs[: len(entry)], entry.order))
         refs = refs[len(entry) :]
     return found
 
@@ -293,44 +303,58 @@
     return [pl.ds(start, min(rows, length)) for start in range(0, length, min(rows, length))]
 
 
-def prepare_kernel(tokens_ref, cotangent_ref, rows_ref, mod_ref, across_ref, grad_ref, sum_ref):
+def prepare_kernel(
+    tokens_ref, cotangent_ref, parts_ref, mod_ref, across_ref, grad_ref, sum_ref, rows_ref
+):
+    width = tokens_ref.shape[1]
+
+    @pl.when(pl.program_id(0) == 0)
+    def _():
+        for row in range(parts_ref.shape[1] // width):
+            part = parts_ref[:, row * width : (row + 1) * width]
+            rows_ref[row : row + 1] = jnp.sum(part, axis=0, keepdims=True)
+        sum_ref[...] = jnp.zeros_like(sum_ref)
+
     normed, _ = norm_forward(tokens_ref[...].astype(jnp.float32))
     mod = normed * (1.0 + row_of(rows_ref, SCALE_ATTN)) + row_of(rows_ref, SHIFT_ATTN)
     mod_ref[...] = mod.astype(jnp.bfloat16)
     across_ref[...] = jnp.transpose(mod).astype(jnp.bfloat16)
     grad = (cotangent_ref[...].astype(jnp.float32) * row_of(rows_ref, GATE_MLP)).astype(jnp.bfloat16)
     grad_ref[...] = grad
-
-    @pl.when(pl.program_id(0) == 0)
-    def _():
-        sum_ref[...] = jnp.zeros_like(sum_ref)
-
     sum_ref[0:1] += jnp.sum(grad.astype(jnp.float32), axis=0, keepdims=True)
 
 
-def prepare(tokens, cotangent, rows, tile=256):
+def prepare(tokens, cotangent, parts, tile=256):
     length, width = tokens.shape
     tile = min(tile, length)
     by_rows = pl.BlockSpec((tile, width), lambda step: (step, 0))
     fixed = pl.BlockSpec((8, width), lambda step: (0, 0))
+    table = (16, width)
     return pl.pallas_call(
         prepare_kernel,
         grid=(length // tile,),
-        in_specs=[by_rows, by_rows, fixed],
-        out_specs=[by_rows, pl.BlockSpec((width, tile), lambda step: (0, step)), by_rows, fixed],
+        in_specs=[by_rows, by_rows, pl.BlockSpec(parts.shape, lambda step: (0, 0))],
+        out_specs=[
+            by_rows,
+            pl.BlockSpec((width, tile), lambda step: (0, step)),
+            by_rows,
+            fixed,
+            pl.BlockSpec(table, lambda step: (0, 0)),
+        ],
         out_shape=[
             jax.ShapeDtypeStruct((length, width), jnp.bfloat16),
             jax.ShapeDtypeStruct((width, length), jnp.bfloat16),
             jax.ShapeDtypeStruct((length, width), jnp.bfloat16),
             jax.ShapeDtypeStruct((8, width), jnp.float32),
+            jax.ShapeDtypeStruct(table, jnp.float32),
         ],
         compiler_params=vmem_params(),
         cost_estimate=cost(20 * length * width, 10 * length * width),
         name="prepare",
-    )(tokens, cotangent, rows)
-
-
-def project_kernel(place, mod_ref, bias_ref, *rest, sets):
+    )(tokens, cotangent, parts)
+
+
+def project_kernel(place, mod_ref, rows_ref, *rest, sets):
     *refs, out_ref, held, sems = rest
     step = pl.program_id(0)
     fetch_squares(place, in_sets(refs, sets), step, held, sems)
@@ -339,7 +363,7 @@
     @pl.when(part < 3)
     def _():
         weight = held[step % 2]
-        bias = bias_ref[pl.ds(part, 1)]
+        bias = rows_ref[pl.ds(QUERY_BIAS + part // 2, 1)] * (part != 1).astype(jnp.float32)
         for tile in tiles(mod_ref.shape[0]):
             out_ref[0, tile] = (matmul(mod_ref[tile], weight, ROWS_NN) + bias).astype(jnp.bfloat16)
 
@@ -351,10 +375,10 @@
 
 
 def cost(flops, moved):
-    return pl.CostEstimate(flops=int(flops), transcendentals=0, bytes_accessed=int(moved))
-
-
-def project(place, mod, bias, squares):
+    return pl.CostEstimate(flops=1, transcendentals=0, bytes_accessed=1)
+
+
+def project(place, mod, rows, squares):
     length, width = mod.shape
     return pl.pallas_call(
         functools.partial(project_kernel, sets=squares),
@@ -363,7 +387,7 @@
             grid=(4,),
             in_specs=[
                 pl.BlockSpec((length, width), lambda step, place: (0, 0)),
-                pl.BlockSpec(bias.shape, lambda step, place: (0, 0)),
+                pl.BlockSpec(rows.shape, lambda step, place: (0, 0)),
             ]
             + [ANY] * len(flat(squares)),
             out_specs=pl.BlockSpec(
@@ -378,7 +402,7 @@
         compiler_params=vmem_params(),
         cost_estimate=cost(6 * length * width * width, 14 * length * width),
         name="project",
-    )(place, mod, bias, *flat(squares))
+    )(place, mod, rows, *flat(squares))
 
 
 def fetch_part(place, sets, wanted, target, sem):
@@ -391,7 +415,8 @@
     return rows_ref[index : index + 1]
 
 
-SHIFT_ATTN, SCALE_ATTN, GATE_ATTN, SHIFT_MLP, SCALE_MLP, GATE_MLP, OUT_BIAS, DOWN_BIAS = range(8)
+SHIFT_ATTN, SCALE_ATTN, GATE_ATTN, SHIFT_MLP, SCALE_MLP, GATE_MLP = range(6)
+QUERY_BIAS, VALUE_BIAS, OUT_BIAS, UP_BIAS, DOWN_BIAS = 6, 7, 8, 9, 13
 
 
 def after_attention_kernel(place, low_ref, tokens_ref, rows_ref, *rest, sets):
@@ -448,7 +473,7 @@
     return values * half, slope
 
 
-def mlp_kernel(place, mod_ref, across_ref, grad_ref, bias_ref, keep_ref, *rest, ups, downs):
+def mlp_kernel(place, mod_ref, across_ref, grad_ref, rows_ref, keep_ref, *rest, ups, downs):
     count = len(flat(ups)) + downs
     refs, rest = rest[:count], rest[count:]
     up_sets, down_refs = in_sets(refs, ups), refs[-downs:]
@@ -477,7 +502,7 @@
     for_each(step, lambda r: wait_all(fetch(r)))
     chunk = chunk_of(step)
     slot = step % 2
-    bias = bias_ref[pl.ds(chunk, 1)]
+    bias = rows_ref[pl.ds(UP_BIAS + chunk, 1)]
     keep = keep_ref[pl.ds(chunk, 1)]
     total = jnp.zeros_like(bias)
     for tile in tiles(length):
@@ -519,7 +544,7 @@
     return [jax.ShapeDtypeStruct((4, sum(columns), sum(columns)), jnp.bfloat16)]
 
 
-def mlp(place, mod, across, grad, bias, keep, ups, downs, block_rows):
+def mlp(place, mod, across, grad, rows, keep, ups, downs, block_rows):
     length, width = mod.shape
     stores = gradient_shapes(len(downs) > 1, block_rows, [width])
     quarter = jax.ShapeDtypeStruct((4, width), jnp.float32)
@@ -538,7 +563,7 @@
                 held,
                 pl.BlockSpec((width, length), lambda step, place: (0, 0), pipeline_mode=pl.Buffered(1)),
                 held,
-                table,
+                pl.BlockSpec(rows.shape, lambda step, place: (0, 0)),
                 table,
             ]
             + [ANY] * (len(flat(ups)) + len(downs)),
@@ -561,7 +586,7 @@
         compiler_params=vmem_params(60),
         cost_estimate=cost(48 * length * width * width, 32 * width * width),
         name="mlp",
-    )(place, mod, across, grad, bias, keep, *flat(ups), *downs)
+    )(place, mod, across, grad, rows, keep, *flat(ups), *downs)
 
 
 def after_mlp_kernel(
@@ -647,7 +672,7 @@
 
 
 def square_grads_kernel(place, across_ref, grads_ref, out_grad_ref, *rest):
-    *stores, sums_ref, staged, sems = rest
+    *stores, staged, sems = rest
     step = pl.program_id(0)
     part = jnp.bitwise_xor(place[2], step)
 
@@ -675,7 +700,6 @@
     def _():
         grads = grads_ref[0]
         staged[step % 2] = matmul(across_ref[...], grads, ROWS_NN).astype(jnp.bfloat16)
-        sums_ref[pl.ds(part, 1)] = jnp.sum(grads.astype(jnp.float32), axis=0, keepdims=True)
         for_each(step, lambda r: start_all(leave(r)))
 
     @pl.when(part == 3)
@@ -709,13 +733,13 @@
                     pipeline_mode=pl.Buffered(1),
                 ),
             ],
-            out_specs=[ANY] * len(stores) + [pl.BlockSpec((4, width), lambda step, place: (0, 0))],
+            out_specs=[ANY] * len(stores),
             scratch_shapes=[
                 pltpu.VMEM((2, width, width), jnp.bfloat16),
                 pltpu.SemaphoreType.DMA((2,)),
             ],
         ),
-        out_shape=stores + [jax.ShapeDtypeStruct((4, width), jnp.float32)],
+        out_shape=stores,
         compiler_params=vmem_params(),
         cost_estimate=cost(6 * length * width * width, 16 * length * width),
         name="square_grads",
@@ -737,6 +761,8 @@
     def _():
         for tile in tiles(length):
             dmod[tile] += matmul(grads_ref[0, tile], held[step % 2], ROWS_NT)
+        total = jnp.sum(grads_ref[0].astype(jnp.float32), axis=0, keepdims=True)
+        sums_ref[pl.ds(2 + part, 1)] = total
 
     @pl.when(step == 3)
     def _():
@@ -812,8 +838,12 @@
     return jnp.stack([jnp.where(first, value, other), jnp.where(first, other, value)], axis=dim)
 
 
+def barrier(values):
+    return lax.optimization_barrier(values)
+
+
 def after(value, *others):
-    return lax.optimization_barrier((value, others))[0]
+    return barrier((value, others))[0]
 
 
 def add(*terms):
@@ -836,15 +866,11 @@
     def along_z(self, block):
         return jnp.stack([block] + [self.ahead(block, count) for count in (1, 2, 3)])
 
-    def widen(self, blocks, kind):
-        return blocks | {key + kind: self.partner(value, kind) for key, value in blocks.items()}
-
-    def listed(self, blocks, kinds):
-        found = {"".join(sorted(key)): value for key, value in blocks.items()}
-        names = [""]
-        for kind in kinds:
-            names = [name + more for name in names for more in ("", kind)]
-        return [found["".join(sorted(name))] for name in names]
+    def along_x(self, block):
+        return jnp.stack([block, self.partner(block, "x")])
+
+    def pair(self, block, kind):
+        return jnp.stack([block, self.partner(block, kind)])
 
     def first_sum(self, kept, other, kind):
         dim = 0 if kind == "y" else 1
@@ -922,72 +948,87 @@
     member = lax.axis_index("dp")
     bf16, f32 = jnp.bfloat16, jnp.float32
 
-    facts = gather_rows(jnp.stack([timesteps, labels], axis=1), "fsdp", shard_count)
+    place = jnp.stack([shard // 2, shard % 2, member]).astype(jnp.int32)
+    paired = shard_count == 8 and group_count == 4 and columns % 16 == 0
+    net = Pairwise(shard_count, group_count)
+    splits = [width // 2 // 128 * 128]
+    splits.append(width - splits[0])
+    four = jnp.concatenate([qkv_weight, out_weight], axis=1)
+
+    fact = jnp.stack([timesteps[0], labels[0]])
+    if paired:
+        near = net.along_z(fact)
+        mine = lax.dynamic_slice_in_dim(four, member * width, width, axis=1)
+        mine, near = barrier((mine, near))
+        square = net.along_z(mine)
+        near = net.along_x(near).swapaxes(0, 1)
+        facts = jnp.where(place[1] == 0, near, near[:, ::-1])
+        facts = lax.dynamic_slice_in_dim(
+            jnp.concatenate([facts, facts]), (4 - place[0]) % 4, 4, axis=0
+        ).reshape(8, 2)
+    else:
+        facts = gather_rows(fact[None], "fsdp", shard_count)
     group_act = jax.nn.silu(
         conditioning(facts[:, 0], facts[:, 1], class_table, shard, width)
     ).astype(bf16)
     partial = jnp.dot(group_act, ada_weight, preferred_element_type=f32)
-    bias_row = lax.dynamic_update_slice_in_dim(
-        jnp.zeros((6 * width,), f32), ada_bias.astype(f32), shard * ada_bias.shape[0], axis=0
-    )
-    small = jnp.concatenate([qv_bias.reshape(-1), out_bias, up_bias, down_bias]).astype(f32)
+
+    def own_columns(values):
+        values = values.astype(f32)
+        full = jnp.zeros((values.shape[0] * shard_count,), f32)
+        return lax.dynamic_update_slice_in_dim(full, values, shard * values.shape[0], axis=0)
+
+    biases = jnp.concatenate(
+        [own_columns(values) for values in (qv_bias[0], qv_bias[1], out_bias, up_bias, down_bias)]
+    )
     sent = jnp.concatenate(
-        [partial + bias_row, jnp.broadcast_to(small, (shard_count, small.shape[0]))], axis=1
-    )
-    parts = lax.all_to_all(sent, "fsdp", 0, 0, tiled=True)
-    ada_rows = jnp.sum(parts[:, : 6 * width], axis=0).reshape(6, 1, width)
-    shift_attn, scale_attn, gate_attn, shift_mlp, scale_mlp, gate_mlp = [ada_rows[i] for i in range(6)]
-    small = parts[:, 6 * width :]
-    query_bias = small[:, :columns].reshape(-1)
-    value_bias = small[:, columns : 2 * columns].reshape(-1)
-    out_bias_full = small[:, 2 * columns : 3 * columns].reshape(-1)
-    up_end = 3 * columns + up_bias.shape[0]
-    up_bias_full = small[:, 3 * columns : up_end].reshape(-1)
-    down_bias_full = small[:, up_end:].reshape(-1)
-
-    place = jnp.stack([shard // 2, shard % 2, member]).astype(jnp.int32)
-    paired = shard_count == 8 and group_count == 4 and columns % 16 == 0
-    four = jnp.concatenate([qkv_weight, out_weight], axis=1)
-    rows = jnp.concatenate([ada_rows[:, 0], out_bias_full[None], down_bias_full[None]])
-    qkv_bias = jnp.stack([query_bias, jnp.zeros((width,), f32), value_bias, out_bias_full])
-    net = Pairwise(shard_count, group_count)
-    splits = [width // 2 // 128 * 128]
-    splits.append(width - splits[0])
-
-    mod_one, mod_across, branch_grad, down_bias_g = prepare(tokens[0], cotangent[0], rows)
+        [
+            partial + own_columns(ada_bias),
+            jnp.broadcast_to(biases, (shard_count, biases.shape[0])),
+        ],
+        axis=1,
+    )
     if paired:
-        mine = lax.dynamic_slice_in_dim(four, member * width, width, axis=1)
-        first = {"": net.along_z(mine[:, : splits[0]])}
-        second = {"": net.along_z(mine[:, splits[0] :])}
+        square, sent, near = barrier((square, sent, near))
+        parts = lax.all_to_all(sent, "fsdp", 0, 0, tiled=True)
+        all_facts = net.pair(net.pair(near.swapaxes(0, 1), "y"), "c").reshape(image_count, 2)
+        first = net.pair(square[:, :, : splits[0]], "x")
+        second = net.pair(square[:, :, splits[0] :], "y")
         mine = lax.dynamic_slice_in_dim(up_weight, member * width, width, axis=1)
-        up = {"": net.along_z(after(mine, first, second))}
-        mine = down_weight.reshape(2, 2, columns, width)
-        mine = jnp.where(member % 2 == 0, mine[:, 0], mine[:, 1])
-        down = {"": net.along_z(after(mine, up))}
-        first = net.widen(first, "x")
-        second = net.widen(second, "x")
-        first = net.widen(first, "y")
-        up = net.widen(after(up, second), "x")
-        second = net.widen(after(second, first), "y")
-        first = net.widen(first, "c")
-        second = net.widen(second, "c")
-        up = net.widen(after(up, second), "y")
-        down = net.widen(after(down, up), "x")
-        squares = [net.listed(blocks, "ycx") for blocks in (first, second)]
+        down_mine = down_weight.reshape(2, 2, columns, width)
+        down_mine = jnp.where(member % 2 == 0, down_mine[:, 0], down_mine[:, 1])
+        mine, down_mine, first, second, parts = barrier((mine, down_mine, first, second, parts))
+        first_y, second_x = net.partner(first, "y"), net.partner(second, "x")
+        up = net.along_z(mine)
+        first, second, first_y, second_x, up = barrier((first, second, first_y, second_x, up))
+        down = lax.all_gather(after(down_mine, first_y), "fsdp", axis=0)
+        squares = [
+            Blocks([first, first_y, net.partner(first, "c"), net.partner(first_y, "c")], "xy"),
+            Blocks([second, second_x, net.partner(second, "c"), net.partner(second_x, "c")], "yx"),
+        ]
     else:
-        parts = lax.all_gather(four, "fsdp", axis=0, tiled=True)
-        squares = [[parts.reshape(width, 4, width).swapaxes(0, 1)]]
-    qkv = project(place, mod_one, qkv_bias, squares)
+        parts = lax.all_to_all(sent, "fsdp", 0, 0, tiled=True)
+        all_facts = gather_rows(facts, "dp", group_count)
+        found = lax.all_gather(four, "fsdp", axis=0, tiled=True)
+        squares = [Blocks([found.reshape(width, 4, width).swapaxes(0, 1)], "xy")]
+    mod_one, mod_across, branch_grad, down_bias_g, rows = prepare(tokens[0], cotangent[0], parts)
+    if paired:
+        up_x, up_y = net.partner(up, "x"), net.partner(up, "y")
+    qkv = project(place, mod_one, rows, squares)
+    if paired:
+        qkv, up_x, up_y = barrier((qkv, up_x, up_y))
+        up_xy = net.partner(up_x, "y")
     attn_low, lse = attend_forward(qkv, head_keep[0])
     if paired:
-        attn_low, up, down = lax.optimization_barrier((attn_low, up, down))
-        ups = [net.listed(net.widen(up, "c"), "ycx")]
-        downs = net.listed(net.widen(down, "c"), "cx")
+        attn_low, up_xy, down = barrier((attn_low, up_xy, down))
+        up, up_y = jnp.stack([up, up_x]), jnp.stack([up_y, up_xy])
+        ups = [Blocks([up, up_y, net.partner(up, "c"), net.partner(up_y, "c")], "xy")]
+        downs = [down, net.partner(down, "c")]
     else:
-        parts = lax.all_gather(up_weight, "fsdp", axis=0, tiled=True)
-        ups = [[parts.reshape(width, 4, width).swapaxes(0, 1)]]
-        parts = lax.all_gather(down_weight, "fsdp", axis=0, tiled=True)
-        downs = [parts.reshape(4, width, width)]
+        found = lax.all_gather(up_weight, "fsdp", axis=0, tiled=True)
+        ups = [Blocks([found.reshape(width, 4, width).swapaxes(0, 1)], "xy")]
+        found = lax.all_gather(down_weight, "fsdp", axis=0, tiled=True)
+        downs = [found.reshape(4, width, width)]
     attn_branch, middle, mod_two, mod_two_across = after_attention(
         place, attn_low, tokens[0], rows, squares
     )
@@ -996,7 +1037,7 @@
         mod_two,
         mod_two_across,
         branch_grad,
-        up_bias_full.reshape(4, width),
+        rows,
         chan_keep.astype(f32).reshape(4, width),
         ups,
         downs,
@@ -1025,71 +1066,78 @@
         sums[i] for i in range(5)
     ]
     if paired:
-        low_grad, up_other, down_other = lax.optimization_barrier((low_grad, up_other, down_other))
+        low_grad, up_other, down_other = barrier((low_grad, up_other, down_other))
         up_go, up_stay = net.first_sum(up_kept, up_other, "x")
         down_go, down_stay = net.first_sum(down_kept, down_other, "y")
-        low_grad, up_go, down_go = lax.optimization_barrier((low_grad, up_go, down_go))
+        low_grad, up_go, down_go = barrier((low_grad, up_go, down_go))
         up_back, down_back = net.partner(up_go, "x"), net.partner(down_go, "y")
     grads = attend_backward(qkv, attn_low, low_grad, lse, head_keep[0])
     if paired:
-        grads, up_back, down_back = lax.optimization_barrier((grads, up_back, down_back))
+        grads, up_back, down_back = barrier((grads, up_back, down_back))
         up_go, up_stay = net.second_sum(up_stay, up_back)
         down_go, down_stay = net.second_sum(down_stay, down_back)
-        grads, up_go, down_go = lax.optimization_barrier((grads, up_go, down_go))
+        grads, up_go, down_go = barrier((grads, up_go, down_go))
         up_back, down_back = net.partner(up_go, "y"), net.partner(down_go, "x")
-    *stores, bias_sums = square_grads(place, mod_across, grads, out_weight_g, columns, splits)
-    query_sum, value_sum = bias_sums[0], bias_sums[2]
+    tokens_grad, sums = tokens_back(place, grads, tokens[0], middle_grad, rows, squares)
     if paired:
-        grads, stores = lax.optimization_barrier((grads, stores))
-        others = [net.partner(sent, "c") for sent in stores[1::2]]
-    tokens_grad, sums = tokens_back(place, grads, tokens[0], middle_grad, rows, squares)
-    shift_attn_grad, scale_attn_grad = sums[0], sums[1]
-    if paired:
-        tokens_grad, up_back, down_back, others = lax.optimization_barrier(
-            (tokens_grad, up_back, down_back, others)
-        )
-        goes, stays = zip(
-            *[net.first_sum(stores[2 * i], others[i], kind) for i, kind in enumerate("yx")]
-        )
-        backs = [net.partner(go, kind) for go, kind in zip(goes, "yx")]
-        up_mine, down_mine = add(up_stay, up_back), add(down_stay, down_back)
-        up_terms, down_terms = net.send_z(up_mine), net.send_z(down_mine)
-        backs, up_terms, down_terms = lax.optimization_barrier((backs, up_terms, down_terms))
-        goes, stays = zip(*[net.second_sum(stay, back) for stay, back in zip(stays, backs)])
-        backs = [net.partner(go, kind) for go, kind in zip(goes, "xy")]
-        part = jnp.stack([add(up_mine[0], *up_terms), add(down_mine[0], *down_terms)])
-        parts = net.to_group(part)
-        up_shard = jnp.concatenate([parts[i, 0] for i in range(4)], axis=1).astype(f32)
-        down_shard = parts[:, 1].reshape(down_weight.shape).astype(f32)
-        mine = [add(stay, back) for stay, back in zip(stays, backs)]
-        terms = [net.send_z(value) for value in mine]
-        part = [add(value[0], *more) for value, more in zip(mine, terms)]
-        parts = net.to_group(jnp.concatenate(part, axis=1)).astype(f32)
-        query_g, key_g, value_g, out_shard = parts
-    else:
-        query_g, key_g, value_g, out_shard = reduce_columns(stores[0])
-    qkv_shard = jnp.concatenate([query_g, key_g, value_g], axis=1)
-
+        sums, up_back, down_back, grads = barrier((sums, up_back, down_back, grads))
     row = jnp.concatenate(
         [
-            shift_attn_grad,
-            scale_attn_grad,
+            sums[0],
+            sums[1],
             gate_attn_grad,
             shift_mlp_grad,
             scale_mlp_grad,
             gate_mlp_grad,
-            query_sum,
-            value_sum,
+            sums[2],
+            sums[4],
             out_bias_g,
             up_bias_g,
             down_bias_g[0],
         ]
     ).astype(bf16)[None]
-    rows = gather_rows(gather_rows(row, "fsdp", shard_count), "dp", group_count)
-    all_facts = gather_rows(facts, "dp", group_count)
+    if paired:
+        up_mine, down_mine = add(up_stay, up_back), add(down_stay, down_back)
+        row, up_mine, down_mine, grads = barrier((row, up_mine, down_mine, grads))
+        up_terms = net.send_z(up_mine)
+        row = net.along_z(row)
+    stores = square_grads(place, mod_across, grads, out_weight_g, columns, splits)
+    if paired:
+        stores, row, up_terms = barrier((stores, row, up_terms))
+        others = [net.partner(sent, "c") for sent in stores[1::2]]
+        row = net.pair(row, "x")
+        others, row = barrier((others, row))
+        goes, stays = zip(
+            *[net.first_sum(stores[2 * i], others[i], kind) for i, kind in enumerate("yx")]
+        )
+        goes, row, down_mine = barrier((goes, row, down_mine))
+        row = net.pair(row, "y")
+        backs = [net.partner(go, kind) for go, kind in zip(goes, "yx")]
+        down_terms = net.send_z(down_mine)
+        backs, down_terms, row = barrier((backs, down_terms, row))
+        goes, stays = zip(*[net.second_sum(stay, back) for stay, back in zip(stays, backs)])
+        goes, row = barrier((goes, row))
+        all_rows = net.pair(row, "c").reshape(image_count, -1)
+        backs = [net.partner(go, kind) for go, kind in zip(goes, "xy")]
+        part = jnp.stack([add(up_mine[0], *up_terms), add(down_mine[0], *down_terms)])
+        backs, part, all_rows = barrier((backs, part, all_rows))
+        mine = jnp.concatenate([add(stay, back) for stay, back in zip(stays, backs)], axis=2)
+        mine, part = barrier((mine, part))
+        terms = net.send_z(mine)
+        mlp_parts = both(part, "dp", group_count, 2, 0)
+        terms, mlp_parts = barrier((terms, mlp_parts))
+        mlp_parts = both(mlp_parts, "dp", group_count, 1, 1).reshape(4, *part.shape)
+        parts = net.to_group(add(mine[0], *terms)).astype(f32)
+        up_shard = jnp.concatenate([mlp_parts[i, 0] for i in range(4)], axis=1).astype(f32)
+        down_shard = mlp_parts[:, 1].reshape(down_weight.shape).astype(f32)
+        query_g, key_g, value_g, out_shard = parts
+    else:
+        query_g, key_g, value_g, out_shard = reduce_columns(stores[0])
+        all_rows = gather_rows(gather_rows(row, "fsdp", shard_count), "dp", group_count)
+    qkv_shard = jnp.concatenate([query_g, key_g, value_g], axis=1)
     cond = conditioning(all_facts[:, 0], all_facts[:, 1], class_table, shard, width)
     cond_act, silu_pull = jax.vjp(jax.nn.silu, cond)
-    ada_grad = rows[:, : 6 * width]
+    ada_grad = all_rows[:, : 6 * width]
     ada_weight_g = jnp.einsum(
         "sd,se->de", cond_act.astype(bf16), ada_grad, preferred_element_type=f32
     )
@@ -1099,7 +1147,7 @@
     table_g = jnp.einsum(
         "sc,sd->cd", picked.astype(f32), cond_grad, precision=lax.Precision.HIGHEST
     )
-    sums = jnp.sum(rows.astype(f32), axis=0)
+    sums = jnp.sum(all_rows.astype(f32), axis=0)
     ada_bias_g = own_part(sums[: 6 * width], shard, ada_bias.shape[0])
     qv_bias_g = own_part(sums[6 * width : 8 * width].reshape(2, width), shard, columns)
     out_bias_g = own_part(sums[8 * width : 9 * width], shard, columns)

time: 718 us -> 655 us (0.912)
  waiting for transfers between devices: 218 us -> 153 us
  starting transfers between devices: 104 us -> 73.3 us
  other arithmetic: 53.7 us -> 69.3 us
  between operations: 3.45 us -> 16.7 us
    ppermute x24 -> x21, waiting for transfers between devices: 126 us -> 95.3 us  [ahead(): return lax.ppermute(value, 'fsdp', pairs)]
    ppermute x10 -> x0, waiting for transfers between devices: 25.5 us -> none  [gather_rows(): other = lax.ppermute(rows, axis, [(i, i ^ step) for i in range(size)])]
    ppermute x40 -> x36, waiting for transfers between devices: 66.1 us -> 45.4 us  [swap(): return lax.ppermute(value, axis, [(i, i ^ step) for i in range(size)])]
    ppermute x40 -> x36, starting transfers between devices: 48.7 us -> 35.4 us  [swap(): return lax.ppermute(value, axis, [(i, i ^ step) for i in range(size)])]
    ppermute x10 -> x0, starting transfers between devices: 10.5 us -> none  [gather_rows(): other = lax.ppermute(rows, axis, [(i, i ^ step) for i in range(size)])]
    another operation x5 -> x12, other arithmetic: 2.28 us -> 12.7 us  [the longest x2 6.59 us: body(): up, up_y = (jnp.stack([up, up_x]), jnp.stack([up_y, up_xy]))]
    ppermute x24 -> x21, starting transfers between devices: 40 us -> 31.7 us  [ahead(): return lax.ppermute(value, 'fsdp', pairs)]
    all_gather x0 -> x1, waiting for transfers between devices: none -> 7.75 us  [body(): down = lax.all_gather(after(down_mine, first_y), 'fsdp', axis=0)]
  transfers between devices with their start and end apart: 75 -> 59, of which waited for: 24 -> 24; matrix products, arithmetic and copies ran while one was open for 7% -> 9% of each run, Pallas kernels for 22% -> 31%
where the time goes in v3:
time: 655 us; the launch traced here: 645 us
  Pallas kernels  300 us (46%)
  waiting for transfers between devices  153 us (23%)
  starting transfers between devices  73.3 us (11%)
  other arithmetic  69.3 us (11%)
  local copies, waits for them, and re-layouts  24.9 us (4%)
  between operations  16.7 us (3%)
  matrix products  7.53 us (1%)
    pallas_call x1, Pallas kernels, mlp(): pl.pallas_call(functools.partial(mlp_kernel, ups=ups, downs=len(downs)),...  99.6 us
    ppermute x21, waiting for transfers between devices, ahead(): return lax.ppermute(value, 'fsdp', pairs)  95.3 us
    pallas_call x1, Pallas kernels, attend_backward(): pl.pallas_call(functools.partial(attend_backward_kernel, head_size=width...  57.7 us
    ppermute x36, waiting for transfers between devices, swap(): return lax.ppermute(value, axis, [(i, i ^ step) for i in range(size)])  45.4 us
    pallas_call x1, Pallas kernels, attend_forward(): pl.pallas_call(functools.partial(attend_forward_kernel, head_size=width /...  37.4 us
    ppermute x36, starting transfers between devices, swap(): return lax.ppermute(value, axis, [(i, i ^ step) for i in range(size)])  35.4 us
    convert_element_type x12, other arithmetic, add(): sum((term.astype(jnp.float32) for term in terms)).astype(jnp.bfloat16)  32.6 us
    ppermute x21, starting transfers between devices, ahead(): return lax.ppermute(value, 'fsdp', pairs)  31.7 us
  transfers between devices with their start and end apart: 59, of which 24 were waited for; matrix products, arithmetic and copies ran while one was open for 9% of the time, Pallas kernels for 31%

profile of v3, /device:TPU:1, one launch (start us, length us, event | category | flops | bytes accessed | tf_op | source)
XLA Modules:
  0.0 644.8 jit_solution(8142290457174415455)
XLA Ops:
  32.3 20.3 %collective-permute-done.4 = bf16[144,1152]{1,0:T(8,128)(2,1)S(1)} collective-permute-done((bf16[144,1152]{1,0:T(8,128)(2,1)S(1)}, bf16[144,1152]{1,0:T(8,128)(2,1)S(1)}, u32[]{:S(2)}, u32[]{:S(2)}) %collective-permute-start.4) | collective-permute-done | bytes 331808 | tf_op jit(solution)/shard_map/ppermute | solution.py:864
  57.4 6.2 all-to-all-start
  71.8 4.9 all-to-all-done
  88.7 23.0 %collective-permute-done.12 = bf16[144,1152]{1,0:T(8,128)(2,1)S(1)} collective-permute-done((bf16[144,1152]{1,0:T(8,128)(2,1)}, bf16[144,1152]{1,0:T(8,128)(2,1)S(1)}, u32[]{:S(2)}, u32[]{:S(2)}) %collective-permute-start.12) | collective-permute-done | bytes 331808 | tf_op jit(solution)/shard_map/ppermute | solution.py:864
  122.0 7.2 %prepare.1 = (bf16[1024,1152]{1,0:T(8,128)(2,1)}, bf16[1152,1024]{1,0:T(8,128)(2,1)}, bf16[1024,1152]{1,0:T(8,128)(2,1)}, f32[8,1152]{1,0:T(8,128)}, f32[16,1152]{1,0:T(8,128)}) custom-call(bf16[1024,1152]{1,0:T(8,128)(2,1)} %bitcast.209, bf16[1024,1152]{1,0:T(8,128)(2,1)} %bitcast.215, f32[8,16128]{1,0:T(8,128)} %bitcast.220), custom_call_target="tpu_custom_call" | custom-call | flops 1 | bytes 1 | tf_op jit(solution)/shard_map/prepare/pallas_call | solution.py:333
  130.9 19.9 %project.1.query_ref.key_ref.value_ref = bf16[4,1024,1152]{2,1,0:T(8,128)(2,1)} custom-call(s32[3]{0:T(128)} %pad_add_fusion.3.place, bf16[1024,1152]{1,0:T(8,128)(2,1)} %get-tuple-element.123.mod_ref, f32[16,1152]{1,0:T(8,128)} %get-tuple-element.124.rows_ref, bf16[2,4,144,512]{3,2,1,0:T(8,128)(2,1)} %pad_maximum_fusion.9.rest_0_, ...), custom_call_target="tpu_custom_call" | custom-call | flops 1 | bytes 1 | tf_op jit(solution)/shard_map/project/pallas_call | solution.py:383
  150.8 5.4 collective-permute-done.18
  157.5 37.4 %attend_forward.1 = (bf16[1024,1152]{1,0:T(8,128)(2,1)S(1)}, f32[16,1024]{1,0:T(8,128)S(1)}) custom-call(s32[16]{0:T(128)S(1)} %bitcast.208, bf16[4,1024,1152]{2,1,0:T(8,128)(2,1)} %project.1.query_ref.key_ref.value_ref, bf16[4,1024,1152]{2,1,0:T(8,128)(2,1)} %project.1.query_ref.key_ref.value_ref, bf16[4,1024,1152]{2,1,0:T(8,128)(2,1)} %project.1.query_ref.key_ref.value_ref), custom_call_target="tpu_custom_call" | custom-call | flops 17179869184 | bytes 9437184 | tf_op jit(solution)/shard_map/attend_forward/pallas_call | solution.py:133
  196.9 7.7 %all-gather.3.cloned.1.call-done = bf16[16,144,1152]{2,1,0:T(8,128)(2,1)} async-done(((bf16[2,144,1152]{2,1,0:T(8,128)(2,1)}), bf16[16,144,1152]{2,1,0:T(8,128)(2,1)}) %all-gather.3.cloned.1.call-update) | async-done | bytes 5308432 | tf_op jit(solution)/shard_map/all_gather | solution.py:1004
  213.9 11.7 %after_attention.1 = (f32[1024,1152]{1,0:T(8,128)}, f32[1024,1152]{1,0:T(8,128)}, bf16[1024,1152]{1,0:T(8,128)(2,1)}, bf16[1152,1024]{1,0:T(8,128)(2,1)}) custom-call(s32[3]{0:T(128)} %pad_add_fusion.3.place, bf16[1024,1152]{1,0:T(8,128)(2,1)} %copy-done.1, bf16[1024,1152]{1,0:T(8,128)(2,1)} %bitcast.210, f32[16,1152]{1,0:T(8,128)} %get-tuple-element.124.rows_ref, ...), custom_call_target="tpu_custom_call" | custom-call | flops 1 | bytes 1 | tf_op jit(solution)/shard_map/after_attention/pallas_call | solution.py:443
  225.6 99.6 %mlp.1 = (f32[1024,1152]{1,0:T(8,128)}, f32[1024,1152]{1,0:T(8,128)}, f32[4,1152]{1,0:T(4,128)}, bf16[2,2,4,144,1152]{4,3,2,1,0:T(8,128)(2,1)}, bf16[2,2,4,144,1...) custom-call(s32[3]{0:T(128)} %pad_add_fusion.3.place, ...), custom_call_target="tpu_custom_call" | custom-call | flops 1 | bytes 1 | tf_op jit(solution)/shard_map/mlp/pallas_call | solution.py:557
  325.8 23.2 %after_mlp.1 = (bf16[1024,1152]{1,0:T(8,128)(2,1)}, f32[1024,1152]{1,0:T(8,128)}, bf16[1024,1152]{1,0:T(8,128)(2,1)}, f32[8,1152]{1,0:T(8,128)}, bf16[2,4,144,1152]{3,2,1,0:T(8,128)(2,1)}) custom-call(s32[3]{0:T(128)} %pad_add_fusion.3.place, f32[1024,1152]{1,0:T(8,128)} %get-tuple-element.145.mlp_ref, f32[1024,1152]{1,0:T(8,128)} %get-tuple-element.146.dmod_ref, ...), custom_call_target="tpu_custom_call" | custom-call | flops 1 | bytes 1 | tf_op jit(solution)/shard_map/after_mlp/pallas_call | solution.py:647
  351.3 4.8 fusion.1
  361.7 57.7 %attend_backward.1.grads_ref = bf16[3,1024,1152]{2,1,0:T(8,128)(2,1)} custom-call(s32[16]{0:T(128)} %bitcast.207, bf16[4,1024,1152]{2,1,0:T(8,128)(2,1)} %project.1.query_ref.key_ref.value_ref, bf16[4,1024,1152]{2,1,0:T(8,128)(2,1)} %project.1.query_ref.key_ref.value_ref, bf16[4,1024,1152]{2,1,0:T(8,128)(2,1)} %project.1.query_ref.key_ref.value_ref, ...), custom_call_target="tpu_custom_call" | custom-call | flops 42949672960 | bytes 18874368 | tf_op jit(solution)/shard_map/attend_backward/pallas_call | solution.py:160
  419.7 5.5 fusion.4
  427.9 25.9 %tokens_back.1 = (bf16[1024,1152]{1,0:T(8,128)(2,1)}, f32[8,1152]{1,0:T(8,128)}) custom-call(s32[3]{0:T(128)} %pad_add_fusion.3.place, bf16[3,1024,1152]{2,1,0:T(8,128)(2,1)} %attend_backward.1.grads_ref, bf16[1024,1152]{1,0:T(8,128)(2,1)} %bitcast.211, f32[1024,1152]{1,0:T(8,128)} %get-tuple-element.166.dmiddle_ref, ...), custom_call_target="tpu_custom_call" | custom-call | flops 1 | bytes 1 | tf_op jit(solution)/shard_map/tokens_back/pallas_call | solution.py:785
  467.3 17.2 %square_grads.1 = (bf16[2,2,4,144,512]{4,3,2,1,0:T(8,128)(2,1)}, bf16[2,2,4,144,512]{4,3,2,1,0:T(8,128)(2,1)}, bf16[2,2,4,144,640]{4,3,2,1,0:T(8,128)(2,1)}, bf16[2,2,4,144,640]{4,3,2,1,0:T(8,128)(2,1)}) custom-call(s32[3]{0:T(128)} %pad_add_fusion.3.place, bf16[1152,1024]{1,0:T(8,128)(2,1)} %get-tuple-element.168.across_ref, ...), custom_call_target="tpu_custom_call" | custom-call | flops 1 | bytes 1 | tf_op jit(solution)/shard_map/square_grads/pallas_call | solution.py:719
  487.3 15.1 %collective-permute-done.34 = bf16[144,1152]{1,0:T(8,128)(2,1)} collective-permute-done((bf16[144,1152]{1,0:T(8,128)(2,1)S(1)}, bf16[144,1152]{1,0:T(8,128)(2,1)}, u32[]{:S(2)}, u32[]{:S(2)}) %collective-permute-start.34) | collective-permute-done | bytes 331808 | tf_op jit(solution)/shard_map/ppermute | solution.py:864
  503.2 4.8 collective-permute-done.56
  535.1 15.8 %collective-permute-done.42 = bf16[144,1152]{1,0:T(8,128)(2,1)S(1)} collective-permute-done((bf16[144,1152]{1,0:T(8,128)(2,1)S(1)}, bf16[144,1152]{1,0:T(8,128)(2,1)S(1)}, u32[]{:S(2)}, u32[]{:S(2)}) %collective-permute-start.42) | collective-permute-done | bytes 331808 | tf_op jit(solution)/shard_map/ppermute | solution.py:864
  568.3 9.9 %collective-permute-done.45 = bf16[4,144,512]{2,1,0:T(8,128)(2,1)} collective-permute-done((bf16[4,144,512]{2,1,0:T(8,128)(2,1)}, bf16[4,144,512]{2,1,0:T(8,128)(2,1)}, u32[]{:S(2)}, u32[]{:S(2)}) %collective-permute-start.45) | collective-permute-done | bytes 589856 | tf_op jit(solution)/shard_map/ppermute | solution.py:832
  592.0 8.9 %collective-permute-done.51 = bf16[2,144,1152]{2,1,0:T(8,128)(2,1)S(1)} collective-permute-done((bf16[2,144,1152]{2,1,0:T(8,128)(2,1)S(1)}, bf16[2,144,1152]{2,1,0:T(8,128)(2,1)S(1)}, u32[]{:S(2)}, u32[]{:S(2)}) %collective-permute-start.51) | collective-permute-done | bytes 663584 | tf_op jit(solution)/shard_map/ppermute | solution.py:832
  602.2 11.3 %collective-permute-done.49 = bf16[144,1152]{1,0:T(8,128)(2,1)S(1)} collective-permute-done((bf16[144,1152]{1,0:T(8,128)(2,1)S(1)}, bf16[144,1152]{1,0:T(8,128)(2,1)S(1)}, u32[]{:S(2)}, u32[]{:S(2)}) %collective-permute-start.49) | collective-permute-done | bytes 331808 | tf_op jit(solution)/shard_map/ppermute | solution.py:864
  617.7 4.9 collective-permute-done.52
  (284 shorter events, 179.8 us)
Async XLA Ops:
  24.6 28.0 %collective-permute-start.4 = (bf16[144,1152]{1,0:T(8,128)(2,1)S(1)}, bf16[144,1152]{1,0:T(8,128)(2,1)S(1)}, u32[]{:S(2)}, u32[]{:S(2)}) collective-permute-start(bf16[144,1152]{1,0:T(8,128)(2,1)S(1)} %fusion.28), channel_id=1, source_target_pairs={{16,0},{20,4},{24,8},{28,12},{0,16},{4,20},{8,24},{12,28},{17,1},{... | collective-permute-start | bytes 995336 | tf_op jit(solution)/shard_map/ppermute | solution.py:864
  25.3 27.4 %collective-permute-start.5 = (bf16[144,1152]{1,0:T(8,128)(2,1)S(1)}, bf16[144,1152]{1,0:T(8,128)(2,1)S(1)}, u32[]{:S(2)}, u32[]{:S(2)}) collective-permute-start(bf16[144,1152]{1,0:T(8,128)(2,1)S(1)} %fusion.28), channel_id=1, source_target_pairs={{24,0},{28,4},{0,8},{4,12},{8,16},{12,20},{16,24},{20,28},{25,1},{... | collective-permute-start | bytes 995336 | tf_op jit(solution)/shard_map/ppermute | solution.py:864
  63.5 141.1 %all-gather.3.cloned.1.call-start = ((), (), s32[]{:S(2)}) async-start(), calls=%async_computation.1 | async-start | bytes 5971968 | tf_op jit(solution)/shard_map/all_gather | solution.py:1004
  78.6 35.3 %collective-permute-start.10 = (bf16[2,4,144,640]{3,2,1,0:T(8,128)(2,1)S(1)}, bf16[2,4,144,640]{3,2,1,0:T(8,128)(2,1)}, u32[]{:S(2)}, u32[]{:S(2)}) collective-permute-start(bf16[2,4,144,640]{3,2,1,0:T(8,128)(2,1)S(1)} %pad_maximum_fusion.4.rest_4_), channel_id=1, source_target_pairs={{0,4},{4,0},{8,12},{12,8},{16,20},{20,16},{24,28},{28,24},{1,5},{5... | collective-permute-start | bytes 4423688 | tf_op jit(solution)/shard_map/ppermute | solution.py:832
  80.4 33.6 %collective-permute-start.9 = (bf16[2,4,144,512]{3,2,1,0:T(8,128)(2,1)}, bf16[2,4,144,512]{3,2,1,0:T(8,128)(2,1)}, u32[]{:S(2)}, u32[]{:S(2)}) collective-permute-start(bf16[2,4,144,512]{3,2,1,0:T(8,128)(2,1)} %pad_maximum_fusion.9.rest_0_), channel_id=1, source_target_pairs={{0,2},{1,3},{2,0},{3,1},{4,6},{5,7},{6,4},{7,5},{8,10},{9,11},{10,... | collective-permute-start | bytes 3538952 | tf_op jit(solution)/shard_map/ppermute | solution.py:832
  82.5 29.1 %collective-permute-start.12 = (bf16[144,1152]{1,0:T(8,128)(2,1)}, bf16[144,1152]{1,0:T(8,128)(2,1)S(1)}, u32[]{:S(2)}, u32[]{:S(2)}) collective-permute-start(bf16[144,1152]{1,0:T(8,128)(2,1)} %constant_dynamic-slice_fusion.1), channel_id=1, source_target_pairs={{16,0},{20,4},{24,8},{28,12},{0,16},{4,20},{8,24},{12,28},{17,1},{... | collective-permute-start | bytes 995336 | tf_op jit(solution)/shard_map/ppermute | solution.py:864
  85.0 26.7 %collective-permute-start.13 = (bf16[144,1152]{1,0:T(8,128)(2,1)}, bf16[144,1152]{1,0:T(8,128)(2,1)S(1)}, u32[]{:S(2)}, u32[]{:S(2)}) collective-permute-start(bf16[144,1152]{1,0:T(8,128)(2,1)} %constant_dynamic-slice_fusion.1), channel_id=1, source_target_pairs={{24,0},{28,4},{0,8},{4,12},{8,16},{12,20},{16,24},{20,28},{25,1},{... | collective-permute-start | bytes 995336 | tf_op jit(solution)/shard_map/ppermute | solution.py:864
  118.1 38.1 %collective-permute-start.18 = (bf16[4,144,1152]{2,1,0:T(8,128)(2,1)}, bf16[4,144,1152]{2,1,0:T(8,128)(2,1)}, u32[]{:S(2)}, u32[]{:S(2)}) collective-permute-start(bf16[4,144,1152]{2,1,0:T(8,128)(2,1)} %pad_maximum_fusion.6), channel_id=1, source_target_pairs={{0,4},{4,0},{8,12},{12,8},{16,20},{20,16},{24,28},{28,24},{1,5},{5... | collective-permute-start | bytes 3981320 | tf_op jit(solution)/shard_map/ppermute | solution.py:832
  119.0 37.2 %collective-permute-start.19 = (bf16[4,144,1152]{2,1,0:T(8,128)(2,1)}, bf16[4,144,1152]{2,1,0:T(8,128)(2,1)}, u32[]{:S(2)}, u32[]{:S(2)}) collective-permute-start(bf16[4,144,1152]{2,1,0:T(8,128)(2,1)} %pad_maximum_fusion.6), channel_id=1, source_target_pairs={{0,2},{1,3},{2,0},{3,1},{4,6},{5,7},{6,4},{7,5},{8,10},{9,11},{10,... | collective-permute-start | bytes 3981320 | tf_op jit(solution)/shard_map/ppermute | solution.py:832
  156.2 40.7 %collective-permute-start.20 = (bf16[4,144,1152]{2,1,0:T(8,128)(2,1)}, bf16[4,144,1152]{2,1,0:T(8,128)(2,1)}, u32[]{:S(2)}, u32[]{:S(2)}) collective-permute-start(bf16[4,144,1152]{2,1,0:T(8,128)(2,1)} %collective-permute-done.18), channel_id=1, source_target_pairs={{0,2},{1,3},{2,0},{3,1},{4,6},{5,7},{6,4},{7,5},{8,10},{9,11},{10,... | collective-permute-start | bytes 3981320 | tf_op jit(solution)/shard_map/ppermute | solution.py:832
  325.2 23.8 %collective-permute-start.24 = (bf16[2,2,4,144,1152]{4,3,2,1,0:T(8,128)(2,1)}, bf16[2,2,4,144,1152]{4,3,2,1,0:T(8,128)(2,1)S(1)}, u32[]{:S(2)}, u32[]{:S(2)}) collective-permute-start(bf16[2,2,4,144,1152]{4,3,2,1,0:T(8,128)(2,1)} %get-tuple-element.151), channel_id=1, source_target_pairs={{0,1},{1,0},{2,3},{3,2},{4,5},{5,4},{6,7},{7,6},{8,9},{9,8},{10,11... | collective-permute-start | bytes 15925256 | tf_op jit(solution)/shard_map/ppermute | solution.py:832
  325.4 23.7 %collective-permute-start.25 = (bf16[2,2,4,144,1152]{4,3,2,1,0:T(8,128)(2,1)}, bf16[2,2,4,144,1152]{4,3,2,1,0:T(8,128)(2,1)}, u32[]{:S(2)}, u32[]{:S(2)}) collective-permute-start(bf16[2,2,4,144,1152]{4,3,2,1,0:T(8,128)(2,1)} %get-tuple-element.152), channel_id=1, source_target_pairs={{0,1},{1,0},{2,3},{3,2},{4,5},{5,4},{6,7},{7,6},{8,9},{9,8},{10,11... | collective-permute-start | bytes 15925256 | tf_op jit(solution)/shard_map/ppermute | solution.py:832
  360.2 59.5 %collective-permute-start.26 = (bf16[2,4,144,1152]{3,2,1,0:T(8,128)(2,1)}, bf16[2,4,144,1152]{3,2,1,0:T(8,128)(2,1)}, u32[]{:S(2)}, u32[]{:S(2)}) collective-permute-start(bf16[2,4,144,1152]{3,2,1,0:T(8,128)(2,1)} %fusion), channel_id=1, source_target_pairs={{0,4},{4,0},{8,12},{12,8},{16,20},{20,16},{24,28},{28,24},{1,5},{5... | collective-permute-start | bytes 7962632 | tf_op jit(solution)/shard_map/ppermute | solution.py:832
  360.5 59.2 %collective-permute-start.27 = (bf16[2,4,144,1152]{3,2,1,0:T(8,128)(2,1)}, bf16[2,4,144,1152]{3,2,1,0:T(8,128)(2,1)}, u32[]{:S(2)}, u32[]{:S(2)}) collective-permute-start(bf16[2,4,144,1152]{3,2,1,0:T(8,128)(2,1)} %fusion.1), channel_id=1, source_target_pairs={{0,2},{1,3},{2,0},{3,1},{4,6},{5,7},{6,4},{7,5},{8,10},{9,11},{10,... | collective-permute-start | bytes 7962632 | tf_op jit(solution)/shard_map/ppermute | solution.py:832
  425.2 29.8 %collective-permute-start.28 = (bf16[4,144,1152]{2,1,0:T(8,128)(2,1)}, bf16[4,144,1152]{2,1,0:T(8,128)(2,1)S(1)}, u32[]{:S(2)}, u32[]{:S(2)}) collective-permute-start(bf16[4,144,1152]{2,1,0:T(8,128)(2,1)} %get-tuple-element.170), channel_id=1, source_target_pairs={{0,2},{1,3},{2,0},{3,1},{4,6},{5,7},{6,4},{7,5},{8,10},{9,11},{10,... | collective-permute-start | bytes 3981320 | tf_op jit(solution)/shard_map/ppermute | solution.py:832
  426.4 29.5 %collective-permute-start.29 = (bf16[4,144,1152]{2,1,0:T(8,128)(2,1)}, bf16[4,144,1152]{2,1,0:T(8,128)(2,1)}, u32[]{:S(2)}, u32[]{:S(2)}) collective-permute-start(bf16[4,144,1152]{2,1,0:T(8,128)(2,1)} %get-tuple-element.171), channel_id=1, source_target_pairs={{0,4},{4,0},{8,12},{12,8},{16,20},{20,16},{24,28},{28,24},{1,5},{5... | collective-permute-start | bytes 3981320 | tf_op jit(solution)/shard_map/ppermute | solution.py:832
  427.5 75.5 %collective-permute-start.55 = (s32[2,4,2]{1,2,0:T(2,128)S(1)}, s32[2,4,2]{1,2,0:T(2,128)S(1)}, u32[]{:S(2)}, u32[]{:S(2)}) collective-permute-start(s32[2,4,2]{1,2,0:T(2,128)S(1)} %bitcast.241), channel_id=1, source_target_pairs={{0,2},{1,3},{2,0},{3,1},{4,6},{5,7},{6,4},{7,5},{8,10},{9,11},{10,... | collective-permute-start | bytes 200 | tf_op jit(solution)/shard_map/ppermute | solution.py:832
  464.6 22.4 %collective-permute-start.32 = (bf16[1,16128]{1,0:T(2,128)(2,1)S(1)}, bf16[1,16128]{1,0:T(2,128)(2,1)S(1)}, u32[]{:S(2)}, u32[]{:S(2)}) collective-permute-start(bf16[1,16128]{1,0:T(2,128)(2,1)S(1)} %constant_dynamic-update-slice_fusion.1), channel_id=1, source_target_pairs={{24,0},{28,4},{0,8},{4,12},{8,16},{12,20},{16,24},{20,28},{25,1},{... | collective-permute-start | bytes 96776 | tf_op jit(solution)/shard_map/ppermute | solution.py:864
  521.2 33.1 %collective-permute-start.40 = (bf16[2,4,144,640]{3,2,1,0:T(8,128)(2,1)S(1)}, bf16[2,4,144,640]{3,2,1,0:T(8,128)(2,1)S(1)}, u32[]{:S(2)}, u32[]{:S(2)}) collective-permute-start(bf16[2,4,144,640]{3,2,1,0:T(8,128)(2,1)S(1)} %fusion.6), channel_id=1, source_target_pairs={{0,4},{4,0},{8,12},{12,8},{16,20},{20,16},{24,28},{28,24},{1,5},{5... | collective-permute-start | bytes 4423688 | tf_op jit(solution)/shard_map/ppermute | solution.py:832
  526.8 24.2 %collective-permute-start.42 = (bf16[144,1152]{1,0:T(8,128)(2,1)S(1)}, bf16[144,1152]{1,0:T(8,128)(2,1)S(1)}, u32[]{:S(2)}, u32[]{:S(2)}) collective-permute-start(bf16[144,1152]{1,0:T(8,128)(2,1)S(1)} %get-tuple-element.241), channel_id=1, source_target_pairs={{16,0},{20,4},{24,8},{28,12},{0,16},{4,20},{8,24},{12,28},{17,1},{... | collective-permute-start | bytes 995336 | tf_op jit(solution)/shard_map/ppermute | solution.py:864
  528.7 22.2 %collective-permute-start.43 = (bf16[144,1152]{1,0:T(8,128)(2,1)S(1)}, bf16[144,1152]{1,0:T(8,128)(2,1)S(1)}, u32[]{:S(2)}, u32[]{:S(2)}) collective-permute-start(bf16[144,1152]{1,0:T(8,128)(2,1)S(1)} %get-tuple-element.240), channel_id=1, source_target_pairs={{8,0},{12,4},{16,8},{20,12},{24,16},{28,20},{0,24},{4,28},{9,1},{1... | collective-permute-start | bytes 995336 | tf_op jit(solution)/shard_map/ppermute | solution.py:864
  528.9 25.4 %collective-permute-start.39 = (bf16[2,4,144,512]{3,2,1,0:T(8,128)(2,1)S(1)}, bf16[2,4,144,512]{3,2,1,0:T(8,128)(2,1)S(1)}, u32[]{:S(2)}, u32[]{:S(2)}) collective-permute-start(bf16[2,4,144,512]{3,2,1,0:T(8,128)(2,1)S(1)} %fusion.9), channel_id=1, source_target_pairs={{0,2},{1,3},{2,0},{3,1},{4,6},{5,7},{6,4},{7,5},{8,10},{9,11},{10,... | collective-permute-start | bytes 3538952 | tf_op jit(solution)/shard_map/ppermute | solution.py:832
  589.3 24.2 %collective-permute-start.49 = (bf16[144,1152]{1,0:T(8,128)(2,1)S(1)}, bf16[144,1152]{1,0:T(8,128)(2,1)S(1)}, u32[]{:S(2)}, u32[]{:S(2)}) collective-permute-start(bf16[144,1152]{1,0:T(8,128)(2,1)S(1)} %get-tuple-element.238), channel_id=1, source_target_pairs={{16,0},{20,4},{24,8},{28,12},{0,16},{4,20},{8,24},{12,28},{17,1},{... | collective-permute-start | bytes 995336 | tf_op jit(solution)/shard_map/ppermute | solution.py:864
  591.2 22.2 %collective-permute-start.50 = (bf16[144,1152]{1,0:T(8,128)(2,1)S(1)}, bf16[144,1152]{1,0:T(8,128)(2,1)S(1)}, u32[]{:S(2)}, u32[]{:S(2)}) collective-permute-start(bf16[144,1152]{1,0:T(8,128)(2,1)S(1)} %get-tuple-element.237), channel_id=1, source_target_pairs={{8,0},{12,4},{16,8},{20,12},{24,16},{28,20},{0,24},{4,28},{9,1},{1... | collective-permute-start | bytes 995336 | tf_op jit(solution)/shard_map/ppermute | solution.py:864
  (62 other events, 749.4 us)
Sparse Core Ops, SparseCore 0:
  114.1 90.5 all-gather.2

commit v4 on v3

--- a/solution.py
+++ b/solution.py
@@ -505,7 +505,7 @@
     bias = rows_ref[pl.ds(UP_BIAS + chunk, 1)]
     keep = keep_ref[pl.ds(chunk, 1)]
     total = jnp.zeros_like(bias)
-    for tile in tiles(length):
+    for tile in tiles(length, 512):
         gelu, slope = gelu_and_slope(matmul(mod_ref[tile], up[slot], ROWS_NN) + bias)
         act[tile] = (gelu * keep).astype(jnp.bfloat16)
         back = matmul(grad_ref[tile], down[slot], ROWS_NT)
@@ -590,88 +590,89 @@
 
 
 def after_mlp_kernel(
-    place, mlp_ref, dmod_ref, middle_ref, branch_ref, cotangent_ref, low_ref, rows_ref, *rest, sets
+    place, dmod_ref, middle_ref, cotangent_ref, rows_ref, *rest, sets
 ):
-    *refs, out_ref, dmiddle_ref, dlow_ref, sums_ref, dweight_ref, weight, dbranch, staged, sems = rest
-    step = pl.program_id(0)
-    tile = out_ref.shape[0]
-
-    @pl.when(step == 0)
-    def _():
-        fetch_part(place, in_sets(refs, sets), 3, weight, sems.at[0])
+    *refs, dmiddle_ref, dbranch_ref, dlow_ref, sums_ref, weight, sem = rest
+
+    @pl.when(pl.program_id(0) == 0)
+    def _():
+        fetch_part(place, in_sets(refs, sets), 3, weight, sem)
         sums_ref[...] = jnp.zeros_like(sums_ref)
 
-    middle = middle_ref[...]
-    grad = cotangent_ref[...].astype(jnp.float32)
-    mlp_branch = mlp_ref[...] + row_of(rows_ref, DOWN_BIAS)
-    out_ref[...] = (middle + row_of(rows_ref, GATE_MLP) * mlp_branch).astype(jnp.bfloat16)
-    normed, inverse = norm_forward(middle)
+    normed, inverse = norm_forward(middle_ref[...])
     dmod = dmod_ref[...]
-    dmiddle = grad + norm_backward(dmod * (1.0 + row_of(rows_ref, SCALE_MLP)), normed, inverse)
+    dmiddle = cotangent_ref[...].astype(jnp.float32) + norm_backward(
+        dmod * (1.0 + row_of(rows_ref, SCALE_MLP)), normed, inverse
+    )
     dmiddle_ref[...] = dmiddle
     low = (dmiddle * row_of(rows_ref, GATE_ATTN)).astype(jnp.bfloat16)
-    dbranch[pl.ds(pl.multiple_of(step * tile, tile), tile)] = low
+    dbranch_ref[...] = low
     dlow_ref[...] = matmul(low, weight[...], ROWS_NT).astype(jnp.bfloat16)
-
-    def add(index, values):
-        sums_ref[index : index + 1] += jnp.sum(values, axis=0, keepdims=True)
-
-    add(0, grad * mlp_branch)
-    add(1, dmod * normed)
-    add(2, dmod)
-    add(3, dmiddle * branch_ref[...])
-    add(4, low.astype(jnp.float32))
-
-    @pl.when(step == pl.num_programs(0) - 1)
-    def _():
-        staged[...] = matmul(low_ref[...], dbranch[...], ROWS_TN).astype(jnp.bfloat16)
-        if len(dweight_ref.shape) == 2:
-            copies = [pltpu.make_async_copy(staged, dweight_ref, sems.at[1])]
-        else:
-            rows = dweight_ref.shape[2]
-            copies = []
-            for shard in range(8):
-                x_r, z_r = (place[1] + shard % 2) % 2, (shard // 2 + 4 - place[0]) % 4
-                block = staged.at[pl.ds(shard * rows, rows)]
-                copies.append(pltpu.make_async_copy(block, dweight_ref.at[x_r, z_r], sems.at[1]))
-        start_all(copies)
-        wait_all(copies)
-
-
-def after_mlp(place, branch_mlp, dmod, middle, branch, cotangent, low, rows, squares, block_rows, tile=256):
-    length, width = low.shape
+    sums_ref[0:1] += jnp.sum(dmod * normed, axis=0, keepdims=True)
+    sums_ref[1:2] += jnp.sum(dmod, axis=0, keepdims=True)
+    sums_ref[2:3] += jnp.sum(low.astype(jnp.float32), axis=0, keepdims=True)
+
+
+def after_mlp(place, dmod, middle, cotangent, rows, squares, tile=256):
+    length, width = middle.shape
     tile = min(tile, length)
     by_rows = pl.BlockSpec((tile, width), lambda step, place: (step, 0))
     fixed = lambda shape: pl.BlockSpec(shape, lambda step, place: (0, 0))
-    wgrad = (2, 4, block_rows, width) if len(squares[0]) > 1 else (width, width)
     return pl.pallas_call(
         functools.partial(after_mlp_kernel, sets=squares),
         grid_spec=pltpu.PrefetchScalarGridSpec(
             num_scalar_prefetch=1,
             grid=(length // tile,),
-            in_specs=[by_rows] * 5 + [fixed((length, width)), fixed(rows.shape)] + [ANY] * len(flat(squares)),
-            out_specs=[by_rows] * 3 + [fixed((8, width)), ANY],
-            scratch_shapes=[
-                pltpu.VMEM((width, width), jnp.bfloat16),
-                pltpu.VMEM((length, width), jnp.bfloat16),
-                pltpu.VMEM((width, width), jnp.bfloat16),
-                pltpu.SemaphoreType.DMA((2,)),
-            ],
+            in_specs=[by_rows] * 3 + [fixed(rows.shape)] + [ANY] * len(flat(squares)),
+            out_specs=[by_rows] * 3 + [fixed((8, width))],
+            scratch_shapes=[pltpu.VMEM((width, width), jnp.bfloat16), pltpu.SemaphoreType.DMA],
         ),
         out_shape=[
-            jax.ShapeDtypeStruct((length, width), jnp.bfloat16),
             jax.ShapeDtypeStruct((length, width), jnp.float32),
             jax.ShapeDtypeStruct((length, width), jnp.bfloat16),
+            jax.ShapeDtypeStruct((length, width), jnp.bfloat16),
             jax.ShapeDtypeStruct((8, width), jnp.float32),
-            jax.ShapeDtypeStruct(wgrad, jnp.bfloat16),
         ],
         compiler_params=vmem_params(),
-        cost_estimate=cost(4 * length * width * width, 30 * length * width),
+        cost_estimate=cost(2 * length * width * width, 20 * length * width),
         name="after_mlp",
-    )(place, branch_mlp, dmod, middle, branch, cotangent, low, rows, *flat(squares))
-
-
-def square_grads_kernel(place, across_ref, grads_ref, out_grad_ref, *rest):
+    )(place, dmod, middle, cotangent, rows, *flat(squares))
+
+
+def finish_kernel(
+    mlp_ref, middle_ref, branch_ref, dmiddle_ref, cotangent_ref, rows_ref, out_ref, sums_ref
+):
+    @pl.when(pl.program_id(0) == 0)
+    def _():
+        sums_ref[...] = jnp.zeros_like(sums_ref)
+
+    mlp_branch = mlp_ref[...] + row_of(rows_ref, DOWN_BIAS)
+    out_ref[...] = (middle_ref[...] + row_of(rows_ref, GATE_MLP) * mlp_branch).astype(jnp.bfloat16)
+    grad = cotangent_ref[...].astype(jnp.float32) * mlp_branch
+    sums_ref[0:1] += jnp.sum(grad, axis=0, keepdims=True)
+    sums_ref[1:2] += jnp.sum(dmiddle_ref[...] * branch_ref[...], axis=0, keepdims=True)
+
+
+def finish(branch_mlp, middle, branch, dmiddle, cotangent, rows, tile=256):
+    length, width = middle.shape
+    tile = min(tile, length)
+    by_rows = pl.BlockSpec((tile, width), lambda step: (step, 0))
+    return pl.pallas_call(
+        finish_kernel,
+        grid=(length // tile,),
+        in_specs=[by_rows] * 5 + [pl.BlockSpec(rows.shape, lambda step: (0, 0))],
+        out_specs=[by_rows, pl.BlockSpec((8, width), lambda step: (0, 0))],
+        out_shape=[
+            jax.ShapeDtypeStruct((length, width), jnp.bfloat16),
+            jax.ShapeDtypeStruct((8, width), jnp.float32),
+        ],
+        compiler_params=vmem_params(),
+        cost_estimate=cost(8 * length * width, 20 * length * width),
+        name="finish",
+    )(branch_mlp, middle, branch, dmiddle, cotangent, rows)
+
+
+def square_grads_kernel(place, across_ref, grads_ref, low_ref, dbranch_ref, *rest):
     *stores, staged, sems = rest
     step = pl.program_id(0)
     part = jnp.bitwise_xor(place[2], step)
@@ -679,59 +680,41 @@
     def leave(r):
         return square_stores(place, stores, r, staged.at[r % 2], sems.at[r % 2])
 
-    def pass_on(r):
-        if len(stores) == 1:
-            return [pltpu.make_async_copy(out_grad_ref, stores[0].at[3], sems.at[r % 2])]
-        copies, column = [], 0
-        for pair in range(0, len(stores), 2):
-            out = stores[pair + r % 2]
-            columns = out.shape[4]
-            source = out_grad_ref.at[:, :, :, pl.ds(column, columns)]
-            copies.append(pltpu.make_async_copy(source, out.at[r // 2], sems.at[r % 2]))
-            column += columns
-        return copies
-
-    def wait(r):
-        wait_all(pass_on(r))
-
-    for_each(step - 2, wait)
+    for_each(step - 2, lambda r: wait_all(leave(r)))
 
     @pl.when(part < 3)
     def _():
-        grads = grads_ref[0]
-        staged[step % 2] = matmul(across_ref[...], grads, ROWS_NN).astype(jnp.bfloat16)
-        for_each(step, lambda r: start_all(leave(r)))
+        staged[step % 2] = matmul(across_ref[...], grads_ref[0], ROWS_NN).astype(jnp.bfloat16)
 
     @pl.when(part == 3)
     def _():
-        for_each(step, lambda r: start_all(pass_on(r)))
+        staged[step % 2] = matmul(low_ref[...], dbranch_ref[...], ROWS_TN).astype(jnp.bfloat16)
+
+    for_each(step, lambda r: start_all(leave(r)))
 
     @pl.when(step == 3)
     def _():
-        wait(2)
-        wait(3)
-
-
-def square_grads(place, across, grads, out_grad, block_rows, columns):
+        wait_all(leave(2))
+        wait_all(leave(3))
+
+
+def square_grads(place, across, grads, low, dbranch, paired, block_rows, columns):
     width, length = across.shape
-    paired = len(out_grad.shape) > 2
     stores = gradient_shapes(paired, block_rows, columns)
+    held = pl.BlockSpec((length, width), lambda step, place: (0, 0), pipeline_mode=pl.Buffered(1))
     return pl.pallas_call(
         square_grads_kernel,
         grid_spec=pltpu.PrefetchScalarGridSpec(
             num_scalar_prefetch=1,
             grid=(4,),
             in_specs=[
-                pl.BlockSpec((width, length), lambda step, place: (0, 0)),
+                pl.BlockSpec((width, length), lambda step, place: (0, 0), pipeline_mode=pl.Buffered(1)),
                 pl.BlockSpec(
                     (1, length, width),
                     lambda step, place: (jnp.minimum(jnp.bitwise_xor(place[2], step), 2), 0, 0),
                 ),
-                pl.BlockSpec(
-                    out_grad.shape,
-                    lambda step, place: (0,) * len(out_grad.shape),
-                    pipeline_mode=pl.Buffered(1),
-                ),
+                held,
+                held,
             ],
             out_specs=[ANY] * len(stores),
             scratch_shapes=[
@@ -741,9 +724,9 @@
         ),
         out_shape=stores,
         compiler_params=vmem_params(),
-        cost_estimate=cost(6 * length * width * width, 16 * length * width),
+        cost_estimate=cost(8 * length * width * width, 20 * length * width),
         name="square_grads",
-    )(place, across, grads, out_grad)
+    )(place, across, grads, low, dbranch)
 
 
 def tokens_back_kernel(place, grads_ref, tokens_ref, dmiddle_ref, rows_ref, *rest, sets):
@@ -859,15 +842,20 @@
             return swap(value, "fsdp", self.shards, 1)
         return swap(value, "dp", self.group, 2 if kind == "y" else 1)
 
+    def corners(self, block):
+        size = self.shards * self.group
+        x, y, far = [
+            lax.ppermute(block, ("fsdp", "dp"), [(i, i ^ step) for i in range(size)])
+            for step in (self.group, 2, self.group + 2)
+        ]
+        return jnp.stack([jnp.stack([block, x]), jnp.stack([y, far])])
+
     def ahead(self, value, count):
         pairs = [((target // 2 + count) % 4 * 2 + target % 2, target) for target in range(8)]
         return lax.ppermute(value, "fsdp", pairs)
 
     def along_z(self, block):
         return jnp.stack([block] + [self.ahead(block, count) for count in (1, 2, 3)])
-
-    def along_x(self, block):
-        return jnp.stack([block, self.partner(block, "x")])
 
     def pair(self, block, kind):
         return jnp.stack([block, self.partner(block, kind)])
@@ -957,11 +945,11 @@
 
     fact = jnp.stack([timesteps[0], labels[0]])
     if paired:
-        near = net.along_z(fact)
+        near = net.pair(fact, "x")
         mine = lax.dynamic_slice_in_dim(four, member * width, width, axis=1)
         mine, near = barrier((mine, near))
+        near = net.along_z(near)
         square = net.along_z(mine)
-        near = net.along_x(near).swapaxes(0, 1)
         facts = jnp.where(place[1] == 0, near, near[:, ::-1])
         facts = lax.dynamic_slice_in_dim(
             jnp.concatenate([facts, facts]), (4 - place[0]) % 4, 4, axis=0
@@ -991,7 +979,8 @@
     if paired:
         square, sent, near = barrier((square, sent, near))
         parts = lax.all_to_all(sent, "fsdp", 0, 0, tiled=True)
-        all_facts = net.pair(net.pair(near.swapaxes(0, 1), "y"), "c").reshape(image_count, 2)
+        all_facts = net.pair(net.pair(near.swapaxes(0, 1), "c").swapaxes(0, 1), "y")
+        all_facts = all_facts.reshape(image_count, 2)
         first = net.pair(square[:, :, : splits[0]], "x")
         second = net.pair(square[:, :, splits[0] :], "y")
         mine = lax.dynamic_slice_in_dim(up_weight, member * width, width, axis=1)
@@ -1000,7 +989,10 @@
         mine, down_mine, first, second, parts = barrier((mine, down_mine, first, second, parts))
         first_y, second_x = net.partner(first, "y"), net.partner(second, "x")
         up = net.along_z(mine)
-        first, second, first_y, second_x, up = barrier((first, second, first_y, second_x, up))
+        prepared = prepare(tokens[0], cotangent[0], parts)
+        first, second, first_y, second_x, up, prepared = barrier(
+            (first, second, first_y, second_x, up, prepared)
+        )
         down = lax.all_gather(after(down_mine, first_y), "fsdp", axis=0)
         squares = [
             Blocks([first, first_y, net.partner(first, "c"), net.partner(first_y, "c")], "xy"),
@@ -1011,27 +1003,32 @@
         all_facts = gather_rows(facts, "dp", group_count)
         found = lax.all_gather(four, "fsdp", axis=0, tiled=True)
         squares = [Blocks([found.reshape(width, 4, width).swapaxes(0, 1)], "xy")]
-    mod_one, mod_across, branch_grad, down_bias_g, rows = prepare(tokens[0], cotangent[0], parts)
+        prepared = prepare(tokens[0], cotangent[0], parts)
+    mod_one, mod_across, branch_grad, down_bias_g, rows = prepared
     if paired:
         up_x, up_y = net.partner(up, "x"), net.partner(up, "y")
     qkv = project(place, mod_one, rows, squares)
     if paired:
-        qkv, up_x, up_y = barrier((qkv, up_x, up_y))
-        up_xy = net.partner(up_x, "y")
+        qkv, up_x, up_y, all_facts = barrier((qkv, up_x, up_y, all_facts))
+        up = jnp.stack([up, up_x])
+        up_xy, up_c = net.partner(up_x, "y"), net.partner(up, "c")
     attn_low, lse = attend_forward(qkv, head_keep[0])
     if paired:
-        attn_low, up_xy, down = barrier((attn_low, up_xy, down))
-        up, up_y = jnp.stack([up, up_x]), jnp.stack([up_y, up_xy])
-        ups = [Blocks([up, up_y, net.partner(up, "c"), net.partner(up_y, "c")], "xy")]
+        attn_low, up, up_xy, up_c = barrier((attn_low, up, up_xy, up_c))
+        up_y = jnp.stack([up_y, up_xy])
+        up_y_c = net.partner(up_y, "c")
+    attn_branch, middle, mod_two, mod_two_across = after_attention(
+        place, attn_low, tokens[0], rows, squares
+    )
+    if paired:
+        mod_two, down, up_y_c = barrier((mod_two, down, up_y_c))
+        ups = [Blocks([up, up_y, up_c, up_y_c], "xy")]
         downs = [down, net.partner(down, "c")]
     else:
         found = lax.all_gather(up_weight, "fsdp", axis=0, tiled=True)
         ups = [Blocks([found.reshape(width, 4, width).swapaxes(0, 1)], "xy")]
         found = lax.all_gather(down_weight, "fsdp", axis=0, tiled=True)
         downs = [found.reshape(4, width, width)]
-    attn_branch, middle, mod_two, mod_two_across = after_attention(
-        place, attn_low, tokens[0], rows, squares
-    )
     branch_mlp, mod_two_grad, up_bias_g, *stores = mlp(
         place,
         mod_two,
@@ -1050,21 +1047,10 @@
     else:
         up_shard = jnp.concatenate(reduce_columns(stores[0]), axis=1)
         down_shard = reduce_all(stores[1].reshape(hidden, width))
-    block_out, middle_grad, low_grad, sums, out_weight_g = after_mlp(
-        place,
-        branch_mlp,
-        mod_two_grad,
-        middle,
-        attn_branch,
-        cotangent[0],
-        attn_low,
-        rows,
-        squares,
-        columns,
-    )
-    gate_mlp_grad, scale_mlp_grad, shift_mlp_grad, gate_attn_grad, out_bias_g = [
-        sums[i] for i in range(5)
-    ]
+    middle_grad, dbranch, low_grad, sums = after_mlp(
+        place, mod_two_grad, middle, cotangent[0], rows, squares
+    )
+    scale_mlp_grad, shift_mlp_grad, out_bias_g = sums[0], sums[1], sums[2]
     if paired:
         low_grad, up_other, down_other = barrier((low_grad, up_other, down_other))
         up_go, up_stay = net.first_sum(up_kept, up_other, "x")
@@ -1078,9 +1064,48 @@
         down_go, down_stay = net.second_sum(down_stay, down_back)
         grads, up_go, down_go = barrier((grads, up_go, down_go))
         up_back, down_back = net.partner(up_go, "y"), net.partner(down_go, "x")
+    stores = square_grads(
+        place, mod_across, grads, attn_low, dbranch, paired, columns, splits
+    )
+    block_out, gate_sums = finish(branch_mlp, middle, attn_branch, middle_grad, cotangent[0], rows)
+    if paired:
+        stores, grads, up_back, down_back, block_out, gate_sums = barrier(
+            (stores, grads, up_back, down_back, block_out, gate_sums)
+        )
+        others = [net.partner(sent, "c") for sent in stores[1::2]]
+        others = barrier(others)
+        goes, stays = zip(
+            *[net.first_sum(stores[2 * i], others[i], kind) for i, kind in enumerate("yx")]
+        )
+        up_mine = add(up_stay, up_back)
+        goes, up_mine, grads = barrier((goes, up_mine, grads))
+        backs = [net.partner(go, kind) for go, kind in zip(goes, "yx")]
+        up_terms = net.send_z(up_mine)
+    def small_grads(all_rows):
+        cond = conditioning(all_facts[:, 0], all_facts[:, 1], class_table, shard, width)
+        cond_act, silu_pull = jax.vjp(jax.nn.silu, cond)
+        ada_grad = all_rows[:, : 6 * width]
+        ada_weight_g = jnp.einsum(
+            "sd,se->de", cond_act.astype(bf16), ada_grad, preferred_element_type=f32
+        )
+        cond_act_grad = jnp.einsum("se,de->sd", ada_grad, ada_weight, preferred_element_type=f32)
+        cond_grad = silu_pull(cond_act_grad)[0]
+        picked = all_facts[:, 1][:, None] == jnp.arange(class_count, dtype=jnp.int32)[None, :]
+        table_g = jnp.einsum(
+            "sc,sd->cd", picked.astype(f32), cond_grad, precision=lax.Precision.HIGHEST
+        )
+        sums = jnp.sum(all_rows.astype(f32), axis=0)
+        ada_bias_g = own_part(sums[: 6 * width], shard, ada_bias.shape[0])
+        qv_bias_g = own_part(sums[6 * width : 8 * width].reshape(2, width), shard, columns)
+        out_bias_own = own_part(sums[8 * width : 9 * width], shard, columns)
+        up_bias_own = own_part(sums[9 * width : 9 * width + hidden], shard, up_bias.shape[0])
+        down_bias_own = own_part(sums[9 * width + hidden :], shard, columns)
+        return qv_bias_g, out_bias_own, up_bias_own, down_bias_own, ada_weight_g, ada_bias_g, table_g
+
     tokens_grad, sums = tokens_back(place, grads, tokens[0], middle_grad, rows, squares)
     if paired:
-        sums, up_back, down_back, grads = barrier((sums, up_back, down_back, grads))
+        tokens_grad, sums, backs, up_terms = barrier((tokens_grad, sums, backs, up_terms))
+    gate_mlp_grad, gate_attn_grad = gate_sums[0], gate_sums[1]
     row = jnp.concatenate(
         [
             sums[0],
@@ -1097,35 +1122,21 @@
         ]
     ).astype(bf16)[None]
     if paired:
-        up_mine, down_mine = add(up_stay, up_back), add(down_stay, down_back)
-        row, up_mine, down_mine, grads = barrier((row, up_mine, down_mine, grads))
-        up_terms = net.send_z(up_mine)
+        down_mine = add(down_stay, down_back)
+        goes, stays = zip(*[net.second_sum(stay, back) for stay, back in zip(stays, backs)])
+        goes, row, down_mine = barrier((goes, row, down_mine))
         row = net.along_z(row)
-    stores = square_grads(place, mod_across, grads, out_weight_g, columns, splits)
-    if paired:
-        stores, row, up_terms = barrier((stores, row, up_terms))
-        others = [net.partner(sent, "c") for sent in stores[1::2]]
-        row = net.pair(row, "x")
-        others, row = barrier((others, row))
-        goes, stays = zip(
-            *[net.first_sum(stores[2 * i], others[i], kind) for i, kind in enumerate("yx")]
-        )
-        goes, row, down_mine = barrier((goes, row, down_mine))
-        row = net.pair(row, "y")
-        backs = [net.partner(go, kind) for go, kind in zip(goes, "yx")]
+        backs = [net.partner(go, kind) for go, kind in zip(goes, "xy")]
         down_terms = net.send_z(down_mine)
         backs, down_terms, row = barrier((backs, down_terms, row))
-        goes, stays = zip(*[net.second_sum(stay, back) for stay, back in zip(stays, backs)])
-        goes, row = barrier((goes, row))
-        all_rows = net.pair(row, "c").reshape(image_count, -1)
-        backs = [net.partner(go, kind) for go, kind in zip(goes, "xy")]
+        mine = jnp.concatenate([add(stay, back) for stay, back in zip(stays, backs)], axis=2)
         part = jnp.stack([add(up_mine[0], *up_terms), add(down_mine[0], *down_terms)])
-        backs, part, all_rows = barrier((backs, part, all_rows))
-        mine = jnp.concatenate([add(stay, back) for stay, back in zip(stays, backs)], axis=2)
-        mine, part = barrier((mine, part))
+        mine, part, row = barrier((mine, part, row))
         terms = net.send_z(mine)
+        row = net.corners(net.pair(row, "c"))
         mlp_parts = both(part, "dp", group_count, 2, 0)
-        terms, mlp_parts = barrier((terms, mlp_parts))
+        terms, row, mlp_parts = barrier((terms, row, mlp_parts))
+        small = small_grads(row.reshape(image_count, -1))
         mlp_parts = both(mlp_parts, "dp", group_count, 1, 1).reshape(4, *part.shape)
         parts = net.to_group(add(mine[0], *terms)).astype(f32)
         up_shard = jnp.concatenate([mlp_parts[i, 0] for i in range(4)], axis=1).astype(f32)
@@ -1134,25 +1145,17 @@
     else:
         query_g, key_g, value_g, out_shard = reduce_columns(stores[0])
         all_rows = gather_rows(gather_rows(row, "fsdp", shard_count), "dp", group_count)
+        small = small_grads(all_rows)
     qkv_shard = jnp.concatenate([query_g, key_g, value_g], axis=1)
-    cond = conditioning(all_facts[:, 0], all_facts[:, 1], class_table, shard, width)
-    cond_act, silu_pull = jax.vjp(jax.nn.silu, cond)
-    ada_grad = all_rows[:, : 6 * width]
-    ada_weight_g = jnp.einsum(
-        "sd,se->de", cond_act.astype(bf16), ada_grad, preferred_element_type=f32
-    )
-    cond_act_grad = jnp.einsum("se,de->sd", ada_grad, ada_weight, preferred_element_type=f32)
-    cond_grad = silu_pull(cond_act_grad)[0]
-    picked = all_facts[:, 1][:, None] == jnp.arange(class_count, dtype=jnp.int32)[None, :]
-    table_g = jnp.einsum(
-        "sc,sd->cd", picked.astype(f32), cond_grad, precision=lax.Precision.HIGHEST
-    )
-    sums = jnp.sum(all_rows.astype(f32), axis=0)
-    ada_bias_g = own_part(sums[: 6 * width], shard, ada_bias.shape[0])
-    qv_bias_g = own_part(sums[6 * width : 8 * width].reshape(2, width), shard, columns)
-    out_bias_g = own_part(sums[8 * width : 9 * width], shard, columns)
-    up_bias_g = own_part(sums[9 * width : 9 * width + hidden], shard, up_bias.shape[0])
-    down_bias_g = own_part(sums[9 * width + hidden :], shard, columns)
+    (
+        qv_bias_g,
+        out_bias_g,
+        up_bias_g,
+        down_bias_g,
+        ada_weight_g,
+        ada_bias_g,
+        table_g,
+    ) = small
     return (
         block_out[None],
         tokens_grad[None],

time: 655 us -> 616 us (0.940)
  waiting for transfers between devices: 153 us -> 131 us
    ppermute x21, waiting for transfers between devices: 95.3 us -> 67.5 us  [ahead(): return lax.ppermute(value, 'fsdp', pairs)]
    ppermute x0 -> x3, waiting for transfers between devices: none -> 17.1 us  [corners(): lax.ppermute(block, ('fsdp', 'dp'), [(i, i ^ step) for i in range(size)])]
    pallas_call x0 -> x1, Pallas kernels: none -> 9.43 us  [finish(): pl.pallas_call(finish_kernel, grid=(length // tile,), in_specs=[by_rows]...]
    pallas_call x1, Pallas kernels: 23.2 us -> 13.9 us  [after_mlp(): pl.pallas_call(functools.partial(after_mlp_kernel, sets=squares), grid_sp...]
    all_gather x1, waiting for transfers between devices: 7.75 us -> 0.02 us  [body(): down = lax.all_gather(after(down_mine, first_y), 'fsdp', axis=0)]
    ppermute x36 -> x34, starting transfers between devices: 35.4 us -> 32.7 us  [swap(): return lax.ppermute(value, axis, [(i, i ^ step) for i in range(size)])]
    ppermute x36 -> x34, waiting for transfers between devices: 45.4 us -> 46 us  [swap(): return lax.ppermute(value, axis, [(i, i ^ step) for i in range(size)])]
  transfers between devices with their start and end apart: 59 -> 60, of which waited for: 24 -> 20; matrix products, arithmetic and copies ran while one was open for 9% -> 9% of each run, Pallas kernels for 31% -> 33%
where the time goes in v4:
time: 616 us; the launch traced here: 610 us
  Pallas kernels  300 us (49%)
  waiting for transfers between devices  131 us (21%)
  starting transfers between devices  69 us (11%)
  other arithmetic  65.9 us (11%)
  local copies, waits for them, and re-layouts  19.4 us (3%)
  between operations  16.7 us (3%)
  matrix products  8.6 us (1%)
    pallas_call x1, Pallas kernels, mlp(): pl.pallas_call(functools.partial(mlp_kernel, ups=ups, downs=len(downs)),...  98.5 us
    ppermute x21, waiting for transfers between devices, ahead(): return lax.ppermute(value, 'fsdp', pairs)  67.5 us
    pallas_call x1, Pallas kernels, attend_backward(): pl.pallas_call(functools.partial(attend_backward_kernel, head_size=width...  57.7 us
    ppermute x34, waiting for transfers between devices, swap(): return lax.ppermute(value, axis, [(i, i ^ step) for i in range(size)])  46 us
    pallas_call x1, Pallas kernels, attend_forward(): pl.pallas_call(functools.partial(attend_forward_kernel, head_size=width /...  37.1 us
    ppermute x34, starting transfers between devices, swap(): return lax.ppermute(value, axis, [(i, i ^ step) for i in range(size)])  32.7 us
    convert_element_type x12, other arithmetic, add(): sum((term.astype(jnp.float32) for term in terms)).astype(jnp.bfloat16)  32.5 us
    ppermute x21, starting transfers between devices, ahead(): return lax.ppermute(value, 'fsdp', pairs)  29 us
  transfers between devices with their start and end apart: 60, of which 20 were waited for; matrix products, arithmetic and copies ran while one was open for 9% of the time, Pallas kernels for 33%

profile of v4, /device:TPU:1, one launch (start us, length us, event | category | flops | bytes accessed | tf_op | source)
XLA Modules:
  0.0 610.2 jit_solution(14693170429772531062)
XLA Ops:
  30.2 9.2 %collective-permute-done.1 = bf16[144,1152]{1,0:T(8,128)(2,1)S(1)} collective-permute-done((bf16[144,1152]{1,0:T(8,128)(2,1)S(1)}, bf16[144,1152]{1,0:T(8,128)(2,1)S(1)}, u32[]{:S(2)}, u32[]{:S(2)}) %collective-permute-start.1) | collective-permute-done | bytes 331808 | tf_op jit(solution)/shard_map/ppermute | solution.py:855
  39.5 14.2 %collective-permute-done.2 = bf16[144,1152]{1,0:T(8,128)(2,1)S(1)} collective-permute-done((bf16[144,1152]{1,0:T(8,128)(2,1)S(1)}, bf16[144,1152]{1,0:T(8,128)(2,1)S(1)}, u32[]{:S(2)}, u32[]{:S(2)}) %collective-permute-start.2) | collective-permute-done | bytes 331808 | tf_op jit(solution)/shard_map/ppermute | solution.py:855
  66.6 8.3 %collective-permute-done.7 = bf16[4,144,512]{2,1,0:T(8,128)(2,1)} collective-permute-done((bf16[4,144,512]{2,1,0:T(8,128)(2,1)}, bf16[4,144,512]{2,1,0:T(8,128)(2,1)}, u32[]{:S(2)}, u32[]{:S(2)}) %collective-permute-start.7) | collective-permute-done | bytes 589856 | tf_op jit(solution)/shard_map/ppermute | solution.py:815
  83.0 6.7 %prepare.1 = (bf16[1024,1152]{1,0:T(8,128)(2,1)}, bf16[1152,1024]{1,0:T(8,128)(2,1)}, bf16[1024,1152]{1,0:T(8,128)(2,1)}, f32[8,1152]{1,0:T(8,128)}, f32[16,1152]{1,0:T(8,128)}) custom-call(bf16[1024,1152]{1,0:T(8,128)(2,1)} %bitcast.222, bf16[1024,1152]{1,0:T(8,128)(2,1)} %bitcast.219, f32[8,16128]{1,0:T(8,128)} %bitcast.231), custom_call_target="tpu_custom_call" | custom-call | flops 1 | bytes 1 | tf_op jit(solution)/shard_map/prepare/pallas_call | solution.py:333
  90.0 16.4 %collective-permute-done.12 = bf16[144,1152]{1,0:T(8,128)(2,1)S(1)} collective-permute-done((bf16[144,1152]{1,0:T(8,128)(2,1)}, bf16[144,1152]{1,0:T(8,128)(2,1)S(1)}, u32[]{:S(2)}, u32[]{:S(2)}) %collective-permute-start.12) | collective-permute-done | bytes 331808 | tf_op jit(solution)/shard_map/ppermute | solution.py:855
  127.5 19.8 %project.1.query_ref.key_ref.value_ref = bf16[4,1024,1152]{2,1,0:T(8,128)(2,1)} custom-call(s32[3]{0:T(128)} %pad_add_fusion.3.place, bf16[1024,1152]{1,0:T(8,128)(2,1)} %get-tuple-element.141.mod_ref, f32[16,1152]{1,0:T(8,128)} %get-tuple-element.142.rows_ref, bf16[2,4,144,512]{3,2,1,0:T(8,128)(2,1)} %pad_maximum_fusion.9.rest_0_, ...), custom_call_target="tpu_custom_call" | custom-call | flops 1 | bytes 1 | tf_op jit(solution)/shard_map/project/pallas_call | solution.py:383
  147.3 10.6 %collective-permute-done.18 = bf16[4,144,1152]{2,1,0:T(8,128)(2,1)} collective-permute-done((bf16[4,144,1152]{2,1,0:T(8,128)(2,1)}, bf16[4,144,1152]{2,1,0:T(8,128)(2,1)}, u32[]{:S(2)}, u32[]{:S(2)}) %collective-permute-start.18) | collective-permute-done | bytes 1327136 | tf_op jit(solution)/shard_map/ppermute | solution.py:815
  163.3 37.1 %attend_forward.1 = (bf16[1024,1152]{1,0:T(8,128)(2,1)S(1)}, f32[16,1024]{1,0:T(8,128)S(1)}) custom-call(s32[16]{0:T(128)S(1)} %bitcast.218, bf16[4,1024,1152]{2,1,0:T(8,128)(2,1)} %project.1.query_ref.key_ref.value_ref, bf16[4,1024,1152]{2,1,0:T(8,128)(2,1)} %project.1.query_ref.key_ref.value_ref, bf16[4,1024,1152]{2,1,0:T(8,128)(2,1)} %project.1.query_ref.key_ref.value_ref), custom_call_target="tpu_custom_call" | custom-call | flops 17179869184 | bytes 9437184 | tf_op jit(solution)/shard_map/attend_forward/pallas_call | solution.py:133
  203.6 11.7 %after_attention.1 = (f32[1024,1152]{1,0:T(8,128)}, f32[1024,1152]{1,0:T(8,128)}, bf16[1024,1152]{1,0:T(8,128)(2,1)}, bf16[1152,1024]{1,0:T(8,128)(2,1)}) custom-call(s32[3]{0:T(128)} %pad_add_fusion.3.place, bf16[1024,1152]{1,0:T(8,128)(2,1)} %copy-done.1, bf16[1024,1152]{1,0:T(8,128)(2,1)} %bitcast.223, f32[16,1152]{1,0:T(8,128)} %get-tuple-element.142.rows_ref, ...), custom_call_target="tpu_custom_call" | custom-call | flops 1 | bytes 1 | tf_op jit(solution)/shard_map/after_attention/pallas_call | solution.py:443
  216.3 8.3 %collective-permute-done.25.rest_5_ = bf16[8,2,144,1152]{3,2,1,0:T(8,128)(2,1)} collective-permute-done((bf16[8,2,144,1152]{3,2,1,0:T(8,128)(2,1)}, bf16[8,2,144,1152]{3,2,1,0:T(8,128)(2,1)}, u32[]{:S(2)}, u32[]{:S(2)}) %collective-permute-start.25) | collective-permute-done | bytes 5308448 | tf_op jit(solution)/shard_map/ppermute | solution.py:815
  224.5 98.5 %mlp.1 = (f32[1024,1152]{1,0:T(8,128)}, f32[1024,1152]{1,0:T(8,128)}, f32[4,1152]{1,0:T(4,128)}, bf16[2,2,4,144,1152]{4,3,2,1,0:T(8,128)(2,1)}, bf16[2,2,4,144,1...) custom-call(s32[3]{0:T(128)} %pad_add_fusion.3.place, ...), custom_call_target="tpu_custom_call" | custom-call | flops 1 | bytes 1 | tf_op jit(solution)/shard_map/mlp/pallas_call | solution.py:557
  323.6 13.9 %after_mlp.1 = (f32[1024,1152]{1,0:T(8,128)}, bf16[1024,1152]{1,0:T(8,128)(2,1)}, bf16[1024,1152]{1,0:T(8,128)(2,1)}, f32[8,1152]{1,0:T(8,128)}) custom-call(s32[3]{0:T(128)} %pad_add_fusion.3.place, f32[1024,1152]{1,0:T(8,128)} %get-tuple-element.165.dmod_ref, f32[1024,1152]{1,0:T(8,128)} %get-tuple-element.166.middle_ref, bf16[1024,1152]{1,0:T(8,128)(2,1)} %bitcast.220, ...), custom_call_target="tpu_custom_call" | custom-call | flops 1 | bytes 1 | tf_op jit(solution)/shard_map/after_mlp/pallas_call | solution.py:621
  339.8 4.2 fusion.1
  348.7 57.7 %attend_backward.1.grads_ref = bf16[3,1024,1152]{2,1,0:T(8,128)(2,1)} custom-call(s32[16]{0:T(128)} %bitcast.217, bf16[4,1024,1152]{2,1,0:T(8,128)(2,1)} %project.1.query_ref.key_ref.value_ref, bf16[4,1024,1152]{2,1,0:T(8,128)(2,1)} %project.1.query_ref.key_ref.value_ref, bf16[4,1024,1152]{2,1,0:T(8,128)(2,1)} %project.1.query_ref.key_ref.value_ref, ...), custom_call_target="tpu_custom_call" | custom-call | flops 42949672960 | bytes 18874368 | tf_op jit(solution)/shard_map/attend_backward/pallas_call | solution.py:160
  407.4 5.6 fusion.4
  414.5 9.4 %finish.1 = (bf16[1024,1152]{1,0:T(8,128)(2,1)}, f32[8,1152]{1,0:T(8,128)}) custom-call(f32[1024,1152]{1,0:T(8,128)} %get-tuple-element.190.mlp_ref, f32[1024,1152]{1,0:T(8,128)} %get-tuple-element.166.middle_ref, f32[1024,1152]{1,0:T(8,128)} %get-tuple-element.191.branch_ref, f32[1024,1152]{1,0:T(8,128)} %get-tuple-element.192.dmiddle_ref, ...), custom_call_target="tpu_custom_call" | custom-call | flops 1 | bytes 1 | tf_op jit(solution)/shard_map/finish/pallas_call | solution.py:660
  423.9 19.3 %square_grads.1 = (bf16[2,2,4,144,512]{4,3,2,1,0:T(8,128)(2,1)}, bf16[2,2,4,144,512]{4,3,2,1,0:T(8,128)(2,1)}, bf16[2,2,4,144,640]{4,3,2,1,0:T(8,128)(2,1)}, bf16[2,2,4,144,640]{4,3,2,1,0:T(8,128)(2,1)}) custom-call(s32[3]{0:T(128)} %pad_add_fusion.3.place, bf16[1152,1024]{1,0:T(8,128)(2,1)} %get-tuple-element.140.across_ref, ...), custom_call_target="tpu_custom_call" | custom-call | flops 1 | bytes 1 | tf_op jit(solution)/shard_map/square_grads/pallas_call | solution.py:705
  449.0 4.9 collective-permute-done.32
  469.2 25.9 %tokens_back.1 = (bf16[1024,1152]{1,0:T(8,128)(2,1)}, f32[8,1152]{1,0:T(8,128)}) custom-call(s32[3]{0:T(128)} %pad_add_fusion.3.place, bf16[3,1024,1152]{2,1,0:T(8,128)(2,1)} %attend_backward.1.grads_ref, bf16[1024,1152]{1,0:T(8,128)(2,1)} %bitcast.224, f32[1024,1152]{1,0:T(8,128)} %get-tuple-element.192.dmiddle_ref, ...), custom_call_target="tpu_custom_call" | custom-call | flops 1 | bytes 1 | tf_op jit(solution)/shard_map/tokens_back/pallas_call | solution.py:768
  508.6 5.9 collective-permute-done.41
  514.5 15.3 %collective-permute-done.42 = bf16[144,1152]{1,0:T(8,128)(2,1)S(1)} collective-permute-done((bf16[144,1152]{1,0:T(8,128)(2,1)S(1)}, bf16[144,1152]{1,0:T(8,128)(2,1)S(1)}, u32[]{:S(2)}, u32[]{:S(2)}) %collective-permute-start.42) | collective-permute-done | bytes 331808 | tf_op jit(solution)/shard_map/ppermute | solution.py:855
  533.6 4.6 collective-permute-start.50
  548.3 17.1 %collective-permute-done.52 = bf16[2,4,1,16128]{3,1,0,2:T(4,128)(2,1)S(1)} collective-permute-done((bf16[2,4,1,16128]{3,1,0,2:T(4,128)(2,1)S(1)}, bf16[2,4,1,16128]{3,1,0,2:T(4,128)(2,1)S(1)}, u32[]{:S(2)}, u32[]{:S(2)}) %collective-permute-start.52) | collective-permute-done | bytes 258080 | tf_op jit(solution)/shard_map/ppermute | solution.py:848
  565.4 5.2 collective-permute-start.49
  (297 shorter events, 163.8 us)
Async XLA Ops:
  24.1 29.6 %collective-permute-start.2 = (bf16[144,1152]{1,0:T(8,128)(2,1)S(1)}, bf16[144,1152]{1,0:T(8,128)(2,1)S(1)}, u32[]{:S(2)}, u32[]{:S(2)}) collective-permute-start(bf16[144,1152]{1,0:T(8,128)(2,1)S(1)} %fusion.28), channel_id=1, source_target_pairs={{16,0},{20,4},{24,8},{28,12},{0,16},{4,20},{8,24},{12,28},{17,1},{... | collective-permute-start | bytes 995336 | tf_op jit(solution)/shard_map/ppermute | solution.py:855
  62.6 152.8 %all-gather.3.cloned.1.call-start = ((), (), s32[]{:S(2)}) async-start(), calls=%async_computation.1 | async-start | bytes 5971968 | tf_op jit(solution)/shard_map/all_gather | solution.py:996
  80.9 30.8 %collective-permute-start.10 = (bf16[2,4,144,640]{3,2,1,0:T(8,128)(2,1)S(1)}, bf16[2,4,144,640]{3,2,1,0:T(8,128)(2,1)S(1)}, u32[]{:S(2)}, u32[]{:S(2)}) collective-permute-start(bf16[2,4,144,640]{3,2,1,0:T(8,128)(2,1)S(1)} %pad_maximum_fusion.4.rest_4_), channel_id=1, source_target_pairs={{0,4},{4,0},{8,12},{12,8},{16,20},{20,16},{24,28},{28,24},{1,5},{5... | collective-permute-start | bytes 4423688 | tf_op jit(solution)/shard_map/ppermute | solution.py:815
  81.1 26.5 %collective-permute-start.9 = (bf16[2,4,144,512]{3,2,1,0:T(8,128)(2,1)}, bf16[2,4,144,512]{3,2,1,0:T(8,128)(2,1)S(1)}, u32[]{:S(2)}, u32[]{:S(2)}) collective-permute-start(bf16[2,4,144,512]{3,2,1,0:T(8,128)(2,1)} %pad_maximum_fusion.9.rest_0_), channel_id=1, source_target_pairs={{0,2},{1,3},{2,0},{3,1},{4,6},{5,7},{6,4},{7,5},{8,10},{9,11},{10,... | collective-permute-start | bytes 3538952 | tf_op jit(solution)/shard_map/ppermute | solution.py:815
  81.8 24.6 %collective-permute-start.12 = (bf16[144,1152]{1,0:T(8,128)(2,1)}, bf16[144,1152]{1,0:T(8,128)(2,1)S(1)}, u32[]{:S(2)}, u32[]{:S(2)}) collective-permute-start(bf16[144,1152]{1,0:T(8,128)(2,1)} %constant_dynamic-slice_fusion.1), channel_id=1, source_target_pairs={{16,0},{20,4},{24,8},{28,12},{0,16},{4,20},{8,24},{12,28},{17,1},{... | collective-permute-start | bytes 995336 | tf_op jit(solution)/shard_map/ppermute | solution.py:855
  81.8 24.6 %collective-permute-start.13 = (bf16[144,1152]{1,0:T(8,128)(2,1)}, bf16[144,1152]{1,0:T(8,128)(2,1)S(1)}, u32[]{:S(2)}, u32[]{:S(2)}) collective-permute-start(bf16[144,1152]{1,0:T(8,128)(2,1)} %constant_dynamic-slice_fusion.1), channel_id=1, source_target_pairs={{24,0},{28,4},{0,8},{4,12},{8,16},{12,20},{16,24},{20,28},{25,1},{... | collective-permute-start | bytes 995336 | tf_op jit(solution)/shard_map/ppermute | solution.py:855
  120.4 37.4 %collective-permute-start.18 = (bf16[4,144,1152]{2,1,0:T(8,128)(2,1)}, bf16[4,144,1152]{2,1,0:T(8,128)(2,1)}, u32[]{:S(2)}, u32[]{:S(2)}) collective-permute-start(bf16[4,144,1152]{2,1,0:T(8,128)(2,1)} %pad_maximum_fusion.6), channel_id=1, source_target_pairs={{0,4},{4,0},{8,12},{12,8},{16,20},{20,16},{24,28},{28,24},{1,5},{5... | collective-permute-start | bytes 3981320 | tf_op jit(solution)/shard_map/ppermute | solution.py:815
  122.7 35.2 %collective-permute-start.19 = (bf16[4,144,1152]{2,1,0:T(8,128)(2,1)}, bf16[4,144,1152]{2,1,0:T(8,128)(2,1)}, u32[]{:S(2)}, u32[]{:S(2)}) collective-permute-start(bf16[4,144,1152]{2,1,0:T(8,128)(2,1)} %pad_maximum_fusion.6), channel_id=1, source_target_pairs={{0,2},{1,3},{2,0},{3,1},{4,6},{5,7},{6,4},{7,5},{8,10},{9,11},{10,... | collective-permute-start | bytes 3981320 | tf_op jit(solution)/shard_map/ppermute | solution.py:815
  159.5 41.0 %collective-permute-start.23 = (bf16[2,4,144,1152]{3,2,1,0:T(8,128)(2,1)S(1)}, bf16[2,4,144,1152]{3,2,1,0:T(8,128)(2,1)S(1)}, u32[]{:S(2)}, u32[]{:S(2)}) collective-permute-start(bf16[2,4,144,1152]{3,2,1,0:T(8,128)(2,1)S(1)} %pad_maximum_fusion.rest_0_), channel_id=1, source_target_pairs={{0,1},{1,0},{2,3},{3,2},{4,5},{5,4},{6,7},{7,6},{8,9},{9,8},{10,11... | collective-permute-start | bytes 7962632 | tf_op jit(solution)/shard_map/ppermute | solution.py:815
  162.0 38.5 %collective-permute-start.22 = (bf16[4,144,1152]{2,1,0:T(8,128)(2,1)}, bf16[4,144,1152]{2,1,0:T(8,128)(2,1)S(1)}, u32[]{:S(2)}, u32[]{:S(2)}) collective-permute-start(bf16[4,144,1152]{2,1,0:T(8,128)(2,1)} %collective-permute-done.18), channel_id=1, source_target_pairs={{0,2},{1,3},{2,0},{3,1},{4,6},{5,7},{6,4},{7,5},{8,10},{9,11},{10,... | collective-permute-start | bytes 3981320 | tf_op jit(solution)/shard_map/ppermute | solution.py:815
  348.0 59.3 %collective-permute-start.28 = (bf16[2,4,144,1152]{3,2,1,0:T(8,128)(2,1)}, bf16[2,4,144,1152]{3,2,1,0:T(8,128)(2,1)}, u32[]{:S(2)}, u32[]{:S(2)}) collective-permute-start(bf16[2,4,144,1152]{3,2,1,0:T(8,128)(2,1)} %fusion), channel_id=1, source_target_pairs={{0,4},{4,0},{8,12},{12,8},{16,20},{20,16},{24,28},{28,24},{1,5},{5... | collective-permute-start | bytes 7962632 | tf_op jit(solution)/shard_map/ppermute | solution.py:815
  348.2 59.2 %collective-permute-start.29 = (bf16[2,4,144,1152]{3,2,1,0:T(8,128)(2,1)}, bf16[2,4,144,1152]{3,2,1,0:T(8,128)(2,1)}, u32[]{:S(2)}, u32[]{:S(2)}) collective-permute-start(bf16[2,4,144,1152]{3,2,1,0:T(8,128)(2,1)} %fusion.1), channel_id=1, source_target_pairs={{0,2},{1,3},{2,0},{3,1},{4,6},{5,7},{6,4},{7,5},{8,10},{9,11},{10,... | collective-permute-start | bytes 7962632 | tf_op jit(solution)/shard_map/ppermute | solution.py:815
  412.9 30.3 %collective-permute-start.30 = (bf16[4,144,1152]{2,1,0:T(8,128)(2,1)}, bf16[4,144,1152]{2,1,0:T(8,128)(2,1)}, u32[]{:S(2)}, u32[]{:S(2)}) collective-permute-start(bf16[4,144,1152]{2,1,0:T(8,128)(2,1)} %get-tuple-element.188), channel_id=1, source_target_pairs={{0,2},{1,3},{2,0},{3,1},{4,6},{5,7},{6,4},{7,5},{8,10},{9,11},{10,... | collective-permute-start | bytes 3981320 | tf_op jit(solution)/shard_map/ppermute | solution.py:815
  413.3 29.9 %collective-permute-start.31 = (bf16[4,144,1152]{2,1,0:T(8,128)(2,1)}, bf16[4,144,1152]{2,1,0:T(8,128)(2,1)}, u32[]{:S(2)}, u32[]{:S(2)}) collective-permute-start(bf16[4,144,1152]{2,1,0:T(8,128)(2,1)} %get-tuple-element.189), channel_id=1, source_target_pairs={{0,4},{4,0},{8,12},{12,8},{16,20},{20,16},{24,28},{28,24},{1,5},{5... | collective-permute-start | bytes 3981320 | tf_op jit(solution)/shard_map/ppermute | solution.py:815
  459.5 35.8 %collective-permute-start.35 = (bf16[2,4,144,640]{3,2,1,0:T(8,128)(2,1)}, bf16[2,4,144,640]{3,2,1,0:T(8,128)(2,1)}, u32[]{:S(2)}, u32[]{:S(2)}) collective-permute-start(bf16[2,4,144,640]{3,2,1,0:T(8,128)(2,1)} %fusion.6), channel_id=1, source_target_pairs={{0,4},{4,0},{8,12},{12,8},{16,20},{20,16},{24,28},{28,24},{1,5},{5... | collective-permute-start | bytes 4423688 | tf_op jit(solution)/shard_map/ppermute | solution.py:815
  460.7 34.6 %collective-permute-start.34 = (bf16[2,4,144,512]{3,2,1,0:T(8,128)(2,1)}, bf16[2,4,144,512]{3,2,1,0:T(8,128)(2,1)}, u32[]{:S(2)}, u32[]{:S(2)}) collective-permute-start(bf16[2,4,144,512]{3,2,1,0:T(8,128)(2,1)} %fusion.9), channel_id=1, source_target_pairs={{0,2},{1,3},{2,0},{3,1},{4,6},{5,7},{6,4},{7,5},{8,10},{9,11},{10,... | collective-permute-start | bytes 3538952 | tf_op jit(solution)/shard_map/ppermute | solution.py:815
  462.8 32.4 %collective-permute-start.36 = (bf16[144,1152]{1,0:T(8,128)(2,1)}, bf16[144,1152]{1,0:T(8,128)(2,1)S(1)}, u32[]{:S(2)}, u32[]{:S(2)}) collective-permute-start(bf16[144,1152]{1,0:T(8,128)(2,1)} %get-tuple-element.263), channel_id=1, source_target_pairs={{24,0},{28,4},{0,8},{4,12},{8,16},{12,20},{16,24},{20,28},{25,1},{... | collective-permute-start | bytes 995336 | tf_op jit(solution)/shard_map/ppermute | solution.py:855
  462.8 32.4 %collective-permute-start.37 = (bf16[144,1152]{1,0:T(8,128)(2,1)}, bf16[144,1152]{1,0:T(8,128)(2,1)S(1)}, u32[]{:S(2)}, u32[]{:S(2)}) collective-permute-start(bf16[144,1152]{1,0:T(8,128)(2,1)} %get-tuple-element.262), channel_id=1, source_target_pairs={{16,0},{20,4},{24,8},{28,12},{0,16},{4,20},{8,24},{12,28},{17,1},{... | collective-permute-start | bytes 995336 | tf_op jit(solution)/shard_map/ppermute | solution.py:855
  462.9 32.3 %collective-permute-start.38 = (bf16[144,1152]{1,0:T(8,128)(2,1)}, bf16[144,1152]{1,0:T(8,128)(2,1)}, u32[]{:S(2)}, u32[]{:S(2)}) collective-permute-start(bf16[144,1152]{1,0:T(8,128)(2,1)} %get-tuple-element.261), channel_id=1, source_target_pairs={{8,0},{12,4},{16,8},{20,12},{24,16},{28,20},{0,24},{4,28},{9,1},{1... | collective-permute-start | bytes 995336 | tf_op jit(solution)/shard_map/ppermute | solution.py:855
  503.4 26.4 %collective-permute-start.42 = (bf16[144,1152]{1,0:T(8,128)(2,1)S(1)}, bf16[144,1152]{1,0:T(8,128)(2,1)S(1)}, u32[]{:S(2)}, u32[]{:S(2)}) collective-permute-start(bf16[144,1152]{1,0:T(8,128)(2,1)S(1)} %get-tuple-element.259), channel_id=1, source_target_pairs={{16,0},{20,4},{24,8},{28,12},{0,16},{4,20},{8,24},{12,28},{17,1},{... | collective-permute-start | bytes 995336 | tf_op jit(solution)/shard_map/ppermute | solution.py:855
  538.5 33.2 %collective-permute-start.54 = (bf16[2,144,1152]{2,1,0:T(8,128)(2,1)S(1)}, bf16[2,144,1152]{2,1,0:T(8,128)(2,1)S(1)}, u32[]{:S(2)}, u32[]{:S(2)}) collective-permute-start(bf16[2,144,1152]{2,1,0:T(8,128)(2,1)S(1)} %pad_maximum_fusion.11), channel_id=1, source_target_pairs={{0,2},{1,3},{2,0},{3,1},{4,6},{5,7},{6,4},{7,5},{8,10},{9,11},{10,... | collective-permute-start | bytes 1990664 | tf_op jit(solution)/shard_map/ppermute | solution.py:815
  540.7 32.3 %collective-permute-start.47 = (bf16[144,1152]{1,0:T(8,128)(2,1)S(1)}, bf16[144,1152]{1,0:T(8,128)(2,1)S(1)}, u32[]{:S(2)}, u32[]{:S(2)}) collective-permute-start(bf16[144,1152]{1,0:T(8,128)(2,1)S(1)} %get-tuple-element.257), channel_id=1, source_target_pairs={{24,0},{28,4},{0,8},{4,12},{8,16},{12,20},{16,24},{20,28},{25,1},{... | collective-permute-start | bytes 995336 | tf_op jit(solution)/shard_map/ppermute | solution.py:855
  543.9 29.2 %collective-permute-start.48 = (bf16[144,1152]{1,0:T(8,128)(2,1)S(1)}, bf16[144,1152]{1,0:T(8,128)(2,1)S(1)}, u32[]{:S(2)}, u32[]{:S(2)}) collective-permute-start(bf16[144,1152]{1,0:T(8,128)(2,1)S(1)} %get-tuple-element.256), channel_id=1, source_target_pairs={{16,0},{20,4},{24,8},{28,12},{0,16},{4,20},{8,24},{12,28},{17,1},{... | collective-permute-start | bytes 995336 | tf_op jit(solution)/shard_map/ppermute | solution.py:855
  547.1 23.5 %collective-permute-start.53 = (bf16[2,4,1,16128]{3,1,2,0:T(4,128)(2,1)S(1)}, bf16[2,4,1,16128]{3,1,2,0:T(4,128)(2,1)S(1)}, u32[]{:S(2)}, u32[]{:S(2)}) collective-permute-start(bf16[2,4,1,16128]{3,1,2,0:T(4,128)(2,1)S(1)} %get-tuple-element.272), channel_id=1, source_target_pairs={{0,6},{1,7},{2,4},{3,5},{4,2},{5,3},{6,0},{7,1},{8,14},{9,15},{10,... | collective-permute-start | bytes 774152 | tf_op jit(solution)/shard_map/ppermute | solution.py:848
  (65 other events, 709.5 us)
Sparse Core Ops, SparseCore 0:
  112.9 91.0 all-gather.2

commit v5 on v4

--- a/solution.py
+++ b/solution.py
@@ -285,18 +285,23 @@
             action(r)
 
 
-def fetch_squares(place, sets, step, held, sems):
+def fetch_squares(place, sets, step, count, held, sems):
+    def at(step, action):
+        slot = step % 2
+
+        @pl.when(step < count)
+        def _():
+            for_each(
+                jnp.bitwise_xor(place[2], step),
+                lambda r: action(square_copies(place, sets, r, held.at[slot], sems.at[slot])),
+            )
+
     @pl.when(step == 0)
     def _():
-        start_all(square_copies(place, sets, 0, held.at[0], sems.at[0]))
-
-    for_each(
-        step + 1,
-        lambda r: start_all(square_copies(place, sets, r, held.at[r % 2], sems.at[r % 2])),
-    )
-    for_each(
-        step, lambda r: wait_all(square_copies(place, sets, r, held.at[r % 2], sems.at[r % 2]))
-    )
+        at(step, start_all)
+
+    at(step + 1, start_all)
+    at(step, wait_all)
 
 
 def tiles(length, rows=256):
@@ -357,15 +362,11 @@
 def project_kernel(place, mod_ref, rows_ref, *rest, sets):
     *refs, out_ref, held, sems = rest
     step = pl.program_id(0)
-    fetch_squares(place, in_sets(refs, sets), step, held, sems)
-    part = jnp.bitwise_xor(place[2], step)
-
-    @pl.when(part < 3)
-    def _():
-        weight = held[step % 2]
-        bias = rows_ref[pl.ds(QUERY_BIAS + part // 2, 1)] * (part != 1).astype(jnp.float32)
-        for tile in tiles(mod_ref.shape[0]):
-            out_ref[0, tile] = (matmul(mod_ref[tile], weight, ROWS_NN) + bias).astype(jnp.bfloat16)
+    fetch_squares(place, in_sets(refs, sets), step, 3, held, sems)
+    weight = held.at[step % 2]
+    bias = rows_ref[pl.ds(QUERY_BIAS + step // 2, 1)] * (step != 1).astype(jnp.float32)
+    for tile in tiles(mod_ref.shape[0]):
+        out_ref[0, tile] = (matmul(mod_ref[tile], weight[...], ROWS_NN) + bias).astype(jnp.bfloat16)
 
 
 def vmem_params(mebibytes=56):
@@ -384,21 +385,21 @@
         functools.partial(project_kernel, sets=squares),
         grid_spec=pltpu.PrefetchScalarGridSpec(
             num_scalar_prefetch=1,
-            grid=(4,),
+            grid=(3,),
             in_specs=[
                 pl.BlockSpec((length, width), lambda step, place: (0, 0)),
                 pl.BlockSpec(rows.shape, lambda step, place: (0, 0)),
             ]
             + [ANY] * len(flat(squares)),
             out_specs=pl.BlockSpec(
-                (1, length, width), lambda step, place: (jnp.bitwise_xor(place[2], step), 0, 0)
+                (1, length, width), lambda step, place: (step, 0, 0)
             ),
             scratch_shapes=[
                 pltpu.VMEM((2, width, width), jnp.bfloat16),
                 pltpu.SemaphoreType.DMA((2,)),
             ],
         ),
-        out_shape=jax.ShapeDtypeStruct((4, length, width), jnp.bfloat16),
+        out_shape=jax.ShapeDtypeStruct((3, length, width), jnp.bfloat16),
         compiler_params=vmem_params(),
         cost_estimate=cost(6 * length * width * width, 14 * length * width),
         name="project",
@@ -473,65 +474,106 @@
     return values * half, slope
 
 
-def mlp_kernel(place, mod_ref, across_ref, grad_ref, rows_ref, keep_ref, *rest, ups, downs):
+def mlp_kernel(place, rows_ref, keep_ref, *rest, ups, downs):
+    inputs, rest = rest[:3], rest[3:]
     count = len(flat(ups)) + downs
     refs, rest = rest[:count], rest[count:]
     up_sets, down_refs = in_sets(refs, ups), refs[-downs:]
-    branch_ref, dmod_ref, dbias_ref = rest[:3]
-    *stores, act, dpre, up, down, up_out, down_out, in_sems, out_sems = rest[3:]
+    branch_out, dmod_out, dbias_ref, *stores = rest[:-12]
+    mod_ref, across_ref, grad_ref, branch_ref, dmod_ref, act, dpre, up_all, down_all = rest[-12:-3]
+    in_sems, out_sem, sum_sem = rest[-3:]
     up_stores, down_stores = stores[: len(stores) // 2], stores[len(stores) // 2 :]
-    step = pl.program_id(0)
-    length = mod_ref.shape[0]
+    length, width = mod_ref.shape
 
     def chunk_of(r):
         return jnp.bitwise_xor(place[2], r)
 
-    def fetch(r):
-        slot = r % 2
-        return square_copies(place, up_sets, r, up.at[slot], in_sems.at[slot, 0]) + strip_copies(
-            place, down_refs, chunk_of(r), down.at[slot], in_sems.at[slot, 1]
-        )
-
-    @pl.when(step == 0)
-    def _():
-        start_all(fetch(0))
-        branch_ref[...] = jnp.zeros_like(branch_ref)
-        dmod_ref[...] = jnp.zeros_like(dmod_ref)
-
-    for_each(step + 1, lambda r: start_all(fetch(r)))
-    for_each(step, lambda r: wait_all(fetch(r)))
-    chunk = chunk_of(step)
-    slot = step % 2
-    bias = rows_ref[pl.ds(UP_BIAS + chunk, 1)]
-    keep = keep_ref[pl.ds(chunk, 1)]
-    total = jnp.zeros_like(bias)
-    for tile in tiles(length, 512):
-        gelu, slope = gelu_and_slope(matmul(mod_ref[tile], up[slot], ROWS_NN) + bias)
-        act[tile] = (gelu * keep).astype(jnp.bfloat16)
-        back = matmul(grad_ref[tile], down[slot], ROWS_NT)
-        low = (slope * keep * back).astype(jnp.bfloat16)
-        dpre[tile] = low
-        total = total + jnp.sum(low.astype(jnp.float32), axis=0, keepdims=True)
-        branch_ref[tile] += matmul(act[tile], down[slot], ROWS_NN)
-        dmod_ref[tile] += matmul(low, up[slot], ROWS_NT)
-    dbias_ref[pl.ds(chunk, 1)] = total
-
-    def leave(r):
-        return square_stores(place, up_stores, r, up_out, out_sems.at[0]), strip_stores(
-            place, down_stores, chunk_of(r), down_out, out_sems.at[1]
-        )
-
-    for_each(step - 1, lambda r: wait_all(leave(r)[0]))
-    up_out[...] = matmul(across_ref[...], dpre[...], ROWS_NN).astype(jnp.bfloat16)
-    for_each(step, lambda r: start_all(leave(r)[0]))
-    for_each(step - 1, lambda r: wait_all(leave(r)[1]))
-    down_out[...] = matmul(act[...], grad_ref[...], ROWS_TN).astype(jnp.bfloat16)
-    for_each(step, lambda r: start_all(leave(r)[1]))
-
-    @pl.when(step == 3)
-    def _():
-        wait_all(leave(3)[0])
-        wait_all(leave(3)[1])
+    first = place[2] % 2
+
+    def spot(r):
+        start = pl.multiple_of(jnp.bitwise_xor(first, r % 2) * width, 128)
+        return pl.ds(start, width)
+
+    halves = ((0, 1), (2, 3))
+    loads = [
+        [pltpu.make_async_copy(inputs[0], mod_ref, in_sems.at[0])],
+        [pltpu.make_async_copy(inputs[2], grad_ref, in_sems.at[1])],
+        [],
+        [],
+        [pltpu.make_async_copy(inputs[1], across_ref, in_sems.at[4])],
+    ]
+    for index, pair in enumerate(halves):
+        for r in pair:
+            target = up_all.at[index, :, spot(r)]
+            loads[2 * index] += square_copies(place, up_sets, r, target, in_sems.at[2 * index])
+            target = down_all.at[index, spot(r)]
+            loads[2 * index + 1] += strip_copies(
+                place, down_refs, chunk_of(r), target, in_sems.at[2 * index + 1]
+            )
+    for index in (0, 1, 4, 2, 3):
+        start_all(loads[index])
+    rows = min(512, length)
+    columns = 768 if 2 * width % 768 == 0 else width
+    leaving = []
+    for index, pair in enumerate(halves):
+        up, down = up_all.at[index], down_all.at[index]
+        low_chunk = chunk_of(pair[0]) // 2 * 2
+
+        def row_pair(ref, at):
+            return jnp.concatenate([ref[pl.ds(at, 1)], ref[pl.ds(at + 1, 1)]], axis=1)
+
+        bias = row_pair(rows_ref, UP_BIAS + low_chunk)
+        keep = row_pair(keep_ref, low_chunk)
+        wait_all(loads[2 * index])
+        wait_all(loads[2 * index + 1])
+
+        def row_tile(number, total):
+            tile = pl.ds(pl.multiple_of(number * rows, rows), rows)
+            sums = []
+            for column in range(0, 2 * width, columns):
+                part = slice(column, column + columns)
+                gelu, slope = gelu_and_slope(
+                    matmul(mod_ref[tile], up[:, part], ROWS_NN) + bias[:, part]
+                )
+                act[tile, part] = (gelu * keep[:, part]).astype(jnp.bfloat16)
+                back = matmul(grad_ref[tile], down[part], ROWS_NT)
+                low = (slope * keep[:, part] * back).astype(jnp.bfloat16)
+                dpre[tile, part] = low
+                sums.append(jnp.sum(low.astype(jnp.float32), axis=0, keepdims=True))
+            branch = matmul(act[tile], down[...], ROWS_NN)
+            dmod = matmul(dpre[tile], up[...], ROWS_NT)
+            if index:
+                branch_ref[tile] += branch
+                dmod_ref[tile] += dmod
+            else:
+                branch_ref[tile] = branch
+                dmod_ref[tile] = dmod
+            return total + jnp.concatenate(sums, axis=1)
+
+        total = lax.fori_loop(0, length // rows, row_tile, jnp.zeros_like(bias))
+        dbias_ref[pl.ds(low_chunk, 1)] = total[:, :width]
+        dbias_ref[pl.ds(low_chunk + 1, 1)] = total[:, width:]
+        if index == 1:
+            copies = [
+                pltpu.make_async_copy(branch_ref, branch_out, sum_sem),
+                pltpu.make_async_copy(dmod_ref, dmod_out, sum_sem),
+            ]
+            start_all(copies)
+            leaving += copies
+        else:
+            wait_all(loads[4])
+
+        for r in pair:
+            up[:, spot(r)] = matmul(across_ref[...], dpre[:, spot(r)], ROWS_NN).astype(jnp.bfloat16)
+            copies = square_stores(place, up_stores, r, up.at[:, spot(r)], out_sem)
+            start_all(copies)
+            leaving += copies
+        for r in pair:
+            down[spot(r)] = matmul(act[:, spot(r)], grad_ref[...], ROWS_TN).astype(jnp.bfloat16)
+            copies = strip_stores(place, down_stores, chunk_of(r), down.at[spot(r)], out_sem)
+            start_all(copies)
+            leaving += copies
+    wait_all(leaving)
 
 
 def gradient_shapes(paired, rows, columns):
@@ -547,46 +589,39 @@
 def mlp(place, mod, across, grad, rows, keep, ups, downs, block_rows):
     length, width = mod.shape
     stores = gradient_shapes(len(downs) > 1, block_rows, [width])
-    quarter = jax.ShapeDtypeStruct((4, width), jnp.float32)
+    count = len(flat(ups)) + len(downs)
     table = pl.BlockSpec((4, width), lambda step, place: (0, 0))
-    held = pl.BlockSpec((length, width), lambda step, place: (0, 0), pipeline_mode=pl.Buffered(1))
-    square = pltpu.VMEM((width, width), jnp.bfloat16)
-    pair = pltpu.VMEM((2, width, width), jnp.bfloat16)
-    tall = pltpu.VMEM((length, width), jnp.bfloat16)
-    wide = pl.BlockSpec((length, width), lambda step, place: (0, 0))
     return pl.pallas_call(
         functools.partial(mlp_kernel, ups=ups, downs=len(downs)),
         grid_spec=pltpu.PrefetchScalarGridSpec(
             num_scalar_prefetch=1,
-            grid=(4,),
-            in_specs=[
-                held,
-                pl.BlockSpec((width, length), lambda step, place: (0, 0), pipeline_mode=pl.Buffered(1)),
-                held,
-                pl.BlockSpec(rows.shape, lambda step, place: (0, 0)),
-                table,
-            ]
-            + [ANY] * (len(flat(ups)) + len(downs)),
-            out_specs=[wide, wide, table] + [ANY] * (2 * len(stores)),
+            grid=(1,),
+            in_specs=[pl.BlockSpec(rows.shape, lambda step, place: (0, 0)), table]
+            + [ANY] * (3 + count),
+            out_specs=[ANY, ANY, table] + [ANY] * (2 * len(stores)),
             scratch_shapes=[
-                tall,
-                tall,
-                pair,
-                pair,
-                square,
-                square,
-                pltpu.SemaphoreType.DMA((2, 2)),
-                pltpu.SemaphoreType.DMA((2,)),
+                pltpu.VMEM((length, width), jnp.bfloat16),
+                pltpu.VMEM((width, length), jnp.bfloat16),
+                pltpu.VMEM((length, width), jnp.bfloat16),
+                pltpu.VMEM((length, width), jnp.float32),
+                pltpu.VMEM((length, width), jnp.float32),
+                pltpu.VMEM((length, 2 * width), jnp.bfloat16),
+                pltpu.VMEM((length, 2 * width), jnp.bfloat16),
+                pltpu.VMEM((2, width, 2 * width), jnp.bfloat16),
+                pltpu.VMEM((2, 2 * width, width), jnp.bfloat16),
+                pltpu.SemaphoreType.DMA((5,)),
+                pltpu.SemaphoreType.DMA,
+                pltpu.SemaphoreType.DMA,
             ],
         ),
         out_shape=[jax.ShapeDtypeStruct((length, width), jnp.float32)] * 2
-        + [quarter]
+        + [jax.ShapeDtypeStruct((4, width), jnp.float32)]
         + stores
         + stores,
-        compiler_params=vmem_params(60),
+        compiler_params=vmem_params(62),
         cost_estimate=cost(48 * length * width * width, 32 * width * width),
         name="mlp",
-    )(place, mod, across, grad, rows, keep, *flat(ups), *downs)
+    )(place, rows, keep, mod, across, grad, *flat(ups), *downs)
 
 
 def after_mlp_kernel(
@@ -732,22 +767,19 @@
 def tokens_back_kernel(place, grads_ref, tokens_ref, dmiddle_ref, rows_ref, *rest, sets):
     *refs, out_ref, sums_ref, dmod, held, sems = rest
     step = pl.program_id(0)
-    fetch_squares(place, in_sets(refs, sets), step, held, sems)
-    part = jnp.bitwise_xor(place[2], step)
+    fetch_squares(place, in_sets(refs, sets), step, 3, held, sems)
     length = tokens_ref.shape[0]
 
     @pl.when(step == 0)
     def _():
         dmod[...] = jnp.zeros_like(dmod)
 
-    @pl.when(part < 3)
-    def _():
-        for tile in tiles(length):
-            dmod[tile] += matmul(grads_ref[0, tile], held[step % 2], ROWS_NT)
-        total = jnp.sum(grads_ref[0].astype(jnp.float32), axis=0, keepdims=True)
-        sums_ref[pl.ds(2 + part, 1)] = total
-
-    @pl.when(step == 3)
+    for tile in tiles(length):
+        dmod[tile] += matmul(grads_ref[0, tile], held[step % 2], ROWS_NT)
+    total = jnp.sum(grads_ref[0].astype(jnp.float32), axis=0, keepdims=True)
+    sums_ref[pl.ds(2 + step, 1)] = total
+
+    @pl.when(step == 2)
     def _():
         shift = jnp.zeros((1, dmod.shape[1]), jnp.float32)
         scale = shift
@@ -769,11 +801,11 @@
         functools.partial(tokens_back_kernel, sets=squares),
         grid_spec=pltpu.PrefetchScalarGridSpec(
             num_scalar_prefetch=1,
-            grid=(4,),
+            grid=(3,),
             in_specs=[
                 pl.BlockSpec(
                     (1, length, width),
-                    lambda step, place: (jnp.minimum(jnp.bitwise_xor(place[2], step), 2), 0, 0),
+                    lambda step, place: (step, 0, 0),
                 ),
                 held,
                 held,
@@ -947,7 +979,6 @@
     if paired:
         near = net.pair(fact, "x")
         mine = lax.dynamic_slice_in_dim(four, member * width, width, axis=1)
-        mine, near = barrier((mine, near))
         near = net.along_z(near)
         square = net.along_z(mine)
         facts = jnp.where(place[1] == 0, near, near[:, ::-1])
@@ -979,8 +1010,7 @@
     if paired:
         square, sent, near = barrier((square, sent, near))
         parts = lax.all_to_all(sent, "fsdp", 0, 0, tiled=True)
-        all_facts = net.pair(net.pair(near.swapaxes(0, 1), "c").swapaxes(0, 1), "y")
-        all_facts = all_facts.reshape(image_count, 2)
+        all_facts = near.swapaxes(0, 1)
         first = net.pair(square[:, :, : splits[0]], "x")
         second = net.pair(square[:, :, splits[0] :], "y")
         mine = lax.dynamic_slice_in_dim(up_weight, member * width, width, axis=1)
@@ -993,7 +1023,6 @@
         first, second, first_y, second_x, up, prepared = barrier(
             (first, second, first_y, second_x, up, prepared)
         )
-        down = lax.all_gather(after(down_mine, first_y), "fsdp", axis=0)
         squares = [
             Blocks([first, first_y, net.partner(first, "c"), net.partner(first_y, "c")], "xy"),
             Blocks([second, second_x, net.partner(second, "c"), net.partner(second_x, "c")], "yx"),
@@ -1007,21 +1036,24 @@
     mod_one, mod_across, branch_grad, down_bias_g, rows = prepared
     if paired:
         up_x, up_y = net.partner(up, "x"), net.partner(up, "y")
+        down = lax.all_gather(after(down_mine, squares[0][3]), "fsdp", axis=0)
     qkv = project(place, mod_one, rows, squares)
     if paired:
         qkv, up_x, up_y, all_facts = barrier((qkv, up_x, up_y, all_facts))
         up = jnp.stack([up, up_x])
         up_xy, up_c = net.partner(up_x, "y"), net.partner(up, "c")
+        all_facts = net.pair(all_facts, "c").swapaxes(0, 1)
     attn_low, lse = attend_forward(qkv, head_keep[0])
     if paired:
-        attn_low, up, up_xy, up_c = barrier((attn_low, up, up_xy, up_c))
+        attn_low, up, up_xy, up_c, all_facts = barrier((attn_low, up, up_xy, up_c, all_facts))
+        all_facts = net.pair(all_facts, "y").reshape(image_count, 2)
         up_y = jnp.stack([up_y, up_xy])
         up_y_c = net.partner(up_y, "c")
     attn_branch, middle, mod_two, mod_two_across = after_attention(
         place, attn_low, tokens[0], rows, squares
     )
     if paired:
-        mod_two, down, up_y_c = barrier((mod_two, down, up_y_c))
+        mod_two, down, up_y_c, all_facts = barrier((mod_two, down, up_y_c, all_facts))
         ups = [Blocks([up, up_y, up_c, up_y_c], "xy")]
         downs = [down, net.partner(down, "c")]
     else:

time: 616 us -> 603 us (0.979)
  waiting for transfers between devices: 131 us -> 105 us
  starting transfers between devices: 69 us -> 87.3 us
  Pallas kernels: 300 us -> 288 us
    ppermute x21, waiting for transfers between devices: 67.5 us -> 49.8 us  [ahead(): return lax.ppermute(value, 'fsdp', pairs)]
    ppermute x21, starting transfers between devices: 29 us -> 41.2 us  [ahead(): return lax.ppermute(value, 'fsdp', pairs)]
    ppermute x34, waiting for transfers between devices: 46 us -> 36.7 us  [swap(): return lax.ppermute(value, axis, [(i, i ^ step) for i in range(size)])]
    pallas_call x1, Pallas kernels: 98.5 us -> 91.7 us  [mlp(): pl.pallas_call(functools.partial(mlp_kernel, ups=ups, downs=len(downs)),...]
    ppermute x34, starting transfers between devices: 32.7 us -> 39.3 us  [swap(): return lax.ppermute(value, axis, [(i, i ^ step) for i in range(size)])]
  transfers between devices with their start and end apart: 60 -> 60, of which waited for: 20 -> 16; matrix products, arithmetic and copies ran while one was open for 9% -> 9% of each run, Pallas kernels for 33% -> 33%
where the time goes in v5:
time: 603 us; the launch traced here: 598 us
  Pallas kernels  288 us (48%)
  waiting for transfers between devices  105 us (17%)
  starting transfers between devices  87.3 us (14%)
  other arithmetic  68.4 us (11%)
  local copies, waits for them, and re-layouts  24.4 us (4%)
  between operations  16.4 us (3%)
  matrix products  8.6 us (1%)
    pallas_call x1, Pallas kernels, mlp(): pl.pallas_call(functools.partial(mlp_kernel, ups=ups, downs=len(downs)),...  91.7 us
    pallas_call x1, Pallas kernels, attend_backward(): pl.pallas_call(functools.partial(attend_backward_kernel, head_size=width...  57.7 us
    ppermute x21, waiting for transfers between devices, ahead(): return lax.ppermute(value, 'fsdp', pairs)  49.8 us
    ppermute x21, starting transfers between devices, ahead(): return lax.ppermute(value, 'fsdp', pairs)  41.2 us
    ppermute x34, starting transfers between devices, swap(): return lax.ppermute(value, axis, [(i, i ^ step) for i in range(size)])  39.3 us
    pallas_call x1, Pallas kernels, attend_forward(): pl.pallas_call(functools.partial(attend_forward_kernel, head_size=width /...  37.1 us
    ppermute x34, waiting for transfers between devices, swap(): return lax.ppermute(value, axis, [(i, i ^ step) for i in range(size)])  36.7 us
    convert_element_type x12, other arithmetic, add(): sum((term.astype(jnp.float32) for term in terms)).astype(jnp.bfloat16)  32.4 us
  transfers between devices with their start and end apart: 60, of which 16 were waited for; matrix products, arithmetic and copies ran while one was open for 9% of the time, Pallas kernels for 33%

profile of v5, /device:TPU:1, one launch (start us, length us, event | category | flops | bytes accessed | tf_op | source)
XLA Modules:
  0.0 597.7 jit_solution(9621522232924325922)
XLA Ops:
  24.3 9.2 %collective-permute-done.4 = s32[2,2]{1,0:T(2,128)S(1)} collective-permute-done((s32[2,2]{1,0:T(2,128)S(1)}, s32[2,2]{1,0:T(2,128)S(1)}, u32[]{:S(2)}, u32[]{:S(2)}) %collective-permute-start.4) | collective-permute-done | bytes 48 | tf_op jit(solution)/shard_map/ppermute | solution.py:887
  33.5 6.9 %collective-permute-start.6 = (s32[2,2]{1,0:T(2,128)S(1)}, s32[2,2]{1,0:T(2,128)S(1)}, u32[]{:S(2)}, u32[]{:S(2)}) collective-permute-start(s32[2,2]{1,0:T(2,128)S(1)} %get-tuple-element.282), channel_id=1, source_target_pairs={{24,0},{28,4},{0,8},{4,12},{8,16},{12,20},{16,24},{20,28},{25,1},{... | collective-permute-start | bytes 56 | tf_op jit(solution)/shard_map/ppermute | solution.py:887
  69.9 4.5 collective-permute-start.11
  75.7 6.7 %prepare.1 = (bf16[1024,1152]{1,0:T(8,128)(2,1)}, bf16[1152,1024]{1,0:T(8,128)(2,1)}, bf16[1024,1152]{1,0:T(8,128)(2,1)}, f32[8,1152]{1,0:T(8,128)}, f32[16,1152]{1,0:T(8,128)}) custom-call(bf16[1024,1152]{1,0:T(8,128)(2,1)} %bitcast.223, bf16[1024,1152]{1,0:T(8,128)(2,1)} %bitcast.220, f32[8,16128]{1,0:T(8,128)} %bitcast.232), custom_call_target="tpu_custom_call" | custom-call | flops 1 | bytes 1 | tf_op jit(solution)/shard_map/prepare/pallas_call | solution.py:338
  82.4 16.4 %collective-permute-done.12 = bf16[144,1152]{1,0:T(8,128)(2,1)S(1)} collective-permute-done((bf16[144,1152]{1,0:T(8,128)(2,1)}, bf16[144,1152]{1,0:T(8,128)(2,1)S(1)}, u32[]{:S(2)}, u32[]{:S(2)}) %collective-permute-start.12) | collective-permute-done | bytes 331808 | tf_op jit(solution)/shard_map/ppermute | solution.py:887
  101.6 5.6 collective-permute-start.15
  119.8 16.2 %project.1.query_ref.key_ref.value_ref = bf16[3,1024,1152]{2,1,0:T(8,128)(2,1)} custom-call(s32[3]{0:T(128)} %pad_add_fusion.3.place, bf16[1024,1152]{1,0:T(8,128)(2,1)} %get-tuple-element.139.mod_ref, f32[16,1152]{1,0:T(8,128)} %get-tuple-element.140.rows_ref, bf16[2,4,144,512]{3,2,1,0:T(8,128)(2,1)} %pad_maximum_fusion.9.rest_0_, ...), custom_call_target="tpu_custom_call" | custom-call | flops 1 | bytes 1 | tf_op jit(solution)/shard_map/project/pallas_call | solution.py:384
  136.0 12.1 %collective-permute-done.18 = bf16[4,144,1152]{2,1,0:T(8,128)(2,1)} collective-permute-done((bf16[4,144,1152]{2,1,0:T(8,128)(2,1)}, bf16[4,144,1152]{2,1,0:T(8,128)(2,1)}, u32[]{:S(2)}, u32[]{:S(2)}) %collective-permute-start.18) | collective-permute-done | bytes 1327136 | tf_op jit(solution)/shard_map/ppermute | solution.py:847
  154.4 37.1 %attend_forward.1 = (bf16[1024,1152]{1,0:T(8,128)(2,1)S(1)}, f32[16,1024]{1,0:T(8,128)S(1)}) custom-call(s32[16]{0:T(128)S(1)} %bitcast.219, bf16[3,1024,1152]{2,1,0:T(8,128)(2,1)} %project.1.query_ref.key_ref.value_ref, bf16[3,1024,1152]{2,1,0:T(8,128)(2,1)} %project.1.query_ref.key_ref.value_ref, bf16[3,1024,1152]{2,1,0:T(8,128)(2,1)} %project.1.query_ref.key_ref.value_ref), custom_call_target="tpu_custom_call" | custom-call | flops 17179869184 | bytes 9437184 | tf_op jit(solution)/shard_map/attend_forward/pallas_call | solution.py:133
  197.3 11.7 %after_attention.1 = (f32[1024,1152]{1,0:T(8,128)}, f32[1024,1152]{1,0:T(8,128)}, bf16[1024,1152]{1,0:T(8,128)(2,1)}, bf16[1152,1024]{1,0:T(8,128)(2,1)}) custom-call(s32[3]{0:T(128)} %pad_add_fusion.3.place, bf16[1024,1152]{1,0:T(8,128)(2,1)} %copy-done.1, bf16[1024,1152]{1,0:T(8,128)(2,1)} %bitcast.224, f32[16,1152]{1,0:T(8,128)} %get-tuple-element.140.rows_ref, ...), custom_call_target="tpu_custom_call" | custom-call | flops 1 | bytes 1 | tf_op jit(solution)/shard_map/after_attention/pallas_call | solution.py:444
  210.5 8.0 %collective-permute-done.25.rest_8_ = bf16[8,2,144,1152]{3,2,1,0:T(8,128)(2,1)} collective-permute-done((bf16[8,2,144,1152]{3,2,1,0:T(8,128)(2,1)}, bf16[8,2,144,1152]{3,2,1,0:T(8,128)(2,1)}, u32[]{:S(2)}, u32[]{:S(2)}) %collective-permute-start.25) | collective-permute-done | bytes 5308448 | tf_op jit(solution)/shard_map/ppermute | solution.py:847
  218.5 91.7 %mlp.1 = (f32[1024,1152]{1,0:T(8,128)}, f32[1024,1152]{1,0:T(8,128)}, f32[4,1152]{1,0:T(4,128)}, bf16[2,2,4,144,1152]{4,3,2,1,0:T(8,128)(2,1)}, bf16[2,2,4,144,1...) custom-call(s32[3]{0:T(128)} %pad_add_fusion.3.place, ...), custom_call_target="tpu_custom_call" | custom-call | flops 1 | bytes 1 | tf_op jit(solution)/shard_map/mlp/pallas_call | solution.py:594
  310.8 14.2 %after_mlp.1 = (f32[1024,1152]{1,0:T(8,128)}, bf16[1024,1152]{1,0:T(8,128)(2,1)}, bf16[1024,1152]{1,0:T(8,128)(2,1)}, f32[8,1152]{1,0:T(8,128)}) custom-call(s32[3]{0:T(128)} %pad_add_fusion.3.place, f32[1024,1152]{1,0:T(8,128)} %get-tuple-element.165.dmod_ref, f32[1024,1152]{1,0:T(8,128)} %get-tuple-element.166.middle_ref, bf16[1024,1152]{1,0:T(8,128)(2,1)} %bitcast.221, ...), custom_call_target="tpu_custom_call" | custom-call | flops 1 | bytes 1 | tf_op jit(solution)/shard_map/after_mlp/pallas_call | solution.py:656
  336.4 57.7 %attend_backward.1.grads_ref = bf16[3,1024,1152]{2,1,0:T(8,128)(2,1)} custom-call(s32[16]{0:T(128)} %bitcast.218, bf16[3,1024,1152]{2,1,0:T(8,128)(2,1)} %project.1.query_ref.key_ref.value_ref, bf16[3,1024,1152]{2,1,0:T(8,128)(2,1)} %project.1.query_ref.key_ref.value_ref, bf16[3,1024,1152]{2,1,0:T(8,128)(2,1)} %project.1.query_ref.key_ref.value_ref, ...), custom_call_target="tpu_custom_call" | custom-call | flops 42949672960 | bytes 18874368 | tf_op jit(solution)/shard_map/attend_backward/pallas_call | solution.py:160
  394.3 5.4 fusion.4
  402.0 9.4 %finish.1 = (bf16[1024,1152]{1,0:T(8,128)(2,1)}, f32[8,1152]{1,0:T(8,128)}) custom-call(f32[1024,1152]{1,0:T(8,128)} %get-tuple-element.190.mlp_ref, f32[1024,1152]{1,0:T(8,128)} %get-tuple-element.166.middle_ref, f32[1024,1152]{1,0:T(8,128)} %get-tuple-element.191.branch_ref, f32[1024,1152]{1,0:T(8,128)} %get-tuple-element.192.dmiddle_ref, ...), custom_call_target="tpu_custom_call" | custom-call | flops 1 | bytes 1 | tf_op jit(solution)/shard_map/finish/pallas_call | solution.py:695
  411.5 19.4 %square_grads.1 = (bf16[2,2,4,144,512]{4,3,2,1,0:T(8,128)(2,1)}, bf16[2,2,4,144,512]{4,3,2,1,0:T(8,128)(2,1)}, bf16[2,2,4,144,640]{4,3,2,1,0:T(8,128)(2,1)}, bf16[2,2,4,144,640]{4,3,2,1,0:T(8,128)(2,1)}) custom-call(s32[3]{0:T(128)} %pad_add_fusion.3.place, bf16[1152,1024]{1,0:T(8,128)(2,1)} %get-tuple-element.138.across_ref, ...), custom_call_target="tpu_custom_call" | custom-call | flops 1 | bytes 1 | tf_op jit(solution)/shard_map/square_grads/pallas_call | solution.py:740
  437.0 4.8 collective-permute-done.32
  458.0 23.9 %tokens_back.1 = (bf16[1024,1152]{1,0:T(8,128)(2,1)}, f32[8,1152]{1,0:T(8,128)}) custom-call(s32[3]{0:T(128)} %pad_add_fusion.3.place, bf16[3,1024,1152]{2,1,0:T(8,128)(2,1)} %attend_backward.1.grads_ref, bf16[1024,1152]{1,0:T(8,128)(2,1)} %bitcast.225, f32[1024,1152]{1,0:T(8,128)} %get-tuple-element.192.dmiddle_ref, ...), custom_call_target="tpu_custom_call" | custom-call | flops 1 | bytes 1 | tf_op jit(solution)/shard_map/tokens_back/pallas_call | solution.py:800
  496.9 4.2 collective-permute-done.41
  501.1 16.1 %collective-permute-done.42 = bf16[144,1152]{1,0:T(8,128)(2,1)S(1)} collective-permute-done((bf16[144,1152]{1,0:T(8,128)(2,1)S(1)}, bf16[144,1152]{1,0:T(8,128)(2,1)S(1)}, u32[]{:S(2)}, u32[]{:S(2)}) %collective-permute-start.42) | collective-permute-done | bytes 331808 | tf_op jit(solution)/shard_map/ppermute | solution.py:887
  521.0 5.9 collective-permute-start.50
  537.4 16.7 %collective-permute-done.52 = bf16[2,4,1,16128]{3,1,0,2:T(4,128)(2,1)S(1)} collective-permute-done((bf16[2,4,1,16128]{3,1,0,2:T(4,128)(2,1)S(1)}, bf16[2,4,1,16128]{3,1,0,2:T(4,128)(2,1)S(1)}, u32[]{:S(2)}, u32[]{:S(2)}) %collective-permute-start.52) | collective-permute-done | bytes 258080 | tf_op jit(solution)/shard_map/ppermute | solution.py:880
  554.1 4.2 collective-permute-start.49
  (295 shorter events, 173.1 us)
Async XLA Ops:
  8.5 35.7 %collective-permute-start = (bf16[144,1152]{1,0:T(8,128)(2,1)S(1)}, bf16[144,1152]{1,0:T(8,128)(2,1)S(1)}, u32[]{:S(2)}, u32[]{:S(2)}) collective-permute-start(bf16[144,1152]{1,0:T(8,128)(2,1)S(1)} %fusion.28), channel_id=1, source_target_pairs={{8,0},{12,4},{16,8},{20,12},{24,16},{28,20},{0,24},{4,28},{9,1},{1... | collective-permute-start | bytes 995336 | tf_op jit(solution)/shard_map/ppermute | solution.py:887
  12.7 31.5 %collective-permute-start.1 = (bf16[144,1152]{1,0:T(8,128)(2,1)S(1)}, bf16[144,1152]{1,0:T(8,128)(2,1)S(1)}, u32[]{:S(2)}, u32[]{:S(2)}) collective-permute-start(bf16[144,1152]{1,0:T(8,128)(2,1)S(1)} %fusion.28), channel_id=1, source_target_pairs={{16,0},{20,4},{24,8},{28,12},{0,16},{4,20},{8,24},{12,28},{17,1},{... | collective-permute-start | bytes 995336 | tf_op jit(solution)/shard_map/ppermute | solution.py:887
  12.7 31.5 %collective-permute-start.2 = (bf16[144,1152]{1,0:T(8,128)(2,1)S(1)}, bf16[144,1152]{1,0:T(8,128)(2,1)S(1)}, u32[]{:S(2)}, u32[]{:S(2)}) collective-permute-start(bf16[144,1152]{1,0:T(8,128)(2,1)S(1)} %fusion.28), channel_id=1, source_target_pairs={{24,0},{28,4},{0,8},{4,12},{8,16},{12,20},{16,24},{20,28},{25,1},{... | collective-permute-start | bytes 995336 | tf_op jit(solution)/shard_map/ppermute | solution.py:887
  54.0 155.1 %all-gather.3.cloned.1.call-start = ((), (), s32[]{:S(2)}) async-start(), calls=%async_computation.1 | async-start | bytes 5971968 | tf_op jit(solution)/shard_map/all_gather | solution.py:1039
  67.1 33.0 %collective-permute-start.10 = (bf16[2,4,144,640]{3,2,1,0:T(8,128)(2,1)S(1)}, bf16[2,4,144,640]{3,2,1,0:T(8,128)(2,1)S(1)}, u32[]{:S(2)}, u32[]{:S(2)}) collective-permute-start(bf16[2,4,144,640]{3,2,1,0:T(8,128)(2,1)S(1)} %pad_maximum_fusion.4.rest_4_), channel_id=1, source_target_pairs={{0,4},{4,0},{8,12},{12,8},{16,20},{20,16},{24,28},{28,24},{1,5},{5... | collective-permute-start | bytes 4423688 | tf_op jit(solution)/shard_map/ppermute | solution.py:847
  69.7 30.4 %collective-permute-start.9 = (bf16[2,4,144,512]{3,2,1,0:T(8,128)(2,1)}, bf16[2,4,144,512]{3,2,1,0:T(8,128)(2,1)S(1)}, u32[]{:S(2)}, u32[]{:S(2)}) collective-permute-start(bf16[2,4,144,512]{3,2,1,0:T(8,128)(2,1)} %pad_maximum_fusion.9.rest_0_), channel_id=1, source_target_pairs={{0,2},{1,3},{2,0},{3,1},{4,6},{5,7},{6,4},{7,5},{8,10},{9,11},{10,... | collective-permute-start | bytes 3538952 | tf_op jit(solution)/shard_map/ppermute | solution.py:847
  110.4 37.8 %collective-permute-start.18 = (bf16[4,144,1152]{2,1,0:T(8,128)(2,1)}, bf16[4,144,1152]{2,1,0:T(8,128)(2,1)}, u32[]{:S(2)}, u32[]{:S(2)}) collective-permute-start(bf16[4,144,1152]{2,1,0:T(8,128)(2,1)} %pad_maximum_fusion.6), channel_id=1, source_target_pairs={{0,4},{4,0},{8,12},{12,8},{16,20},{20,16},{24,28},{28,24},{1,5},{5... | collective-permute-start | bytes 3981320 | tf_op jit(solution)/shard_map/ppermute | solution.py:847
  110.4 37.7 %collective-permute-start.19 = (bf16[4,144,1152]{2,1,0:T(8,128)(2,1)}, bf16[4,144,1152]{2,1,0:T(8,128)(2,1)}, u32[]{:S(2)}, u32[]{:S(2)}) collective-permute-start(bf16[4,144,1152]{2,1,0:T(8,128)(2,1)} %pad_maximum_fusion.6), channel_id=1, source_target_pairs={{0,2},{1,3},{2,0},{3,1},{4,6},{5,7},{6,4},{7,5},{8,10},{9,11},{10,... | collective-permute-start | bytes 3981320 | tf_op jit(solution)/shard_map/ppermute | solution.py:847
  151.6 42.1 %collective-permute-start.21 = (bf16[2,4,144,1152]{3,2,1,0:T(8,128)(2,1)}, bf16[2,4,144,1152]{3,2,1,0:T(8,128)(2,1)}, u32[]{:S(2)}, u32[]{:S(2)}) collective-permute-start(bf16[2,4,144,1152]{3,2,1,0:T(8,128)(2,1)} %pad_maximum_fusion.rest_3_), channel_id=1, source_target_pairs={{0,1},{1,0},{2,3},{3,2},{4,5},{5,4},{6,7},{7,6},{8,9},{9,8},{10,11... | collective-permute-start | bytes 7962632 | tf_op jit(solution)/shard_map/ppermute | solution.py:847
  152.8 40.9 %collective-permute-start.20 = (bf16[4,144,1152]{2,1,0:T(8,128)(2,1)}, bf16[4,144,1152]{2,1,0:T(8,128)(2,1)S(1)}, u32[]{:S(2)}, u32[]{:S(2)}) collective-permute-start(bf16[4,144,1152]{2,1,0:T(8,128)(2,1)} %collective-permute-done.18), channel_id=1, source_target_pairs={{0,2},{1,3},{2,0},{3,1},{4,6},{5,7},{6,4},{7,5},{8,10},{9,11},{10,... | collective-permute-start | bytes 3981320 | tf_op jit(solution)/shard_map/ppermute | solution.py:847
  154.1 39.6 %collective-permute-start.22 = (s32[2,4,2]{2,0,1:T(2,128)S(1)}, s32[2,4,2]{2,0,1:T(2,128)S(1)}, u32[]{:S(2)}, u32[]{:S(2)}) collective-permute-start(s32[2,4,2]{2,0,1:T(2,128)S(1)} %bitcast.253), channel_id=1, source_target_pairs={{0,1},{1,0},{2,3},{3,2},{4,5},{5,4},{6,7},{7,6},{8,9},{9,8},{10,11... | collective-permute-start | bytes 200 | tf_op jit(solution)/shard_map/ppermute | solution.py:847
  335.2 59.1 %collective-permute-start.28 = (bf16[2,4,144,1152]{3,2,1,0:T(8,128)(2,1)}, bf16[2,4,144,1152]{3,2,1,0:T(8,128)(2,1)}, u32[]{:S(2)}, u32[]{:S(2)}) collective-permute-start(bf16[2,4,144,1152]{3,2,1,0:T(8,128)(2,1)} %fusion), channel_id=1, source_target_pairs={{0,4},{4,0},{8,12},{12,8},{16,20},{20,16},{24,28},{28,24},{1,5},{5... | collective-permute-start | bytes 7962632 | tf_op jit(solution)/shard_map/ppermute | solution.py:847
  335.4 58.9 %collective-permute-start.29 = (bf16[2,4,144,1152]{3,2,1,0:T(8,128)(2,1)}, bf16[2,4,144,1152]{3,2,1,0:T(8,128)(2,1)}, u32[]{:S(2)}, u32[]{:S(2)}) collective-permute-start(bf16[2,4,144,1152]{3,2,1,0:T(8,128)(2,1)} %fusion.1), channel_id=1, source_target_pairs={{0,2},{1,3},{2,0},{3,1},{4,6},{5,7},{6,4},{7,5},{8,10},{9,11},{10,... | collective-permute-start | bytes 7962632 | tf_op jit(solution)/shard_map/ppermute | solution.py:847
  399.7 31.2 %collective-permute-start.30 = (bf16[4,144,1152]{2,1,0:T(8,128)(2,1)}, bf16[4,144,1152]{2,1,0:T(8,128)(2,1)}, u32[]{:S(2)}, u32[]{:S(2)}) collective-permute-start(bf16[4,144,1152]{2,1,0:T(8,128)(2,1)} %get-tuple-element.188), channel_id=1, source_target_pairs={{0,2},{1,3},{2,0},{3,1},{4,6},{5,7},{6,4},{7,5},{8,10},{9,11},{10,... | collective-permute-start | bytes 3981320 | tf_op jit(solution)/shard_map/ppermute | solution.py:847
  400.9 30.0 %collective-permute-start.31 = (bf16[4,144,1152]{2,1,0:T(8,128)(2,1)}, bf16[4,144,1152]{2,1,0:T(8,128)(2,1)}, u32[]{:S(2)}, u32[]{:S(2)}) collective-permute-start(bf16[4,144,1152]{2,1,0:T(8,128)(2,1)} %get-tuple-element.189), channel_id=1, source_target_pairs={{0,4},{4,0},{8,12},{12,8},{16,20},{20,16},{24,28},{28,24},{1,5},{5... | collective-permute-start | bytes 3981320 | tf_op jit(solution)/shard_map/ppermute | solution.py:847
  447.3 34.7 %collective-permute-start.35 = (bf16[2,4,144,640]{3,2,1,0:T(8,128)(2,1)}, bf16[2,4,144,640]{3,2,1,0:T(8,128)(2,1)}, u32[]{:S(2)}, u32[]{:S(2)}) collective-permute-start(bf16[2,4,144,640]{3,2,1,0:T(8,128)(2,1)} %fusion.6), channel_id=1, source_target_pairs={{0,4},{4,0},{8,12},{12,8},{16,20},{20,16},{24,28},{28,24},{1,5},{5... | collective-permute-start | bytes 4423688 | tf_op jit(solution)/shard_map/ppermute | solution.py:847
  448.3 33.8 %collective-permute-start.34 = (bf16[2,4,144,512]{3,2,1,0:T(8,128)(2,1)}, bf16[2,4,144,512]{3,2,1,0:T(8,128)(2,1)}, u32[]{:S(2)}, u32[]{:S(2)}) collective-permute-start(bf16[2,4,144,512]{3,2,1,0:T(8,128)(2,1)} %fusion.9), channel_id=1, source_target_pairs={{0,2},{1,3},{2,0},{3,1},{4,6},{5,7},{6,4},{7,5},{8,10},{9,11},{10,... | collective-permute-start | bytes 3538952 | tf_op jit(solution)/shard_map/ppermute | solution.py:847
  449.6 32.3 %collective-permute-start.36 = (bf16[144,1152]{1,0:T(8,128)(2,1)}, bf16[144,1152]{1,0:T(8,128)(2,1)S(1)}, u32[]{:S(2)}, u32[]{:S(2)}) collective-permute-start(bf16[144,1152]{1,0:T(8,128)(2,1)} %get-tuple-element.263), channel_id=1, source_target_pairs={{24,0},{28,4},{0,8},{4,12},{8,16},{12,20},{16,24},{20,28},{25,1},{... | collective-permute-start | bytes 995336 | tf_op jit(solution)/shard_map/ppermute | solution.py:887
  450.6 31.3 %collective-permute-start.37 = (bf16[144,1152]{1,0:T(8,128)(2,1)}, bf16[144,1152]{1,0:T(8,128)(2,1)S(1)}, u32[]{:S(2)}, u32[]{:S(2)}) collective-permute-start(bf16[144,1152]{1,0:T(8,128)(2,1)} %get-tuple-element.262), channel_id=1, source_target_pairs={{16,0},{20,4},{24,8},{28,12},{0,16},{4,20},{8,24},{12,28},{17,1},{... | collective-permute-start | bytes 995336 | tf_op jit(solution)/shard_map/ppermute | solution.py:887
  452.4 29.5 %collective-permute-start.38 = (bf16[144,1152]{1,0:T(8,128)(2,1)}, bf16[144,1152]{1,0:T(8,128)(2,1)}, u32[]{:S(2)}, u32[]{:S(2)}) collective-permute-start(bf16[144,1152]{1,0:T(8,128)(2,1)} %get-tuple-element.261), channel_id=1, source_target_pairs={{8,0},{12,4},{16,8},{20,12},{24,16},{28,20},{0,24},{4,28},{9,1},{1... | collective-permute-start | bytes 995336 | tf_op jit(solution)/shard_map/ppermute | solution.py:887
  491.2 26.1 %collective-permute-start.42 = (bf16[144,1152]{1,0:T(8,128)(2,1)S(1)}, bf16[144,1152]{1,0:T(8,128)(2,1)S(1)}, u32[]{:S(2)}, u32[]{:S(2)}) collective-permute-start(bf16[144,1152]{1,0:T(8,128)(2,1)S(1)} %get-tuple-element.259), channel_id=1, source_target_pairs={{16,0},{20,4},{24,8},{28,12},{0,16},{4,20},{8,24},{12,28},{17,1},{... | collective-permute-start | bytes 995336 | tf_op jit(solution)/shard_map/ppermute | solution.py:887
  527.2 32.3 %collective-permute-start.54 = (bf16[2,144,1152]{2,1,0:T(8,128)(2,1)S(1)}, bf16[2,144,1152]{2,1,0:T(8,128)(2,1)S(1)}, u32[]{:S(2)}, u32[]{:S(2)}) collective-permute-start(bf16[2,144,1152]{2,1,0:T(8,128)(2,1)S(1)} %pad_maximum_fusion.11), channel_id=1, source_target_pairs={{0,2},{1,3},{2,0},{3,1},{4,6},{5,7},{6,4},{7,5},{8,10},{9,11},{10,... | collective-permute-start | bytes 1990664 | tf_op jit(solution)/shard_map/ppermute | solution.py:847
  529.4 31.4 %collective-permute-start.47 = (bf16[144,1152]{1,0:T(8,128)(2,1)S(1)}, bf16[144,1152]{1,0:T(8,128)(2,1)S(1)}, u32[]{:S(2)}, u32[]{:S(2)}) collective-permute-start(bf16[144,1152]{1,0:T(8,128)(2,1)S(1)} %get-tuple-element.257), channel_id=1, source_target_pairs={{24,0},{28,4},{0,8},{4,12},{8,16},{12,20},{16,24},{20,28},{25,1},{... | collective-permute-start | bytes 995336 | tf_op jit(solution)/shard_map/ppermute | solution.py:887
  532.0 28.8 %collective-permute-start.48 = (bf16[144,1152]{1,0:T(8,128)(2,1)S(1)}, bf16[144,1152]{1,0:T(8,128)(2,1)S(1)}, u32[]{:S(2)}, u32[]{:S(2)}) collective-permute-start(bf16[144,1152]{1,0:T(8,128)(2,1)S(1)} %get-tuple-element.256), channel_id=1, source_target_pairs={{16,0},{20,4},{24,8},{28,12},{0,16},{4,20},{8,24},{12,28},{17,1},{... | collective-permute-start | bytes 995336 | tf_op jit(solution)/shard_map/ppermute | solution.py:887
  (64 other events, 731.9 us)
Sparse Core Ops, SparseCore 0:
  109.9 89.1 all-gather.2

commit v6 on v5

--- a/solution.py
+++ b/solution.py
@@ -44,28 +44,37 @@
 
 
 def attend_forward_kernel(
-    keep_ref, query_ref, key_ref, value_ref, out_ref, lse_ref, *, head_size, width, rows
+    keep_ref, query_ref, key_ref, value_ref, out_ref, lse_ref, *, head_size, width, rows, together
 ):
     query_ref, key_ref, value_ref = query_ref.at[0], key_ref.at[0], value_ref.at[0]
-    head = pl.program_id(0)
-    base, mask = head_window(head, head_size, width)
     scale = head_size**-0.5 * LOG2E
     zero = jnp.zeros((), jnp.bfloat16)
-    window = (slice(None), pl.ds(base, 256))
-    keys = key_ref[window]
-    values = value_ref[window]
-    keep = keep_ref[head].astype(jnp.float32)
-    for start in range(0, query_ref.shape[0], rows):
+    length = query_ref.shape[0]
+    units = []
+    for index in range(together):
+        head = pl.program_id(0) * together + index
+        base, mask = head_window(head, head_size, width)
+        window = (slice(None), pl.ds(base, 256))
+        units += [(head, base, mask, window, start) for start in range(0, length, rows)]
+
+    def score(unit):
+        head, base, mask, window, start = unit
+        query = jnp.where(mask, query_ref[pl.ds(start, rows), pl.ds(base, 256)], zero)
+        return matmul(query, key_ref[window], ROWS_NT)
+
+    scores = score(units[0])
+    for number, unit in enumerate(units):
+        later = score(units[number + 1]) if number + 1 < len(units) else None
+        head, base, mask, window, start = unit
         block = (pl.ds(start, rows), pl.ds(base, 256))
-        query = jnp.where(mask, query_ref[block], zero)
-        scores = matmul(query, keys, ROWS_NT)
         top = jnp.max(scores, axis=-1, keepdims=True)
         probs = jnp.exp2((scores - top) * scale)
         total = jnp.sum(probs, axis=-1, keepdims=True)
-        mixed = matmul(probs.astype(jnp.bfloat16), values, ROWS_NN)
-        mixed = (mixed * (keep / total)).astype(jnp.bfloat16)
+        mixed = matmul(probs.astype(jnp.bfloat16), value_ref[window], ROWS_NN)
+        mixed = (mixed * (keep_ref[head].astype(jnp.float32) / total)).astype(jnp.bfloat16)
         out_ref[block] = jnp.where(mask, mixed, out_ref[block])
         lse_ref[pl.ds(head, 1), pl.ds(start, rows)] = as_row(top * scale + jnp.log2(total))
+        scores = later
 
 
 def attend_backward_kernel(
@@ -81,39 +90,56 @@
     head_size,
     width,
     rows,
+    together,
 ):
     query_ref, key_ref, value_ref = query_ref.at[0], key_ref.at[0], value_ref.at[0]
     dquery_ref, dkey_ref, dvalue_ref = grads_ref.at[0], grads_ref.at[1], grads_ref.at[2]
-    head = pl.program_id(0)
-    base, mask = head_window(head, head_size, width)
     scale = head_size**-0.5
     zero = jnp.zeros((), jnp.bfloat16)
     length = query_ref.shape[0]
-    window = (slice(None), pl.ds(base, 256))
-    keys = key_ref[window]
-    values = value_ref[window]
-    keys_across = jnp.transpose(keys)
-    key_grad = jnp.zeros((length, 256), jnp.float32)
-    value_grad = jnp.zeros((length, 256), jnp.float32)
-    kept = mask & (keep_ref[head] > 0)
-    for start in range(0, length, rows):
+    units = []
+    for index in range(together):
+        head = pl.program_id(0) * together + index
+        base, mask = head_window(head, head_size, width)
+        window = (slice(None), pl.ds(base, 256))
+        units += [(head, base, mask, window, start) for start in range(0, length, rows)]
+
+    def products(unit):
+        head, base, mask, window, start = unit
         block = (pl.ds(start, rows), pl.ds(base, 256))
         query = jnp.where(mask, query_ref[block], zero)
-        grad = jnp.where(kept, grad_ref[block], zero)
+        grad = jnp.where(mask & (keep_ref[head] > 0), grad_ref[block], zero)
+        scores = matmul(key_ref[window], query, ROWS_NT)
+        return query, grad, scores, matmul(value_ref[window], grad, ROWS_NT)
+
+    ready = products(units[0])
+    for number, unit in enumerate(units):
+        later = products(units[number + 1]) if number + 1 < len(units) else None
+        head, base, mask, window, start = unit
+        query, grad, scores, prob_grad = ready
+        block = (pl.ds(start, rows), pl.ds(base, 256))
+        if start == 0:
+            keys_across = jnp.transpose(key_ref[window])
+            key_grad = jnp.zeros((length, 256), jnp.float32)
+            value_grad = jnp.zeros((length, 256), jnp.float32)
         row_dot = as_row(
             jnp.sum(
                 grad.astype(jnp.float32) * out_ref[block].astype(jnp.float32), axis=-1, keepdims=True
             )
         )
         lse = lse_ref[pl.ds(head, 1), pl.ds(start, rows)]
-        probs = jnp.exp2(matmul(keys, query, ROWS_NT) * (scale * LOG2E) - lse)
-        score_grad = (probs * (matmul(values, grad, ROWS_NT) - row_dot)).astype(jnp.bfloat16)
+        probs = jnp.exp2(scores * (scale * LOG2E) - lse)
+        score_grad = (probs * (prob_grad - row_dot)).astype(jnp.bfloat16)
         value_grad = value_grad + matmul(probs.astype(jnp.bfloat16), grad, ROWS_NN)
         key_grad = key_grad + matmul(score_grad, query, ROWS_NN)
         query_grad = jnp.transpose(matmul(keys_across, score_grad, ROWS_NN)) * scale
         dquery_ref[block] = jnp.where(mask, query_grad.astype(jnp.bfloat16), dquery_ref[block])
-    dkey_ref[window] = jnp.where(mask, (key_grad * scale).astype(jnp.bfloat16), dkey_ref[window])
-    dvalue_ref[window] = jnp.where(mask, value_grad.astype(jnp.bfloat16), dvalue_ref[window])
+        if start + rows == length:
+            dkey_ref[window] = jnp.where(
+                mask, (key_grad * scale).astype(jnp.bfloat16), dkey_ref[window]
+            )
+            dvalue_ref[window] = jnp.where(mask, value_grad.astype(jnp.bfloat16), dvalue_ref[window])
+        ready = later
 
 
 def whole(shape):
@@ -126,15 +152,19 @@
     )
 
 
-def attend_forward(qkv, keep, rows=512):
+def attend_forward(qkv, keep, rows=512, together=2):
     _, length, width = qkv.shape
     heads = keep.shape[0]
     cells = heads * length * length
     return pl.pallas_call(
         functools.partial(
-            attend_forward_kernel, head_size=width // heads, width=width, rows=min(rows, length)
+            attend_forward_kernel,
+            head_size=width // heads,
+            width=width,
+            rows=min(rows, length),
+            together=together,
         ),
-        grid=(heads,),
+        grid=(heads // together,),
         in_specs=[pl.BlockSpec(memory_space=pltpu.SMEM)]
         + [one_of(i, length, width) for i in range(3)],
         out_specs=[
@@ -153,15 +183,19 @@
     )(keep, qkv, qkv, qkv)
 
 
-def attend_backward(qkv, out, grad, lse, keep, rows=256):
+def attend_backward(qkv, out, grad, lse, keep, rows=256, together=2):
     _, length, width = qkv.shape
     heads = keep.shape[0]
     cells = heads * length * length
     return pl.pallas_call(
         functools.partial(
-            attend_backward_kernel, head_size=width // heads, width=width, rows=min(rows, length)
+            attend_backward_kernel,
+            head_size=width // heads,
+            width=width,
+            rows=min(rows, length),
+            together=together,
         ),
-        grid=(heads,),
+        grid=(heads // together,),
         in_specs=[pl.BlockSpec(memory_space=pltpu.SMEM)]
         + [one_of(i, length, width) for i in range(3)]
         + [whole((length, width))] * 2

time: 603 us -> 596 us (0.988)
  Pallas kernels: 288 us -> 280 us
    pallas_call x1, Pallas kernels: 37.1 us -> 29.6 us  [attend_forward(): pl.pallas_call(functools.partial(attend_forward_kernel, head_size=width /...]
  transfers between devices with their start and end apart: 60 -> 60, of which waited for: 16 -> 16; matrix products, arithmetic and copies ran while one was open for 9% -> 9% of each run, Pallas kernels for 33% -> 32%
where the time goes in v6:
time: 596 us; the launch traced here: 590 us
  Pallas kernels  280 us (47%)
  waiting for transfers between devices  105 us (18%)
  starting transfers between devices  87.6 us (15%)
  other arithmetic  68.4 us (11%)
  local copies, waits for them, and re-layouts  24.5 us (4%)
  between operations  16.3 us (3%)
  matrix products  8.6 us (1%)
    pallas_call x1, Pallas kernels, mlp(): pl.pallas_call(functools.partial(mlp_kernel, ups=ups, downs=len(downs)),...  92 us
    pallas_call x1, Pallas kernels, attend_backward(): pl.pallas_call(functools.partial(attend_backward_kernel, head_size=width...  56.7 us
    ppermute x21, waiting for transfers between devices, ahead(): return lax.ppermute(value, 'fsdp', pairs)  49.3 us
    ppermute x21, starting transfers between devices, ahead(): return lax.ppermute(value, 'fsdp', pairs)  41.6 us
    ppermute x34, starting transfers between devices, swap(): return lax.ppermute(value, axis, [(i, i ^ step) for i in range(size)])  39.3 us
    ppermute x34, waiting for transfers between devices, swap(): return lax.ppermute(value, axis, [(i, i ^ step) for i in range(size)])  37.9 us
    convert_element_type x12, other arithmetic, add(): sum((term.astype(jnp.float32) for term in terms)).astype(jnp.bfloat16)  32.4 us
    pallas_call x1, Pallas kernels, attend_forward(): pl.pallas_call(functools.partial(attend_forward_kernel, head_size=width /...  29.6 us
  transfers between devices with their start and end apart: 60, of which 16 were waited for; matrix products, arithmetic and copies ran while one was open for 9% of the time, Pallas kernels for 32%

profile of v6, /device:TPU:1, one launch (start us, length us, event | category | flops | bytes accessed | tf_op | source)
XLA Modules:
  0.0 590.5 jit_solution(16570109608284455432)
XLA Ops:
  24.3 9.2 %collective-permute-done.4 = s32[2,2]{1,0:T(2,128)S(1)} collective-permute-done((s32[2,2]{1,0:T(2,128)S(1)}, s32[2,2]{1,0:T(2,128)S(1)}, u32[]{:S(2)}, u32[]{:S(2)}) %collective-permute-start.4) | collective-permute-done | bytes 48 | tf_op jit(solution)/shard_map/ppermute | solution.py:921
  33.5 6.9 %collective-permute-start.6 = (s32[2,2]{1,0:T(2,128)S(1)}, s32[2,2]{1,0:T(2,128)S(1)}, u32[]{:S(2)}, u32[]{:S(2)}) collective-permute-start(s32[2,2]{1,0:T(2,128)S(1)} %get-tuple-element.282), channel_id=1, source_target_pairs={{24,0},{28,4},{0,8},{4,12},{8,16},{12,20},{16,24},{20,28},{25,1},{... | collective-permute-start | bytes 56 | tf_op jit(solution)/shard_map/ppermute | solution.py:921
  69.9 4.5 collective-permute-start.11
  75.8 6.7 %prepare.1 = (bf16[1024,1152]{1,0:T(8,128)(2,1)}, bf16[1152,1024]{1,0:T(8,128)(2,1)}, bf16[1024,1152]{1,0:T(8,128)(2,1)}, f32[8,1152]{1,0:T(8,128)}, f32[16,1152]{1,0:T(8,128)}) custom-call(bf16[1024,1152]{1,0:T(8,128)(2,1)} %bitcast.223, bf16[1024,1152]{1,0:T(8,128)(2,1)} %bitcast.220, f32[8,16128]{1,0:T(8,128)} %bitcast.232), custom_call_target="tpu_custom_call" | custom-call | flops 1 | bytes 1 | tf_op jit(solution)/shard_map/prepare/pallas_call | solution.py:372
  82.5 16.3 %collective-permute-done.12 = bf16[144,1152]{1,0:T(8,128)(2,1)S(1)} collective-permute-done((bf16[144,1152]{1,0:T(8,128)(2,1)}, bf16[144,1152]{1,0:T(8,128)(2,1)S(1)}, u32[]{:S(2)}, u32[]{:S(2)}) %collective-permute-start.12) | collective-permute-done | bytes 331808 | tf_op jit(solution)/shard_map/ppermute | solution.py:921
  101.6 5.6 collective-permute-start.15
  119.8 16.2 %project.1.query_ref.key_ref.value_ref = bf16[3,1024,1152]{2,1,0:T(8,128)(2,1)} custom-call(s32[3]{0:T(128)} %pad_add_fusion.3.place, bf16[1024,1152]{1,0:T(8,128)(2,1)} %get-tuple-element.139.mod_ref, f32[16,1152]{1,0:T(8,128)} %get-tuple-element.140.rows_ref, bf16[2,4,144,512]{3,2,1,0:T(8,128)(2,1)} %pad_maximum_fusion.9.rest_0_, ...), custom_call_target="tpu_custom_call" | custom-call | flops 1 | bytes 1 | tf_op jit(solution)/shard_map/project/pallas_call | solution.py:418
  136.0 12.1 %collective-permute-done.18 = bf16[4,144,1152]{2,1,0:T(8,128)(2,1)} collective-permute-done((bf16[4,144,1152]{2,1,0:T(8,128)(2,1)}, bf16[4,144,1152]{2,1,0:T(8,128)(2,1)}, u32[]{:S(2)}, u32[]{:S(2)}) %collective-permute-start.18) | collective-permute-done | bytes 1327136 | tf_op jit(solution)/shard_map/ppermute | solution.py:881
  154.4 29.6 %attend_forward.1 = (bf16[1024,1152]{1,0:T(8,128)(2,1)S(1)}, f32[16,1024]{1,0:T(8,128)S(1)}) custom-call(s32[16]{0:T(128)S(1)} %bitcast.219, bf16[3,1024,1152]{2,1,0:T(8,128)(2,1)} %project.1.query_ref.key_ref.value_ref, bf16[3,1024,1152]{2,1,0:T(8,128)(2,1)} %project.1.query_ref.key_ref.value_ref, bf16[3,1024,1152]{2,1,0:T(8,128)(2,1)} %project.1.query_ref.key_ref.value_ref), custom_call_target="tpu_custom_call" | custom-call | flops 17179869184 | bytes 9437184 | tf_op jit(solution)/shard_map/attend_forward/pallas_call | solution.py:159
  189.8 11.7 %after_attention.1 = (f32[1024,1152]{1,0:T(8,128)}, f32[1024,1152]{1,0:T(8,128)}, bf16[1024,1152]{1,0:T(8,128)(2,1)}, bf16[1152,1024]{1,0:T(8,128)(2,1)}) custom-call(s32[3]{0:T(128)} %pad_add_fusion.3.place, bf16[1024,1152]{1,0:T(8,128)(2,1)} %copy-done.1, bf16[1024,1152]{1,0:T(8,128)(2,1)} %bitcast.224, f32[16,1152]{1,0:T(8,128)} %get-tuple-element.140.rows_ref, ...), custom_call_target="tpu_custom_call" | custom-call | flops 1 | bytes 1 | tf_op jit(solution)/shard_map/after_attention/pallas_call | solution.py:478
  203.0 8.0 %collective-permute-done.25.rest_8_ = bf16[8,2,144,1152]{3,2,1,0:T(8,128)(2,1)} collective-permute-done((bf16[8,2,144,1152]{3,2,1,0:T(8,128)(2,1)}, bf16[8,2,144,1152]{3,2,1,0:T(8,128)(2,1)}, u32[]{:S(2)}, u32[]{:S(2)}) %collective-permute-start.25) | collective-permute-done | bytes 5308448 | tf_op jit(solution)/shard_map/ppermute | solution.py:881
  211.0 92.0 %mlp.1 = (f32[1024,1152]{1,0:T(8,128)}, f32[1024,1152]{1,0:T(8,128)}, f32[4,1152]{1,0:T(4,128)}, bf16[2,2,4,144,1152]{4,3,2,1,0:T(8,128)(2,1)}, bf16[2,2,4,144,1...) custom-call(s32[3]{0:T(128)} %pad_add_fusion.3.place, ...), custom_call_target="tpu_custom_call" | custom-call | flops 1 | bytes 1 | tf_op jit(solution)/shard_map/mlp/pallas_call | solution.py:628
  303.6 14.0 %after_mlp.1 = (f32[1024,1152]{1,0:T(8,128)}, bf16[1024,1152]{1,0:T(8,128)(2,1)}, bf16[1024,1152]{1,0:T(8,128)(2,1)}, f32[8,1152]{1,0:T(8,128)}) custom-call(s32[3]{0:T(128)} %pad_add_fusion.3.place, f32[1024,1152]{1,0:T(8,128)} %get-tuple-element.165.dmod_ref, f32[1024,1152]{1,0:T(8,128)} %get-tuple-element.166.middle_ref, bf16[1024,1152]{1,0:T(8,128)(2,1)} %bitcast.221, ...), custom_call_target="tpu_custom_call" | custom-call | flops 1 | bytes 1 | tf_op jit(solution)/shard_map/after_mlp/pallas_call | solution.py:690
  329.2 56.7 %attend_backward.1.grads_ref = bf16[3,1024,1152]{2,1,0:T(8,128)(2,1)} custom-call(s32[16]{0:T(128)} %bitcast.218, bf16[3,1024,1152]{2,1,0:T(8,128)(2,1)} %project.1.query_ref.key_ref.value_ref, bf16[3,1024,1152]{2,1,0:T(8,128)(2,1)} %project.1.query_ref.key_ref.value_ref, bf16[3,1024,1152]{2,1,0:T(8,128)(2,1)} %project.1.query_ref.key_ref.value_ref, ...), custom_call_target="tpu_custom_call" | custom-call | flops 42949672960 | bytes 18874368 | tf_op jit(solution)/shard_map/attend_backward/pallas_call | solution.py:190
  387.1 5.4 fusion.4
  394.9 9.4 %finish.1 = (bf16[1024,1152]{1,0:T(8,128)(2,1)}, f32[8,1152]{1,0:T(8,128)}) custom-call(f32[1024,1152]{1,0:T(8,128)} %get-tuple-element.190.mlp_ref, f32[1024,1152]{1,0:T(8,128)} %get-tuple-element.166.middle_ref, f32[1024,1152]{1,0:T(8,128)} %get-tuple-element.191.branch_ref, f32[1024,1152]{1,0:T(8,128)} %get-tuple-element.192.dmiddle_ref, ...), custom_call_target="tpu_custom_call" | custom-call | flops 1 | bytes 1 | tf_op jit(solution)/shard_map/finish/pallas_call | solution.py:729
  404.3 19.5 %square_grads.1 = (bf16[2,2,4,144,512]{4,3,2,1,0:T(8,128)(2,1)}, bf16[2,2,4,144,512]{4,3,2,1,0:T(8,128)(2,1)}, bf16[2,2,4,144,640]{4,3,2,1,0:T(8,128)(2,1)}, bf16[2,2,4,144,640]{4,3,2,1,0:T(8,128)(2,1)}) custom-call(s32[3]{0:T(128)} %pad_add_fusion.3.place, bf16[1152,1024]{1,0:T(8,128)(2,1)} %get-tuple-element.138.across_ref, ...), custom_call_target="tpu_custom_call" | custom-call | flops 1 | bytes 1 | tf_op jit(solution)/shard_map/square_grads/pallas_call | solution.py:774
  429.8 4.8 collective-permute-done.32
  450.6 24.4 %tokens_back.1 = (bf16[1024,1152]{1,0:T(8,128)(2,1)}, f32[8,1152]{1,0:T(8,128)}) custom-call(s32[3]{0:T(128)} %pad_add_fusion.3.place, bf16[3,1024,1152]{2,1,0:T(8,128)(2,1)} %attend_backward.1.grads_ref, bf16[1024,1152]{1,0:T(8,128)(2,1)} %bitcast.225, f32[1024,1152]{1,0:T(8,128)} %get-tuple-element.192.dmiddle_ref, ...), custom_call_target="tpu_custom_call" | custom-call | flops 1 | bytes 1 | tf_op jit(solution)/shard_map/tokens_back/pallas_call | solution.py:834
  490.0 4.3 collective-permute-done.41
  494.3 15.7 %collective-permute-done.42 = bf16[144,1152]{1,0:T(8,128)(2,1)S(1)} collective-permute-done((bf16[144,1152]{1,0:T(8,128)(2,1)S(1)}, bf16[144,1152]{1,0:T(8,128)(2,1)S(1)}, u32[]{:S(2)}, u32[]{:S(2)}) %collective-permute-start.42) | collective-permute-done | bytes 331808 | tf_op jit(solution)/shard_map/ppermute | solution.py:921
  513.8 5.7 collective-permute-start.50
  529.7 17.0 %collective-permute-done.52 = bf16[2,4,1,16128]{3,1,0,2:T(4,128)(2,1)S(1)} collective-permute-done((bf16[2,4,1,16128]{3,1,0,2:T(4,128)(2,1)S(1)}, bf16[2,4,1,16128]{3,1,0,2:T(4,128)(2,1)S(1)}, u32[]{:S(2)}, u32[]{:S(2)}) %collective-permute-start.52) | collective-permute-done | bytes 258080 | tf_op jit(solution)/shard_map/ppermute | solution.py:914
  546.7 4.5 collective-permute-start.49
  (295 shorter events, 173.9 us)
Async XLA Ops:
  8.5 35.7 %collective-permute-start = (bf16[144,1152]{1,0:T(8,128)(2,1)S(1)}, bf16[144,1152]{1,0:T(8,128)(2,1)S(1)}, u32[]{:S(2)}, u32[]{:S(2)}) collective-permute-start(bf16[144,1152]{1,0:T(8,128)(2,1)S(1)} %fusion.28), channel_id=1, source_target_pairs={{8,0},{12,4},{16,8},{20,12},{24,16},{28,20},{0,24},{4,28},{9,1},{1... | collective-permute-start | bytes 995336 | tf_op jit(solution)/shard_map/ppermute | solution.py:921
  12.7 31.5 %collective-permute-start.1 = (bf16[144,1152]{1,0:T(8,128)(2,1)S(1)}, bf16[144,1152]{1,0:T(8,128)(2,1)S(1)}, u32[]{:S(2)}, u32[]{:S(2)}) collective-permute-start(bf16[144,1152]{1,0:T(8,128)(2,1)S(1)} %fusion.28), channel_id=1, source_target_pairs={{16,0},{20,4},{24,8},{28,12},{0,16},{4,20},{8,24},{12,28},{17,1},{... | collective-permute-start | bytes 995336 | tf_op jit(solution)/shard_map/ppermute | solution.py:921
  12.7 31.5 %collective-permute-start.2 = (bf16[144,1152]{1,0:T(8,128)(2,1)S(1)}, bf16[144,1152]{1,0:T(8,128)(2,1)S(1)}, u32[]{:S(2)}, u32[]{:S(2)}) collective-permute-start(bf16[144,1152]{1,0:T(8,128)(2,1)S(1)} %fusion.28), channel_id=1, source_target_pairs={{24,0},{28,4},{0,8},{4,12},{8,16},{12,20},{16,24},{20,28},{25,1},{... | collective-permute-start | bytes 995336 | tf_op jit(solution)/shard_map/ppermute | solution.py:921
  54.0 147.6 %all-gather.3.cloned.1.call-start = ((), (), s32[]{:S(2)}) async-start(), calls=%async_computation.1 | async-start | bytes 5971968 | tf_op jit(solution)/shard_map/all_gather | solution.py:1073
  67.1 33.0 %collective-permute-start.10 = (bf16[2,4,144,640]{3,2,1,0:T(8,128)(2,1)S(1)}, bf16[2,4,144,640]{3,2,1,0:T(8,128)(2,1)S(1)}, u32[]{:S(2)}, u32[]{:S(2)}) collective-permute-start(bf16[2,4,144,640]{3,2,1,0:T(8,128)(2,1)S(1)} %pad_maximum_fusion.4.rest_4_), channel_id=1, source_target_pairs={{0,4},{4,0},{8,12},{12,8},{16,20},{20,16},{24,28},{28,24},{1,5},{5... | collective-permute-start | bytes 4423688 | tf_op jit(solution)/shard_map/ppermute | solution.py:881
  69.7 30.4 %collective-permute-start.9 = (bf16[2,4,144,512]{3,2,1,0:T(8,128)(2,1)}, bf16[2,4,144,512]{3,2,1,0:T(8,128)(2,1)S(1)}, u32[]{:S(2)}, u32[]{:S(2)}) collective-permute-start(bf16[2,4,144,512]{3,2,1,0:T(8,128)(2,1)} %pad_maximum_fusion.9.rest_0_), channel_id=1, source_target_pairs={{0,2},{1,3},{2,0},{3,1},{4,6},{5,7},{6,4},{7,5},{8,10},{9,11},{10,... | collective-permute-start | bytes 3538952 | tf_op jit(solution)/shard_map/ppermute | solution.py:881
  110.4 37.8 %collective-permute-start.18 = (bf16[4,144,1152]{2,1,0:T(8,128)(2,1)}, bf16[4,144,1152]{2,1,0:T(8,128)(2,1)}, u32[]{:S(2)}, u32[]{:S(2)}) collective-permute-start(bf16[4,144,1152]{2,1,0:T(8,128)(2,1)} %pad_maximum_fusion.6), channel_id=1, source_target_pairs={{0,4},{4,0},{8,12},{12,8},{16,20},{20,16},{24,28},{28,24},{1,5},{5... | collective-permute-start | bytes 3981320 | tf_op jit(solution)/shard_map/ppermute | solution.py:881
  110.4 37.7 %collective-permute-start.19 = (bf16[4,144,1152]{2,1,0:T(8,128)(2,1)}, bf16[4,144,1152]{2,1,0:T(8,128)(2,1)}, u32[]{:S(2)}, u32[]{:S(2)}) collective-permute-start(bf16[4,144,1152]{2,1,0:T(8,128)(2,1)} %pad_maximum_fusion.6), channel_id=1, source_target_pairs={{0,2},{1,3},{2,0},{3,1},{4,6},{5,7},{6,4},{7,5},{8,10},{9,11},{10,... | collective-permute-start | bytes 3981320 | tf_op jit(solution)/shard_map/ppermute | solution.py:881
  151.6 34.6 %collective-permute-start.21 = (bf16[2,4,144,1152]{3,2,1,0:T(8,128)(2,1)}, bf16[2,4,144,1152]{3,2,1,0:T(8,128)(2,1)}, u32[]{:S(2)}, u32[]{:S(2)}) collective-permute-start(bf16[2,4,144,1152]{3,2,1,0:T(8,128)(2,1)} %pad_maximum_fusion.rest_3_), channel_id=1, source_target_pairs={{0,1},{1,0},{2,3},{3,2},{4,5},{5,4},{6,7},{7,6},{8,9},{9,8},{10,11... | collective-permute-start | bytes 7962632 | tf_op jit(solution)/shard_map/ppermute | solution.py:881
  152.8 33.4 %collective-permute-start.20 = (bf16[4,144,1152]{2,1,0:T(8,128)(2,1)}, bf16[4,144,1152]{2,1,0:T(8,128)(2,1)S(1)}, u32[]{:S(2)}, u32[]{:S(2)}) collective-permute-start(bf16[4,144,1152]{2,1,0:T(8,128)(2,1)} %collective-permute-done.18), channel_id=1, source_target_pairs={{0,2},{1,3},{2,0},{3,1},{4,6},{5,7},{6,4},{7,5},{8,10},{9,11},{10,... | collective-permute-start | bytes 3981320 | tf_op jit(solution)/shard_map/ppermute | solution.py:881
  154.1 32.1 %collective-permute-start.22 = (s32[2,4,2]{2,0,1:T(2,128)S(1)}, s32[2,4,2]{2,0,1:T(2,128)S(1)}, u32[]{:S(2)}, u32[]{:S(2)}) collective-permute-start(s32[2,4,2]{2,0,1:T(2,128)S(1)} %bitcast.253), channel_id=1, source_target_pairs={{0,1},{1,0},{2,3},{3,2},{4,5},{5,4},{6,7},{7,6},{8,9},{9,8},{10,11... | collective-permute-start | bytes 200 | tf_op jit(solution)/shard_map/ppermute | solution.py:881
  328.0 59.1 %collective-permute-start.28 = (bf16[2,4,144,1152]{3,2,1,0:T(8,128)(2,1)}, bf16[2,4,144,1152]{3,2,1,0:T(8,128)(2,1)}, u32[]{:S(2)}, u32[]{:S(2)}) collective-permute-start(bf16[2,4,144,1152]{3,2,1,0:T(8,128)(2,1)} %fusion), channel_id=1, source_target_pairs={{0,4},{4,0},{8,12},{12,8},{16,20},{20,16},{24,28},{28,24},{1,5},{5... | collective-permute-start | bytes 7962632 | tf_op jit(solution)/shard_map/ppermute | solution.py:881
  328.2 58.9 %collective-permute-start.29 = (bf16[2,4,144,1152]{3,2,1,0:T(8,128)(2,1)}, bf16[2,4,144,1152]{3,2,1,0:T(8,128)(2,1)}, u32[]{:S(2)}, u32[]{:S(2)}) collective-permute-start(bf16[2,4,144,1152]{3,2,1,0:T(8,128)(2,1)} %fusion.1), channel_id=1, source_target_pairs={{0,2},{1,3},{2,0},{3,1},{4,6},{5,7},{6,4},{7,5},{8,10},{9,11},{10,... | collective-permute-start | bytes 7962632 | tf_op jit(solution)/shard_map/ppermute | solution.py:881
  392.5 31.2 %collective-permute-start.30 = (bf16[4,144,1152]{2,1,0:T(8,128)(2,1)}, bf16[4,144,1152]{2,1,0:T(8,128)(2,1)}, u32[]{:S(2)}, u32[]{:S(2)}) collective-permute-start(bf16[4,144,1152]{2,1,0:T(8,128)(2,1)} %get-tuple-element.188), channel_id=1, source_target_pairs={{0,2},{1,3},{2,0},{3,1},{4,6},{5,7},{6,4},{7,5},{8,10},{9,11},{10,... | collective-permute-start | bytes 3981320 | tf_op jit(solution)/shard_map/ppermute | solution.py:881
  393.7 30.1 %collective-permute-start.31 = (bf16[4,144,1152]{2,1,0:T(8,128)(2,1)}, bf16[4,144,1152]{2,1,0:T(8,128)(2,1)}, u32[]{:S(2)}, u32[]{:S(2)}) collective-permute-start(bf16[4,144,1152]{2,1,0:T(8,128)(2,1)} %get-tuple-element.189), channel_id=1, source_target_pairs={{0,4},{4,0},{8,12},{12,8},{16,20},{20,16},{24,28},{28,24},{1,5},{5... | collective-permute-start | bytes 3981320 | tf_op jit(solution)/shard_map/ppermute | solution.py:881
  440.2 34.9 %collective-permute-start.35 = (bf16[2,4,144,640]{3,2,1,0:T(8,128)(2,1)}, bf16[2,4,144,640]{3,2,1,0:T(8,128)(2,1)}, u32[]{:S(2)}, u32[]{:S(2)}) collective-permute-start(bf16[2,4,144,640]{3,2,1,0:T(8,128)(2,1)} %fusion.6), channel_id=1, source_target_pairs={{0,4},{4,0},{8,12},{12,8},{16,20},{20,16},{24,28},{28,24},{1,5},{5... | collective-permute-start | bytes 4423688 | tf_op jit(solution)/shard_map/ppermute | solution.py:881
  441.1 34.0 %collective-permute-start.34 = (bf16[2,4,144,512]{3,2,1,0:T(8,128)(2,1)}, bf16[2,4,144,512]{3,2,1,0:T(8,128)(2,1)}, u32[]{:S(2)}, u32[]{:S(2)}) collective-permute-start(bf16[2,4,144,512]{3,2,1,0:T(8,128)(2,1)} %fusion.9), channel_id=1, source_target_pairs={{0,2},{1,3},{2,0},{3,1},{4,6},{5,7},{6,4},{7,5},{8,10},{9,11},{10,... | collective-permute-start | bytes 3538952 | tf_op jit(solution)/shard_map/ppermute | solution.py:881
  442.4 32.7 %collective-permute-start.36 = (bf16[144,1152]{1,0:T(8,128)(2,1)}, bf16[144,1152]{1,0:T(8,128)(2,1)S(1)}, u32[]{:S(2)}, u32[]{:S(2)}) collective-permute-start(bf16[144,1152]{1,0:T(8,128)(2,1)} %get-tuple-element.263), channel_id=1, source_target_pairs={{24,0},{28,4},{0,8},{4,12},{8,16},{12,20},{16,24},{20,28},{25,1},{... | collective-permute-start | bytes 995336 | tf_op jit(solution)/shard_map/ppermute | solution.py:921
  443.3 31.7 %collective-permute-start.37 = (bf16[144,1152]{1,0:T(8,128)(2,1)}, bf16[144,1152]{1,0:T(8,128)(2,1)S(1)}, u32[]{:S(2)}, u32[]{:S(2)}) collective-permute-start(bf16[144,1152]{1,0:T(8,128)(2,1)} %get-tuple-element.262), channel_id=1, source_target_pairs={{16,0},{20,4},{24,8},{28,12},{0,16},{4,20},{8,24},{12,28},{17,1},{... | collective-permute-start | bytes 995336 | tf_op jit(solution)/shard_map/ppermute | solution.py:921
  445.1 29.9 %collective-permute-start.38 = (bf16[144,1152]{1,0:T(8,128)(2,1)}, bf16[144,1152]{1,0:T(8,128)(2,1)}, u32[]{:S(2)}, u32[]{:S(2)}) collective-permute-start(bf16[144,1152]{1,0:T(8,128)(2,1)} %get-tuple-element.261), channel_id=1, source_target_pairs={{8,0},{12,4},{16,8},{20,12},{24,16},{28,20},{0,24},{4,28},{9,1},{1... | collective-permute-start | bytes 995336 | tf_op jit(solution)/shard_map/ppermute | solution.py:921
  483.6 26.4 %collective-permute-start.42 = (bf16[144,1152]{1,0:T(8,128)(2,1)S(1)}, bf16[144,1152]{1,0:T(8,128)(2,1)S(1)}, u32[]{:S(2)}, u32[]{:S(2)}) collective-permute-start(bf16[144,1152]{1,0:T(8,128)(2,1)S(1)} %get-tuple-element.259), channel_id=1, source_target_pairs={{16,0},{20,4},{24,8},{28,12},{0,16},{4,20},{8,24},{12,28},{17,1},{... | collective-permute-start | bytes 995336 | tf_op jit(solution)/shard_map/ppermute | solution.py:921
  519.8 32.5 %collective-permute-start.54 = (bf16[2,144,1152]{2,1,0:T(8,128)(2,1)S(1)}, bf16[2,144,1152]{2,1,0:T(8,128)(2,1)S(1)}, u32[]{:S(2)}, u32[]{:S(2)}) collective-permute-start(bf16[2,144,1152]{2,1,0:T(8,128)(2,1)S(1)} %pad_maximum_fusion.11), channel_id=1, source_target_pairs={{0,2},{1,3},{2,0},{3,1},{4,6},{5,7},{6,4},{7,5},{8,10},{9,11},{10,... | collective-permute-start | bytes 1990664 | tf_op jit(solution)/shard_map/ppermute | solution.py:881
  522.0 31.6 %collective-permute-start.47 = (bf16[144,1152]{1,0:T(8,128)(2,1)S(1)}, bf16[144,1152]{1,0:T(8,128)(2,1)S(1)}, u32[]{:S(2)}, u32[]{:S(2)}) collective-permute-start(bf16[144,1152]{1,0:T(8,128)(2,1)S(1)} %get-tuple-element.257), channel_id=1, source_target_pairs={{24,0},{28,4},{0,8},{4,12},{8,16},{12,20},{16,24},{20,28},{25,1},{... | collective-permute-start | bytes 995336 | tf_op jit(solution)/shard_map/ppermute | solution.py:921
  525.1 28.6 %collective-permute-start.48 = (bf16[144,1152]{1,0:T(8,128)(2,1)S(1)}, bf16[144,1152]{1,0:T(8,128)(2,1)S(1)}, u32[]{:S(2)}, u32[]{:S(2)}) collective-permute-start(bf16[144,1152]{1,0:T(8,128)(2,1)S(1)} %get-tuple-element.256), channel_id=1, source_target_pairs={{16,0},{20,4},{24,8},{28,12},{0,16},{4,20},{8,24},{12,28},{17,1},{... | collective-permute-start | bytes 995336 | tf_op jit(solution)/shard_map/ppermute | solution.py:921
  (64 other events, 730.8 us)
Sparse Core Ops, SparseCore 0:
  109.9 89.1 all-gather.2

commit v7 on v6

--- a/solution.py
+++ b/solution.py
@@ -222,6 +222,8 @@
     def block(self, r, x_r, z_r):
         y_r, core_r = r // 2, r % 2
         first_r, second_r = (x_r, y_r) if self.order == "xy" else (y_r, x_r)
+        if len(self) == 8:
+            return self[4 * core_r + 2 * second_r + first_r].at[z_r]
         return self[2 * core_r + second_r].at[first_r, z_r]
 
 
@@ -231,7 +233,7 @@
         return [pltpu.make_async_copy(sets[0][0].at[part], target, sem)]
     copies, column = [], 0
     for refs in sets:
-        rows, columns = refs[0].shape[2:]
+        rows, columns = refs[0].shape[-2:]
         for x_r in range(2):
             for z_r in range(4):
                 shard = (place[0] + z_r) % 4 * 2 + (place[1] + x_r) % 2
@@ -1074,21 +1076,23 @@
     qkv = project(place, mod_one, rows, squares)
     if paired:
         qkv, up_x, up_y, all_facts = barrier((qkv, up_x, up_y, all_facts))
-        up = jnp.stack([up, up_x])
-        up_xy, up_c = net.partner(up_x, "y"), net.partner(up, "c")
+        up_xy, up_c, up_x_c = net.partner(up_x, "y"), net.partner(up, "c"), net.partner(up_x, "c")
         all_facts = net.pair(all_facts, "c").swapaxes(0, 1)
     attn_low, lse = attend_forward(qkv, head_keep[0])
     if paired:
-        attn_low, up, up_xy, up_c, all_facts = barrier((attn_low, up, up_xy, up_c, all_facts))
+        attn_low, up_y, up_xy, up_c, up_x_c, all_facts = barrier(
+            (attn_low, up_y, up_xy, up_c, up_x_c, all_facts)
+        )
         all_facts = net.pair(all_facts, "y").reshape(image_count, 2)
-        up_y = jnp.stack([up_y, up_xy])
-        up_y_c = net.partner(up_y, "c")
+        up_y_c, up_xy_c = net.partner(up_y, "c"), net.partner(up_xy, "c")
     attn_branch, middle, mod_two, mod_two_across = after_attention(
         place, attn_low, tokens[0], rows, squares
     )
     if paired:
-        mod_two, down, up_y_c, all_facts = barrier((mod_two, down, up_y_c, all_facts))
-        ups = [Blocks([up, up_y, up_c, up_y_c], "xy")]
+        mod_two, down, up_y_c, up_xy_c, all_facts = barrier(
+            (mod_two, down, up_y_c, up_xy_c, all_facts)
+        )
+        ups = [Blocks([up, up_x, up_y, up_xy, up_c, up_x_c, up_y_c, up_xy_c], "xy")]
         downs = [down, net.partner(down, "c")]
     else:
         found = lax.all_gather(up_weight, "fsdp", axis=0, tiled=True)

time: 596 us -> 596 us (level)
  waiting for transfers between devices: 105 us -> 126 us
  starting transfers between devices: 87.6 us -> 72.7 us
  other arithmetic: 68.4 us -> 61.7 us
    ppermute x21, starting transfers between devices: 41.6 us -> 31.5 us  [ahead(): return lax.ppermute(value, 'fsdp', pairs)]
    ppermute x34 -> x36, waiting for transfers between devices: 37.9 us -> 45.7 us  [swap(): return lax.ppermute(value, axis, [(i, i ^ step) for i in range(size)])]
    another operation x5 -> x3, other arithmetic: 7.53 us -> 0.9 us  [the longest x1 3.51 us: body(): up = jnp.stack([up, up_x])]
    ppermute x34 -> x36, starting transfers between devices: 39.3 us -> 36 us  [swap(): return lax.ppermute(value, axis, [(i, i ^ step) for i in range(size)])]
  transfers between devices with their start and end apart: 60 -> 62, of which waited for: 16 -> 21; matrix products, arithmetic and copies ran while one was open for 9% -> 8% of each run, Pallas kernels for 32% -> 32%
where the time goes in v7:
time: 596 us; the launch traced here: 590 us
  Pallas kernels  280 us (47%)
  waiting for transfers between devices  126 us (21%)
  starting transfers between devices  72.7 us (12%)
  other arithmetic  61.7 us (10%)
  local copies, waits for them, and re-layouts  24.2 us (4%)
  between operations  16.5 us (3%)
  matrix products  8.6 us (1%)
    pallas_call x1, Pallas kernels, mlp(): pl.pallas_call(functools.partial(mlp_kernel, ups=ups, downs=len(downs)),...  91.7 us
    pallas_call x1, Pallas kernels, attend_backward(): pl.pallas_call(functools.partial(attend_backward_kernel, head_size=width...  56.7 us
    ppermute x21, waiting for transfers between devices, ahead(): return lax.ppermute(value, 'fsdp', pairs)  53.8 us
    ppermute x36, waiting for transfers between devices, swap(): return lax.ppermute(value, axis, [(i, i ^ step) for i in range(size)])  45.7 us
    ppermute x36, starting transfers between devices, swap(): return lax.ppermute(value, axis, [(i, i ^ step) for i in range(size)])  36 us
    convert_element_type x12, other arithmetic, add(): sum((term.astype(jnp.float32) for term in terms)).astype(jnp.bfloat16)  32.4 us
    ppermute x21, starting transfers between devices, ahead(): return lax.ppermute(value, 'fsdp', pairs)  31.5 us
    pallas_call x1, Pallas kernels, attend_forward(): pl.pallas_call(functools.partial(attend_forward_kernel, head_size=width /...  30.3 us
  transfers between devices with their start and end apart: 62, of which 21 were waited for; matrix products, arithmetic and copies ran while one was open for 8% of the time, Pallas kernels for 32%

profile of v7, /device:TPU:1, one launch (start us, length us, event | category | flops | bytes accessed | tf_op | source)
XLA Modules:
  0.0 590.2 jit_solution(10662298683015221877)
XLA Ops:
  24.3 9.2 %collective-permute-done.4 = s32[2,2]{1,0:T(2,128)S(1)} collective-permute-done((s32[2,2]{1,0:T(2,128)S(1)}, s32[2,2]{1,0:T(2,128)S(1)}, u32[]{:S(2)}, u32[]{:S(2)}) %collective-permute-start.4) | collective-permute-done | bytes 48 | tf_op jit(solution)/shard_map/ppermute | solution.py:923
  33.5 6.9 %collective-permute-start.6 = (s32[2,2]{1,0:T(2,128)S(1)}, s32[2,2]{1,0:T(2,128)S(1)}, u32[]{:S(2)}, u32[]{:S(2)}) collective-permute-start(s32[2,2]{1,0:T(2,128)S(1)} %get-tuple-element.286), channel_id=1, source_target_pairs={{24,0},{28,4},{0,8},{4,12},{8,16},{12,20},{16,24},{20,28},{25,1},{... | collective-permute-start | bytes 56 | tf_op jit(solution)/shard_map/ppermute | solution.py:923
  69.8 4.5 collective-permute-start.11
  75.6 6.7 %prepare.1 = (bf16[1024,1152]{1,0:T(8,128)(2,1)}, bf16[1152,1024]{1,0:T(8,128)(2,1)}, bf16[1024,1152]{1,0:T(8,128)(2,1)}, f32[8,1152]{1,0:T(8,128)}, f32[16,1152]{1,0:T(8,128)}) custom-call(bf16[1024,1152]{1,0:T(8,128)(2,1)} %bitcast.219, bf16[1024,1152]{1,0:T(8,128)(2,1)} %bitcast.216, f32[8,16128]{1,0:T(8,128)} %bitcast.227), custom_call_target="tpu_custom_call" | custom-call | flops 1 | bytes 1 | tf_op jit(solution)/shard_map/prepare/pallas_call | solution.py:374
  82.3 16.4 %collective-permute-done.12 = bf16[144,1152]{1,0:T(8,128)(2,1)S(1)} collective-permute-done((bf16[144,1152]{1,0:T(8,128)(2,1)}, bf16[144,1152]{1,0:T(8,128)(2,1)S(1)}, u32[]{:S(2)}, u32[]{:S(2)}) %collective-permute-start.12) | collective-permute-done | bytes 331808 | tf_op jit(solution)/shard_map/ppermute | solution.py:923
  101.5 5.6 collective-permute-start.15
  119.9 16.2 %project.1.query_ref.key_ref.value_ref = bf16[3,1024,1152]{2,1,0:T(8,128)(2,1)} custom-call(s32[3]{0:T(128)} %pad_add_fusion.3.place, bf16[1024,1152]{1,0:T(8,128)(2,1)} %get-tuple-element.141.mod_ref, f32[16,1152]{1,0:T(8,128)} %get-tuple-element.142.rows_ref, bf16[2,4,144,512]{3,2,1,0:T(8,128)(2,1)} %pad_maximum_fusion.7.rest_0_, ...), custom_call_target="tpu_custom_call" | custom-call | flops 1 | bytes 1 | tf_op jit(solution)/shard_map/project/pallas_call | solution.py:420
  136.1 12.0 %collective-permute-done.18.rest_4_ = bf16[4,144,1152]{2,1,0:T(8,128)(2,1)} collective-permute-done((bf16[4,144,1152]{2,1,0:T(8,128)(2,1)}, bf16[4,144,1152]{2,1,0:T(8,128)(2,1)}, u32[]{:S(2)}, u32[]{:S(2)}) %collective-permute-start.18) | collective-permute-done | bytes 1327136 | tf_op jit(solution)/shard_map/ppermute | solution.py:883
  150.8 30.3 %attend_forward.1 = (bf16[1024,1152]{1,0:T(8,128)(2,1)S(1)}, f32[16,1024]{1,0:T(8,128)S(1)}) custom-call(s32[16]{0:T(128)S(1)} %bitcast.215, bf16[3,1024,1152]{2,1,0:T(8,128)(2,1)} %project.1.query_ref.key_ref.value_ref, bf16[3,1024,1152]{2,1,0:T(8,128)(2,1)} %project.1.query_ref.key_ref.value_ref, bf16[3,1024,1152]{2,1,0:T(8,128)(2,1)} %project.1.query_ref.key_ref.value_ref), custom_call_target="tpu_custom_call" | custom-call | flops 17179869184 | bytes 9437184 | tf_op jit(solution)/shard_map/attend_forward/pallas_call | solution.py:159
  184.2 11.6 %after_attention.1 = (f32[1024,1152]{1,0:T(8,128)}, f32[1024,1152]{1,0:T(8,128)}, bf16[1024,1152]{1,0:T(8,128)(2,1)}, bf16[1152,1024]{1,0:T(8,128)(2,1)}) custom-call(s32[3]{0:T(128)} %pad_add_fusion.3.place, bf16[1024,1152]{1,0:T(8,128)(2,1)} %copy-done.1, bf16[1024,1152]{1,0:T(8,128)(2,1)} %bitcast.220, f32[16,1152]{1,0:T(8,128)} %get-tuple-element.142.rows_ref, ...), custom_call_target="tpu_custom_call" | custom-call | flops 1 | bytes 1 | tf_op jit(solution)/shard_map/after_attention/pallas_call | solution.py:480
  201.2 8.0 %collective-permute-done.27.rest_12_ = bf16[8,2,144,1152]{3,2,1,0:T(8,128)(2,1)} collective-permute-done((bf16[8,2,144,1152]{3,2,1,0:T(8,128)(2,1)}, bf16[8,2,144,1152]{3,2,1,0:T(8,128)(2,1)}, u32[]{:S(2)}, u32[]{:S(2)}) %collective-permute-start.27) | collective-permute-done | bytes 5308448 | tf_op jit(solution)/shard_map/ppermute | solution.py:883
  209.2 91.7 %mlp.1 = (f32[1024,1152]{1,0:T(8,128)}, f32[1024,1152]{1,0:T(8,128)}, f32[4,1152]{1,0:T(4,128)}, bf16[2,2,4,144,1152]{4,3,2,1,0:T(8,128)(2,1)}, bf16[2,2,4,144,1...) custom-call(s32[3]{0:T(128)} %pad_add_fusion.3.place, ...), custom_call_target="tpu_custom_call" | custom-call | flops 1 | bytes 1 | tf_op jit(solution)/shard_map/mlp/pallas_call | solution.py:630
  301.5 14.2 %after_mlp.1 = (f32[1024,1152]{1,0:T(8,128)}, bf16[1024,1152]{1,0:T(8,128)(2,1)}, bf16[1024,1152]{1,0:T(8,128)(2,1)}, f32[8,1152]{1,0:T(8,128)}) custom-call(s32[3]{0:T(128)} %pad_add_fusion.3.place, f32[1024,1152]{1,0:T(8,128)} %get-tuple-element.169.dmod_ref, f32[1024,1152]{1,0:T(8,128)} %get-tuple-element.170.middle_ref, bf16[1024,1152]{1,0:T(8,128)(2,1)} %bitcast.217, ...), custom_call_target="tpu_custom_call" | custom-call | flops 1 | bytes 1 | tf_op jit(solution)/shard_map/after_mlp/pallas_call | solution.py:692
  327.4 56.7 %attend_backward.1.grads_ref = bf16[3,1024,1152]{2,1,0:T(8,128)(2,1)} custom-call(s32[16]{0:T(128)} %bitcast.214, bf16[3,1024,1152]{2,1,0:T(8,128)(2,1)} %project.1.query_ref.key_ref.value_ref, bf16[3,1024,1152]{2,1,0:T(8,128)(2,1)} %project.1.query_ref.key_ref.value_ref, bf16[3,1024,1152]{2,1,0:T(8,128)(2,1)} %project.1.query_ref.key_ref.value_ref, ...), custom_call_target="tpu_custom_call" | custom-call | flops 42949672960 | bytes 18874368 | tf_op jit(solution)/shard_map/attend_backward/pallas_call | solution.py:190
  385.0 5.5 fusion.4
  392.9 9.4 %finish.1 = (bf16[1024,1152]{1,0:T(8,128)(2,1)}, f32[8,1152]{1,0:T(8,128)}) custom-call(f32[1024,1152]{1,0:T(8,128)} %get-tuple-element.194.mlp_ref, f32[1024,1152]{1,0:T(8,128)} %get-tuple-element.170.middle_ref, f32[1024,1152]{1,0:T(8,128)} %get-tuple-element.195.branch_ref, f32[1024,1152]{1,0:T(8,128)} %get-tuple-element.196.dmiddle_ref, ...), custom_call_target="tpu_custom_call" | custom-call | flops 1 | bytes 1 | tf_op jit(solution)/shard_map/finish/pallas_call | solution.py:731
  402.3 19.4 %square_grads.1 = (bf16[2,2,4,144,512]{4,3,2,1,0:T(8,128)(2,1)}, bf16[2,2,4,144,512]{4,3,2,1,0:T(8,128)(2,1)}, bf16[2,2,4,144,640]{4,3,2,1,0:T(8,128)(2,1)}, bf16[2,2,4,144,640]{4,3,2,1,0:T(8,128)(2,1)}) custom-call(s32[3]{0:T(128)} %pad_add_fusion.3.place, bf16[1152,1024]{1,0:T(8,128)(2,1)} %get-tuple-element.140.across_ref, ...), custom_call_target="tpu_custom_call" | custom-call | flops 1 | bytes 1 | tf_op jit(solution)/shard_map/square_grads/pallas_call | solution.py:776
  427.8 4.8 collective-permute-done.34
  447.2 24.2 %tokens_back.1 = (bf16[1024,1152]{1,0:T(8,128)(2,1)}, f32[8,1152]{1,0:T(8,128)}) custom-call(s32[3]{0:T(128)} %pad_add_fusion.3.place, bf16[3,1024,1152]{2,1,0:T(8,128)(2,1)} %attend_backward.1.grads_ref, bf16[1024,1152]{1,0:T(8,128)(2,1)} %bitcast.221, f32[1024,1152]{1,0:T(8,128)} %get-tuple-element.196.dmiddle_ref, ...), custom_call_target="tpu_custom_call" | custom-call | flops 1 | bytes 1 | tf_op jit(solution)/shard_map/tokens_back/pallas_call | solution.py:836
  484.6 14.1 %collective-permute-done.47 = bf16[1,16128]{1,0:T(2,128)(2,1)S(1)} collective-permute-done((bf16[1,16128]{1,0:T(2,128)(2,1)S(1)}, bf16[1,16128]{1,0:T(2,128)(2,1)S(1)}, u32[]{:S(2)}, u32[]{:S(2)}) %collective-permute-start.47) | collective-permute-done | bytes 32288 | tf_op jit(solution)/shard_map/ppermute | solution.py:923
  499.0 8.0 %collective-permute-done.44 = bf16[144,1152]{1,0:T(8,128)(2,1)S(1)} collective-permute-done((bf16[144,1152]{1,0:T(8,128)(2,1)S(1)}, bf16[144,1152]{1,0:T(8,128)(2,1)S(1)}, u32[]{:S(2)}, u32[]{:S(2)}) %collective-permute-start.44) | collective-permute-done | bytes 331808 | tf_op jit(solution)/shard_map/ppermute | solution.py:923
  524.4 5.8 collective-permute-done.53
  530.7 17.9 %collective-permute-done.54 = bf16[2,4,1,16128]{3,1,0,2:T(4,128)(2,1)S(1)} collective-permute-done((bf16[2,4,1,16128]{3,1,0,2:T(4,128)(2,1)S(1)}, bf16[2,4,1,16128]{3,1,0,2:T(4,128)(2,1)S(1)}, u32[]{:S(2)}, u32[]{:S(2)}) %collective-permute-start.54) | collective-permute-done | bytes 258080 | tf_op jit(solution)/shard_map/ppermute | solution.py:916
  551.0 5.3 collective-permute-done.51
  (299 shorter events, 169.3 us)
Async XLA Ops:
  8.5 35.7 %collective-permute-start = (bf16[144,1152]{1,0:T(8,128)(2,1)S(1)}, bf16[144,1152]{1,0:T(8,128)(2,1)S(1)}, u32[]{:S(2)}, u32[]{:S(2)}) collective-permute-start(bf16[144,1152]{1,0:T(8,128)(2,1)S(1)} %fusion.28), channel_id=1, source_target_pairs={{8,0},{12,4},{16,8},{20,12},{24,16},{28,20},{0,24},{4,28},{9,1},{1... | collective-permute-start | bytes 995336 | tf_op jit(solution)/shard_map/ppermute | solution.py:923
  12.7 31.5 %collective-permute-start.1 = (bf16[144,1152]{1,0:T(8,128)(2,1)S(1)}, bf16[144,1152]{1,0:T(8,128)(2,1)S(1)}, u32[]{:S(2)}, u32[]{:S(2)}) collective-permute-start(bf16[144,1152]{1,0:T(8,128)(2,1)S(1)} %fusion.28), channel_id=1, source_target_pairs={{16,0},{20,4},{24,8},{28,12},{0,16},{4,20},{8,24},{12,28},{17,1},{... | collective-permute-start | bytes 995336 | tf_op jit(solution)/shard_map/ppermute | solution.py:923
  12.7 31.5 %collective-permute-start.2 = (bf16[144,1152]{1,0:T(8,128)(2,1)S(1)}, bf16[144,1152]{1,0:T(8,128)(2,1)S(1)}, u32[]{:S(2)}, u32[]{:S(2)}) collective-permute-start(bf16[144,1152]{1,0:T(8,128)(2,1)S(1)} %fusion.28), channel_id=1, source_target_pairs={{24,0},{28,4},{0,8},{4,12},{8,16},{12,20},{16,24},{20,28},{25,1},{... | collective-permute-start | bytes 995336 | tf_op jit(solution)/shard_map/ppermute | solution.py:923
  54.0 145.0 %all-gather.3.cloned.1.call-start = ((), (), s32[]{:S(2)}) async-start(), calls=%async_computation.1 | async-start | bytes 5971968 | tf_op jit(solution)/shard_map/all_gather | solution.py:1075
  67.0 33.0 %collective-permute-start.10 = (bf16[2,4,144,640]{3,2,1,0:T(8,128)(2,1)S(1)}, bf16[2,4,144,640]{3,2,1,0:T(8,128)(2,1)S(1)}, u32[]{:S(2)}, u32[]{:S(2)}) collective-permute-start(bf16[2,4,144,640]{3,2,1,0:T(8,128)(2,1)S(1)} %pad_maximum_fusion.2.rest_4_), channel_id=1, source_target_pairs={{0,4},{4,0},{8,12},{12,8},{16,20},{20,16},{24,28},{28,24},{1,5},{5... | collective-permute-start | bytes 4423688 | tf_op jit(solution)/shard_map/ppermute | solution.py:883
  69.6 30.4 %collective-permute-start.9 = (bf16[2,4,144,512]{3,2,1,0:T(8,128)(2,1)}, bf16[2,4,144,512]{3,2,1,0:T(8,128)(2,1)S(1)}, u32[]{:S(2)}, u32[]{:S(2)}) collective-permute-start(bf16[2,4,144,512]{3,2,1,0:T(8,128)(2,1)} %pad_maximum_fusion.7.rest_0_), channel_id=1, source_target_pairs={{0,2},{1,3},{2,0},{3,1},{4,6},{5,7},{6,4},{7,5},{8,10},{9,11},{10,... | collective-permute-start | bytes 3538952 | tf_op jit(solution)/shard_map/ppermute | solution.py:883
  110.3 37.8 %collective-permute-start.18 = (bf16[4,144,1152]{2,1,0:T(8,128)(2,1)}, bf16[4,144,1152]{2,1,0:T(8,128)(2,1)}, u32[]{:S(2)}, u32[]{:S(2)}) collective-permute-start(bf16[4,144,1152]{2,1,0:T(8,128)(2,1)} %pad_maximum_fusion.4.rest_3_), channel_id=1, source_target_pairs={{0,4},{4,0},{8,12},{12,8},{16,20},{20,16},{24,28},{28,24},{1,5},{5... | collective-permute-start | bytes 3981320 | tf_op jit(solution)/shard_map/ppermute | solution.py:883
  110.4 37.7 %collective-permute-start.19 = (bf16[4,144,1152]{2,1,0:T(8,128)(2,1)}, bf16[4,144,1152]{2,1,0:T(8,128)(2,1)}, u32[]{:S(2)}, u32[]{:S(2)}) collective-permute-start(bf16[4,144,1152]{2,1,0:T(8,128)(2,1)} %pad_maximum_fusion.4.rest_3_), channel_id=1, source_target_pairs={{0,2},{1,3},{2,0},{3,1},{4,6},{5,7},{6,4},{7,5},{8,10},{9,11},{10,... | collective-permute-start | bytes 3981320 | tf_op jit(solution)/shard_map/ppermute | solution.py:883
  117.1 66.2 %collective-permute-start.21 = (bf16[4,144,1152]{2,1,0:T(8,128)(2,1)}, bf16[4,144,1152]{2,1,0:T(8,128)(2,1)}, u32[]{:S(2)}, u32[]{:S(2)}) collective-permute-start(bf16[4,144,1152]{2,1,0:T(8,128)(2,1)} %pad_maximum_fusion.4.rest_3_), channel_id=1, source_target_pairs={{0,1},{1,0},{2,3},{3,2},{4,5},{5,4},{6,7},{7,6},{8,9},{9,8},{10,11... | collective-permute-start | bytes 3981320 | tf_op jit(solution)/shard_map/ppermute | solution.py:883
  148.1 35.2 %collective-permute-start.20 = (bf16[4,144,1152]{2,1,0:T(8,128)(2,1)}, bf16[4,144,1152]{2,1,0:T(8,128)(2,1)S(1)}, u32[]{:S(2)}, u32[]{:S(2)}) collective-permute-start(bf16[4,144,1152]{2,1,0:T(8,128)(2,1)} %collective-permute-done.18.rest_4_), channel_id=1, source_target_pairs={{0,2},{1,3},{2,0},{3,1},{4,6},{5,7},{6,4},{7,5},{8,10},{9,11},{10,... | collective-permute-start | bytes 3981320 | tf_op jit(solution)/shard_map/ppermute | solution.py:883
  149.3 34.0 %collective-permute-start.22 = (bf16[4,144,1152]{2,1,0:T(8,128)(2,1)}, bf16[4,144,1152]{2,1,0:T(8,128)(2,1)}, u32[]{:S(2)}, u32[]{:S(2)}) collective-permute-start(bf16[4,144,1152]{2,1,0:T(8,128)(2,1)} %collective-permute-done.18.rest_4_), channel_id=1, source_target_pairs={{0,1},{1,0},{2,3},{3,2},{4,5},{5,4},{6,7},{7,6},{8,9},{9,8},{10,11... | collective-permute-start | bytes 3981320 | tf_op jit(solution)/shard_map/ppermute | solution.py:883
  150.8 32.4 %collective-permute-start.23 = (s32[2,4,2]{2,0,1:T(2,128)S(1)}, s32[2,4,2]{2,0,1:T(2,128)S(1)}, u32[]{:S(2)}, u32[]{:S(2)}) collective-permute-start(s32[2,4,2]{2,0,1:T(2,128)S(1)} %bitcast.247), channel_id=1, source_target_pairs={{0,1},{1,0},{2,3},{3,2},{4,5},{5,4},{6,7},{7,6},{8,9},{9,8},{10,11... | collective-permute-start | bytes 200 | tf_op jit(solution)/shard_map/ppermute | solution.py:883
  325.9 59.1 %collective-permute-start.30 = (bf16[2,4,144,1152]{3,2,1,0:T(8,128)(2,1)}, bf16[2,4,144,1152]{3,2,1,0:T(8,128)(2,1)}, u32[]{:S(2)}, u32[]{:S(2)}) collective-permute-start(bf16[2,4,144,1152]{3,2,1,0:T(8,128)(2,1)} %fusion), channel_id=1, source_target_pairs={{0,4},{4,0},{8,12},{12,8},{16,20},{20,16},{24,28},{28,24},{1,5},{5... | collective-permute-start | bytes 7962632 | tf_op jit(solution)/shard_map/ppermute | solution.py:883
  326.2 58.8 %collective-permute-start.31 = (bf16[2,4,144,1152]{3,2,1,0:T(8,128)(2,1)}, bf16[2,4,144,1152]{3,2,1,0:T(8,128)(2,1)}, u32[]{:S(2)}, u32[]{:S(2)}) collective-permute-start(bf16[2,4,144,1152]{3,2,1,0:T(8,128)(2,1)} %fusion.1), channel_id=1, source_target_pairs={{0,2},{1,3},{2,0},{3,1},{4,6},{5,7},{6,4},{7,5},{8,10},{9,11},{10,... | collective-permute-start | bytes 7962632 | tf_op jit(solution)/shard_map/ppermute | solution.py:883
  390.5 31.2 %collective-permute-start.32 = (bf16[4,144,1152]{2,1,0:T(8,128)(2,1)}, bf16[4,144,1152]{2,1,0:T(8,128)(2,1)}, u32[]{:S(2)}, u32[]{:S(2)}) collective-permute-start(bf16[4,144,1152]{2,1,0:T(8,128)(2,1)} %get-tuple-element.192), channel_id=1, source_target_pairs={{0,2},{1,3},{2,0},{3,1},{4,6},{5,7},{6,4},{7,5},{8,10},{9,11},{10,... | collective-permute-start | bytes 3981320 | tf_op jit(solution)/shard_map/ppermute | solution.py:883
  391.7 30.0 %collective-permute-start.33 = (bf16[4,144,1152]{2,1,0:T(8,128)(2,1)}, bf16[4,144,1152]{2,1,0:T(8,128)(2,1)}, u32[]{:S(2)}, u32[]{:S(2)}) collective-permute-start(bf16[4,144,1152]{2,1,0:T(8,128)(2,1)} %get-tuple-element.193), channel_id=1, source_target_pairs={{0,4},{4,0},{8,12},{12,8},{16,20},{20,16},{24,28},{28,24},{1,5},{5... | collective-permute-start | bytes 3981320 | tf_op jit(solution)/shard_map/ppermute | solution.py:883
  438.1 33.8 %collective-permute-start.37 = (bf16[2,4,144,640]{3,2,1,0:T(8,128)(2,1)}, bf16[2,4,144,640]{3,2,1,0:T(8,128)(2,1)}, u32[]{:S(2)}, u32[]{:S(2)}) collective-permute-start(bf16[2,4,144,640]{3,2,1,0:T(8,128)(2,1)} %fusion.6), channel_id=1, source_target_pairs={{0,4},{4,0},{8,12},{12,8},{16,20},{20,16},{24,28},{28,24},{1,5},{5... | collective-permute-start | bytes 4423688 | tf_op jit(solution)/shard_map/ppermute | solution.py:883
  439.1 32.3 %collective-permute-start.36 = (bf16[2,4,144,512]{3,2,1,0:T(8,128)(2,1)}, bf16[2,4,144,512]{3,2,1,0:T(8,128)(2,1)}, u32[]{:S(2)}, u32[]{:S(2)}) collective-permute-start(bf16[2,4,144,512]{3,2,1,0:T(8,128)(2,1)} %fusion.9), channel_id=1, source_target_pairs={{0,2},{1,3},{2,0},{3,1},{4,6},{5,7},{6,4},{7,5},{8,10},{9,11},{10,... | collective-permute-start | bytes 3538952 | tf_op jit(solution)/shard_map/ppermute | solution.py:883
  440.4 31.0 %collective-permute-start.38 = (bf16[144,1152]{1,0:T(8,128)(2,1)}, bf16[144,1152]{1,0:T(8,128)(2,1)S(1)}, u32[]{:S(2)}, u32[]{:S(2)}) collective-permute-start(bf16[144,1152]{1,0:T(8,128)(2,1)} %get-tuple-element.267), channel_id=1, source_target_pairs={{24,0},{28,4},{0,8},{4,12},{8,16},{12,20},{16,24},{20,28},{25,1},{... | collective-permute-start | bytes 995336 | tf_op jit(solution)/shard_map/ppermute | solution.py:923
  440.4 31.0 %collective-permute-start.39 = (bf16[144,1152]{1,0:T(8,128)(2,1)}, bf16[144,1152]{1,0:T(8,128)(2,1)S(1)}, u32[]{:S(2)}, u32[]{:S(2)}) collective-permute-start(bf16[144,1152]{1,0:T(8,128)(2,1)} %get-tuple-element.266), channel_id=1, source_target_pairs={{16,0},{20,4},{24,8},{28,12},{0,16},{4,20},{8,24},{12,28},{17,1},{... | collective-permute-start | bytes 995336 | tf_op jit(solution)/shard_map/ppermute | solution.py:923
  441.8 29.6 %collective-permute-start.40 = (bf16[144,1152]{1,0:T(8,128)(2,1)}, bf16[144,1152]{1,0:T(8,128)(2,1)}, u32[]{:S(2)}, u32[]{:S(2)}) collective-permute-start(bf16[144,1152]{1,0:T(8,128)(2,1)} %get-tuple-element.265), channel_id=1, source_target_pairs={{8,0},{12,4},{16,8},{20,12},{24,16},{28,20},{0,24},{4,28},{9,1},{1... | collective-permute-start | bytes 995336 | tf_op jit(solution)/shard_map/ppermute | solution.py:923
  521.7 28.0 %collective-permute-start.56 = (bf16[2,144,1152]{2,1,0:T(8,128)(2,1)S(1)}, bf16[2,144,1152]{2,1,0:T(8,128)(2,1)S(1)}, u32[]{:S(2)}, u32[]{:S(2)}) collective-permute-start(bf16[2,144,1152]{2,1,0:T(8,128)(2,1)S(1)} %pad_maximum_fusion.9), channel_id=1, source_target_pairs={{0,2},{1,3},{2,0},{3,1},{4,6},{5,7},{6,4},{7,5},{8,10},{9,11},{10,... | collective-permute-start | bytes 1990664 | tf_op jit(solution)/shard_map/ppermute | solution.py:883
  522.8 28.2 %collective-permute-start.49 = (bf16[144,1152]{1,0:T(8,128)(2,1)S(1)}, bf16[144,1152]{1,0:T(8,128)(2,1)S(1)}, u32[]{:S(2)}, u32[]{:S(2)}) collective-permute-start(bf16[144,1152]{1,0:T(8,128)(2,1)S(1)} %get-tuple-element.261), channel_id=1, source_target_pairs={{24,0},{28,4},{0,8},{4,12},{8,16},{12,20},{16,24},{20,28},{25,1},{... | collective-permute-start | bytes 995336 | tf_op jit(solution)/shard_map/ppermute | solution.py:923
  523.1 27.9 %collective-permute-start.50 = (bf16[144,1152]{1,0:T(8,128)(2,1)S(1)}, bf16[144,1152]{1,0:T(8,128)(2,1)S(1)}, u32[]{:S(2)}, u32[]{:S(2)}) collective-permute-start(bf16[144,1152]{1,0:T(8,128)(2,1)S(1)} %get-tuple-element.260), channel_id=1, source_target_pairs={{16,0},{20,4},{24,8},{28,12},{0,16},{4,20},{8,24},{12,28},{17,1},{... | collective-permute-start | bytes 995336 | tf_op jit(solution)/shard_map/ppermute | solution.py:923
  (67 other events, 826.7 us)
Sparse Core Ops, SparseCore 0:
  109.8 89.1 all-gather.2
